TPU v7x, 128 devices: a whole 4x4x4 slice. The times are simulated.
128 devices in a mesh: branch: 2 (over core), seq: 64 (over x, z, y).
Axes of the slice: x: 4, y: 4, z: 4, core: 2. Of those that a mesh axis runs over, the one named last changes fastest.
Arguments:
- hidden: bfloat16 [2, 49152, 1024], P('branch', 'seq')
- noisy_mel_state: float32 [100, 49152], P(None, 'seq'), may hold values from -6 to 6
- modulation: float32 [5, 1024], replicated, may hold values from -3 to 3
- feedforward_in_weight: bfloat16 [1024, 2048], replicated, may hold values from -0.1875 to 0.1875
- feedforward_in_bias: float32 [2048], replicated, may hold values from -1.75 to 1.75
- feedforward_out_weight: bfloat16 [2048, 1024], replicated, may hold values from -0.125 to 0.125
- feedforward_out_bias: float32 [1024], replicated, may hold values from -1.75 to 1.75
- mel_velocity_weight: bfloat16 [1024, 100], replicated, may hold values from -0.1875 to 0.1875
- mel_velocity_bias: float32 [100], replicated, may hold values from -3 to 3
- input_conv_weight: bfloat16 [700, 512], replicated, may hold values from -0.21875 to 0.21875
- input_conv_bias: float32 [512], replicated, may hold values from -1.75 to 1.75
- transposed_conv_weight: bfloat16 [4096, 512], replicated, may hold values from -0.1875 to 0.1875
- transposed_conv_bias: float32 [256], replicated, may hold values from -1.75 to 1.75
- snake_freq_first: float32 [256], replicated, may hold values from 0.5 to 3
- dilated_conv_weight: bfloat16 [768, 256], replicated, may hold values from -0.21875 to 0.21875
- dilated_conv_bias: float32 [256], replicated, may hold values from -1.75 to 1.75
- snake_freq_second: float32 [256], replicated, may hold values from 0.5 to 3
- second_conv_weight: bfloat16 [768, 256], replicated, may hold values from -0.21875 to 0.21875
- second_conv_bias: float32 [256], replicated, may hold values from -1.75 to 1.75
- frame_holder: int32 [49152], P('seq'), may hold values from 0 to 127, as said below
- frame_position: int32 [49152], P('seq'), may hold values from 0 to 767, as said below
- holder_utterance_length: int32 [128], replicated, may hold values from 1 to 768, as said below
Outputs:
- wave: bfloat16 [128, 256, 6144], P(('branch', 'seq'))
Inputs may be any that keep to these rules, and one draw needn't show every extreme that they name: `frame_holder`: the frames form 128 utterances, each a run of consecutive frames; all frames of an utterance name one owner, and each owner is named by exactly one utterance. `frame_position`: A frame's position in its utterance, 0 at the utterance's first frame. `holder_utterance_length`: the number of frames that name the owner; every utterance has at least one frame.
All inputs are finite; a program needn't handle non-finite values.
Results may differ from a plain program's by a relative error of at most 0.015.
Values may be sent and summed in bfloat16 or wider, within the bound.
No kernel may reach another device: no remote copies, remote signals or barrier semaphores. Data moves between devices by JAX's collectives and lax.ppermute only.
A program may use at most 128 MiB of HBM per device.

v0:
```python
import math

import jax
import jax.numpy as jnp
from jax import lax
from jax.sharding import PartitionSpec as P

UP = 8
KT = 16
KPRE = 7
DILATION_RATE = 3
NFE = 16


GUIDE = 2.0


def partner(block, axis, distance):
    count = lax.axis_size(axis)
    route = []
    for low in range(count):
        high = low | 1 << distance
        if high != low and high < count:
            route += [(low, high), (high, low)]
    return lax.ppermute(block, axis, route)


def layer_norm(row_block):
    row_mean = jnp.mean(row_block, axis=-1, keepdims=True)
    centred = row_block - row_mean
    row_var = jnp.mean(centred * centred, axis=-1, keepdims=True)
    return centred * lax.rsqrt(row_var + 1e-06)


def velocity(
    row_block,
    modulation,
    feedforward_in_weight,
    feedforward_in_bias,
    feedforward_out_weight,
    feedforward_out_bias,
    mel_velocity_weight,
    mel_velocity_bias,
):
    residual_in = row_block.astype(jnp.float32)
    normed = (layer_norm(residual_in) * (1.0 + modulation[1]) + modulation[0]).astype(jnp.bfloat16)
    inner_pre = (
        jnp.dot(normed, feedforward_in_weight, preferred_element_type=jnp.float32)
        + feedforward_in_bias
    )
    active = jax.nn.gelu(inner_pre, approximate=True).astype(jnp.bfloat16)
    back_proj = (
        jnp.dot(active, feedforward_out_weight, preferred_element_type=jnp.float32)
        + feedforward_out_bias
    )
    block_out = residual_in + modulation[2] * back_proj
    final_norm = (layer_norm(block_out) * (1.0 + modulation[4]) + modulation[3]).astype(
        jnp.bfloat16
    )
    speed = lax.dot_general(
        mel_velocity_weight,
        final_norm,
        (((0,), (1,)), ((), ())),
        preferred_element_type=jnp.float32,
    )
    return speed + mel_velocity_bias[:, None]


def shifted(values, offset):
    pad_width = abs(offset)
    last_axis = values.ndim - 1
    pad_spec = [(0, 0)] * last_axis + [(pad_width, pad_width)]
    padded = jnp.pad(values, pad_spec)
    return lax.slice_in_dim(
        padded, pad_width + offset, pad_width + offset + values.shape[last_axis], axis=last_axis
    )


def snake(signal, alpha_vec):
    sine_part = jnp.sin(alpha_vec[:, None] * signal)
    return signal + sine_part * sine_part / alpha_vec[:, None]


def dilated_output(values, weight, bias_vec, spacing, keep_mask):
    stacked = jnp.concatenate([shifted(values, -spacing), values, shifted(values, spacing)], axis=0)
    conv_out = lax.dot_general(
        weight, stacked, (((0,), (0,)), ((), ())), preferred_element_type=jnp.float32
    )
    return jnp.where(keep_mask[None, :], conv_out + bias_vec[:, None], 0.0)


def vocoder_synthesize(
    holder_mel,
    utterance_frames_length,
    input_conv_weight,
    input_conv_bias,
    transposed_conv_weight,
    transposed_conv_bias,
    snake_freq_first,
    dilated_conv_weight,
    dilated_conv_bias,
    snake_freq_second,
    second_conv_weight,
    second_conv_bias,
):
    most_rows = holder_mel.shape[1]
    channels = transposed_conv_weight.shape[0] // KT
    frame_keep = jnp.arange(most_rows) < utterance_frames_length
    half_kernel = KPRE // 2
    tap_list = [shifted(holder_mel, tap_index - half_kernel) for tap_index in range(KPRE)]
    stacked = jnp.concatenate(tap_list, axis=0)
    pre_out = lax.dot_general(
        input_conv_weight, stacked, (((0,), (0,)), ((), ())), preferred_element_type=jnp.float32
    )
    pre_out = jnp.where(frame_keep[None, :], pre_out + input_conv_bias[:, None], 0.0).astype(
        jnp.bfloat16
    )
    phases = jnp.dot(transposed_conv_weight, pre_out, preferred_element_type=jnp.float32).reshape(
        KT, channels, most_rows
    )
    pad_up = UP // 2
    direct = phases[pad_up : pad_up + UP]
    early_part = shifted(phases[UP + pad_up :], -1)
    late_part = shifted(phases[: UP - pad_up], 1)
    phase_sum = direct + jnp.concatenate([early_part, late_part], axis=0)
    woven_out = (
        jnp.transpose(phase_sum, (1, 2, 0)).reshape(channels, most_rows * UP)
        + transposed_conv_bias[:, None]
    )
    sample_keep_mask = jnp.arange(most_rows * UP) < utterance_frames_length * UP
    upsampled = jnp.where(sample_keep_mask[None, :], woven_out, 0.0).astype(jnp.bfloat16)
    first_snake_output = snake(upsampled.astype(jnp.float32), snake_freq_first).astype(jnp.bfloat16)
    inner_convolved = dilated_output(
        first_snake_output, dilated_conv_weight, dilated_conv_bias, DILATION_RATE, sample_keep_mask
    )
    second_act = snake(inner_convolved, snake_freq_second).astype(jnp.bfloat16)
    outer_conv = dilated_output(
        second_act, second_conv_weight, second_conv_bias, 1, sample_keep_mask
    )
    return (upsampled.astype(jnp.float32) + outer_conv).astype(jnp.bfloat16)


def slot_table(slot_ids, slot_count):
    return (slot_ids[:, None] == jnp.arange(slot_count, dtype=jnp.int32)[None, :]).astype(
        jnp.bfloat16
    )


def local(
    hidden,
    noisy_mel_state,
    modulation,
    feedforward_in_weight,
    feedforward_in_bias,
    feedforward_out_weight,
    feedforward_out_bias,
    mel_velocity_weight,
    mel_velocity_bias,
    input_conv_weight,
    input_conv_bias,
    transposed_conv_weight,
    transposed_conv_bias,
    snake_freq_first,
    dilated_conv_weight,
    dilated_conv_bias,
    snake_freq_second,
    second_conv_weight,
    second_conv_bias,
    frame_holder,
    frame_position,
    holder_utterance_length,
):
    step_size = math.cos(0.5 * math.pi * (NFE - 1) / NFE)
    own_velocity = velocity(
        hidden[0],
        modulation,
        feedforward_in_weight,
        feedforward_in_bias,
        feedforward_out_weight,
        feedforward_out_bias,
        mel_velocity_weight,
        mel_velocity_bias,
    )
    mel_bins = own_velocity.shape[0]
    frame_count = own_velocity.shape[1]
    half_rows = frame_count // 2
    branch_side = lax.axis_index("branch")
    own_half = lax.dynamic_slice_in_dim(own_velocity, branch_side * half_rows, half_rows, 1)
    peer_full = partner(own_velocity, "branch", 0)
    peer_half = lax.dynamic_slice_in_dim(peer_full, branch_side * half_rows, half_rows, 1)
    conditional = jnp.where(branch_side == 0, own_half, peer_half)
    unconditional = jnp.where(branch_side == 0, peer_half, own_half)
    guided = (1.0 + GUIDE) * conditional - GUIDE * unconditional
    noisy_half = lax.dynamic_slice_in_dim(noisy_mel_state, branch_side * half_rows, half_rows, 1)
    refined = (noisy_half + step_size * guided).astype(jnp.bfloat16)
    owner_half = lax.dynamic_slice_in_dim(frame_holder, branch_side * half_rows, half_rows, 0)
    offset_half = lax.dynamic_slice_in_dim(frame_position, branch_side * half_rows, half_rows, 0)
    frame_tags = jnp.stack([owner_half, offset_half], axis=0)
    self_owner = lax.axis_index(("branch", "seq"))
    values = lax.all_gather(refined, ("branch", "seq"), axis=1, tiled=True)
    tag_rows = lax.all_gather(frame_tags, ("branch", "seq"), axis=1, tiled=True)
    piece_rows = values.shape[1]
    block_rows = math.gcd(piece_rows, 512)

    def add_block(block_index, total):
        block_values = lax.dynamic_slice_in_dim(values, block_index * block_rows, block_rows, 1)
        block_tags = lax.dynamic_slice_in_dim(tag_rows, block_index * block_rows, block_rows, 1)
        target = jnp.where(block_tags[0] == self_owner, block_tags[1], frame_count)
        return total + jnp.dot(
            block_values, slot_table(target, frame_count), preferred_element_type=jnp.float32
        )

    gathered_sum = lax.fori_loop(
        0, piece_rows // block_rows, add_block, jnp.zeros((mel_bins, frame_count), jnp.float32)
    )
    holder_mel = gathered_sum.astype(jnp.bfloat16)
    utterance_frames_length = holder_utterance_length[self_owner]
    wave = vocoder_synthesize(
        holder_mel,
        utterance_frames_length,
        input_conv_weight,
        input_conv_bias,
        transposed_conv_weight,
        transposed_conv_bias,
        snake_freq_first,
        dilated_conv_weight,
        dilated_conv_bias,
        snake_freq_second,
        second_conv_weight,
        second_conv_bias,
    )
    return wave[None]


def solution(mesh):
    return jax.shard_map(
        local,
        mesh=mesh,
        in_specs=(
            P("branch", "seq", None),
            P(None, "seq"),
            P(),
            P(),
            P(),
            P(),
            P(),
            P(),
            P(),
            P(),
            P(),
            P(),
            P(),
            P(),
            P(),
            P(),
            P(),
            P(),
            P(),
            P("seq"),
            P("seq"),
            P(),
        ),
        out_specs=P(("branch", "seq"), None, None),
        check_vma=False,
    )
```

profile of v0, /device:TPU:1, one launch (start us, length us, event | category | flops | bytes accessed | tf_op | source)
XLA Modules:
  0.0 618.9 jit_solution(10566197206418479175)
XLA Ops:
  7.6 1.7 convert_reduce_fusion
  9.3 2.0 fusion.61
  11.3 12.4 %fusion.91 = (f32[768]{0:T(1024)S(1)}, f32[768,1024]{1,0:T(8,128)}) fusion(f32[1024]{0:T(1024)S(1)} %copy-done.16, bf16[2048,1024]{1,0:T(8,128)(2,1)} %param.29, bf16[1024,2048]{1,0:T(8,128)(2,1)} %param.27, f32[2048]{0:T(1024)S(1)} %copy-done.15, bf16[1,768,1024]{2,1,0:T(8,128)(2,1)S(1)} %copy-done.5, f32[1024]{0:T(1024)S(1)} %bitcast.100, ...), kind=kOutput, calls=%fused_computation.105 | convolution fusion | flops 6466829312 | bytes 13140992 | tf_op jit(solution)/shard_map/dot_general | solution.py:53
  23.7 2.5 multiply_reduce_fusion
  27.4 1.5 collective-permute-start
  32.9 321.1 %all_gather.7 = s32[2,49152]{1,0:T(2,128)S(1)} all-gather(s32[2,384]{1,0:T(2,128)S(1)} %pad_add_fusion), channel_id=1, replica_groups=mesh['branch'=2,'seq'=64] {'branch','seq'}, dimensions={1}, use_global_device_ids=true | all-gather | bytes 396288 | tf_op jit(solution)/shard_map/all_gather | solution.py:201
  354.0 146.8 %while.14 = (s32[]{:T(128)}, f32[100,768]{1,0:T(8,128)S(1)}, bf16[100,49152]{1,0:T(8,128)(2,1)}, s32[2,49152]{1,0:T(2,128)S(1)}, s32[]{:T(128)}, /*index=5*/s32[]{:T(128)}, s32[]{:T(128)}, s32[]{}, s32[]{:T(128)}, s32[]{:T(128)}) while((s32[]{:T(128)}, f32[100,768]{1,0:T(8,128)S(1)}, bf16[100,49152]{1,0:T(8,128)(2,1)}, ...), condition=%wide.region_5.6_spmd.clone, body=%wide.region_4.5_spmd.clone.sunk | while | flops 79191048 | bytes 729273 | solution.py:213
  354.1 1.4 fusion.105
  355.6 1.4 fusion.105
  357.2 1.4 fusion.105
  358.7 1.4 fusion.105
  360.2 1.4 fusion.105
  361.8 1.4 fusion.105
  363.3 1.4 fusion.105
  367.9 1.4 fusion.105
  369.4 1.4 fusion.105
  381.6 1.4 fusion.105
  383.2 1.4 fusion.105
  395.4 1.4 fusion.105
  396.9 1.4 fusion.105
  409.2 1.4 fusion.105
  410.7 1.4 fusion.105
  413.8 1.4 fusion.105
  415.3 1.4 fusion.105
  427.5 1.4 fusion.105
  429.1 1.4 fusion.105
  441.3 1.4 fusion.105
  442.8 1.4 fusion.105
  455.1 1.4 fusion.105
  456.6 1.4 fusion.105
  468.8 1.4 fusion.105
  470.4 1.4 fusion.105
  482.6 1.4 fusion.105
  484.1 1.4 fusion.105
  496.4 1.4 fusion.105
  497.9 1.4 fusion.105
  502.4 9.2 %convolution_bitcast_fusion = f32[4096,768]{0,1:T(8,128)} fusion(bf16[4096,512]{1,0:T(8,128)(2,1)} %param.35, bf16[700,768]{1,0:T(8,128)(2,1)S(1)} %concatenate.12, bf16[700,512]{1,0:T(8,128)(2,1)S(1)} %copy-done, f32[512]{0:T(512)S(1)} %copy-done.17, pred[768]{0:T(1024)(128)(4,1)S(1)} %iota_compare_fusion.5), kind=kOutput, calls=%fused_computation.25 | convolution fusion | flops 3772907520 | bytes 18572032 | tf_op jit(solution)/shard_map/dot_general | solution.py:118
  511.6 7.3 %fusion.90 = (f32[1024,768]{0,1:T(8,128)}, f32[1024,768]{0,1:T(8,128)}) fusion(f32[4096,768]{0,1:T(8,128)} %convolution_bitcast_fusion), kind=kLoop, calls=%fused_computation.104 | loop fusion | bytes 12582912 | tf_op jit(solution)/shard_map/slice | solution.py:123
  520.3 3.1 slice.108
  523.4 5.2 slice.100
  528.6 5.2 slice.97
  533.8 6.0 copy.24
  541.0 27.0 %fusion.54 = (bf16[256,6144]{0,1:T(8,128)(2,1)S(1)}, bf16[256,6144]{0,1:T(8,128)(2,1)S(1)}) fusion(f32[256]{0:T(256)S(1)} %copy-done.8, f32[256]{0:T(256)S(1)} %copy-done.9, f32[4,256,768]{1,0,2:T(4,128)S(1)} %get-tuple-element.149, f32[4,256,768]{1,0,2:T(4,128)S(1)} %get-tuple-element.150, f32[96,8,8,256]{3,2,1,0:T(8,128)S(1)} %copy.24, ...), kind=kLoop, calls=%fused_computation.43 | loop fusion | flops 17301504 | bytes 18882560 | tf_op jit(solution)/shard_map/convert_element_type | solution.py:132
  568.0 1.7 pad_slice_fusion.5
  569.7 29.9 %add_convert_fusion = bf16[256,6144]{0,1:T(8,128)(2,1)S(1)} fusion(f32[256]{0:T(256)S(1)} %copy-done.18, f32[256]{0:T(256)S(1)} %copy-done.19, bf16[768,256]{1,0:T(8,128)(2,1)S(1)} %copy-done.12, bf16[256,6144]{0,1:T(8,128)(2,1)S(1)} %get-tuple-element.135, bf16[256,6144]{0,1:T(8,128)(2,1)S(1)} %get-tuple-element.128, ...), kind=kOutput, calls=%fused_computation.48 | convolution fusion | flops 2455240704 | bytes 12984320 | tf_op jit(solution)/shard_map/dot_general | solution.py:86
  599.6 1.7 pad_slice_fusion.3
  601.3 6.0 fusion.40
  607.4 4.6 copy.23
  (233 shorter events, 112.6 us)
Async XLA Ops:
  6.5 495.8 %copy-start = (bf16[700,512]{1,0:T(8,128)(2,1)S(1)}, bf16[700,512]{1,0:T(8,128)(2,1)}, u32[]{:S(2)}) copy-start(bf16[700,512]{1,0:T(8,128)(2,1)} %param.33) | copy-start | bytes 2150404
  6.5 4.7 copy-start.5
  6.5 4.7 copy-start.15
  6.5 4.7 copy-start.16
  6.5 347.5 %all-gather.2.cloned.1.call-start = ((), (), s32[]{:S(2)}) async-start(), calls=%async_computation | async-start | bytes 10303488 | tf_op jit(solution)/shard_map/all_gather | solution.py:200
  11.3 15.0 %copy-start.14 = (bf16[1024,100]{0,1:T(8,128)(2,1)S(1)}, bf16[1024,100]{0,1:T(8,128)(2,1)}, u32[]{:S(2)}) copy-start(bf16[1024,100]{0,1:T(8,128)(2,1)} %param.31) | copy-start | bytes 614404
  23.7 2.8 copy-start.6
  23.7 2.8 copy-start.21
  23.7 6.4 %copy-start.7 = (f32[100,768]{1,0:T(8,128)S(1)}, f32[100,768]{1,0:T(8,128)}, u32[]{:S(2)}) copy-start(f32[100,768]{1,0:T(8,128)} %param.25) | copy-start | bytes 921604
  26.2 4.6 copy-start.10
  26.2 4.7 copy-start.11
  26.2 4.8 copy-start.22
  27.4 2.7 collective-permute-start
  354.0 148.3 %copy-start.17 = (f32[512]{0:T(512)S(1)}, f32[512]{0:T(512)}, u32[]{:S(2)}) copy-start(f32[512]{0:T(512)} %param.34) | copy-start | bytes 6148
  511.6 8.7 %copy-start.2 = (f32[4096,768]{0,1:T(8,128)S(1)}, f32[4096,768]{0,1:T(8,128)}, u32[]{:S(2)}) copy-start(f32[4096,768]{0,1:T(8,128)} %convolution_bitcast_fusion) | copy-start | bytes 37748740
  533.8 6.0 copy-start.3
  533.8 6.0 copy-start.4
  539.8 1.2 copy-start.8
  539.9 1.2 copy-start.9
  568.0 1.7 copy-start.12
  568.0 1.7 copy-start.18
  568.0 1.7 copy-start.19
  599.6 1.7 copy-start.13
  599.6 1.7 copy-start.20
  601.3 10.7 %copy-start.1 = (bf16[700,512]{1,0:T(8,128)(2,1)S(1)}, bf16[700,512]{1,0:T(8,128)(2,1)}, u32[]{:S(2)}) copy-start(bf16[700,512]{1,0:T(8,128)(2,1)} %param.33) | copy-start | bytes 2150404
Sparse Core Ops, SparseCore 0:
  30.9 79.9 all-gather.1
where the time goes:
time: 622 us; the launch traced here: 619 us
  blocking collectives  321 us (52%)
  matrix products  195 us (31%)
  other arithmetic  43.4 us (7%)
  local copies, waits for them, and re-layouts  39.9 us (6%)
  between operations  14.4 us (2%)
    all_gather x1, blocking collectives, local(): tag_rows = lax.all_gather(frame_tags, ('branch', 'seq'), axis=1, tiled=True)  321 us
    dot_general x96, matrix products, add_block(): jnp.dot(block_values, slot_table(target, frame_count), preferred_element_...  136 us
    dot_general x2, matrix products, dilated_output(): lax.dot_general(weight, stacked, (((0,), (0,)), ((), ())), preferred_elem...  35.9 us
    convert_element_type x1, other arithmetic, vocoder_synthesize(): snake(upsampled.astype(jnp.float32), snake_freq_first).astype(jnp.bfloat16)  27 us
    slice x2, local copies, waits for them, and re-layouts, vocoder_synthesize(): early_part = shifted(phases[UP + pad_up:], -1)  12.5 us
  transfers between devices with their start and end apart: 2, of which 1 were waited for; matrix products, arithmetic and copies ran while one was open for 0% of the time, Pallas kernels for 0%

commit v1 on v0

--- a/solution.py
+++ b/solution.py
@@ -13,16 +13,7 @@
 
 
 GUIDE = 2.0
-
-
-def partner(block, axis, distance):
-    count = lax.axis_size(axis)
-    route = []
-    for low in range(count):
-        high = low | 1 << distance
-        if high != low and high < count:
-            route += [(low, high), (high, low)]
-    return lax.ppermute(block, axis, route)
+LANES = 128
 
 
 def layer_norm(row_block):
@@ -57,13 +48,8 @@
     final_norm = (layer_norm(block_out) * (1.0 + modulation[4]) + modulation[3]).astype(
         jnp.bfloat16
     )
-    speed = lax.dot_general(
-        mel_velocity_weight,
-        final_norm,
-        (((0,), (1,)), ((), ())),
-        preferred_element_type=jnp.float32,
-    )
-    return speed + mel_velocity_bias[:, None]
+    speed = jnp.dot(final_norm, mel_velocity_weight, preferred_element_type=jnp.float32)
+    return speed + mel_velocity_bias
 
 
 def shifted(values, offset):
@@ -138,12 +124,6 @@
         second_act, second_conv_weight, second_conv_bias, 1, sample_keep_mask
     )
     return (upsampled.astype(jnp.float32) + outer_conv).astype(jnp.bfloat16)
-
-
-def slot_table(slot_ids, slot_count):
-    return (slot_ids[:, None] == jnp.arange(slot_count, dtype=jnp.int32)[None, :]).astype(
-        jnp.bfloat16
-    )
 
 
 def local(
@@ -171,6 +151,9 @@
     holder_utterance_length,
 ):
     step_size = math.cos(0.5 * math.pi * (NFE - 1) / NFE)
+    cores = lax.axis_size("branch")
+    chips = lax.axis_size("seq")
+    owners = cores * chips
     own_velocity = velocity(
         hidden[0],
         modulation,
@@ -178,42 +161,49 @@
         feedforward_in_bias,
         feedforward_out_weight,
         feedforward_out_bias,
-        mel_velocity_weight,
-        mel_velocity_bias,
-    )
-    mel_bins = own_velocity.shape[0]
-    frame_count = own_velocity.shape[1]
-    half_rows = frame_count // 2
+        jnp.pad(mel_velocity_weight, ((0, 0), (0, LANES - mel_velocity_weight.shape[1]))),
+        jnp.pad(mel_velocity_bias, (0, LANES - mel_velocity_bias.shape[0])),
+    )
+    mel_bins = mel_velocity_weight.shape[1]
+    frame_count = own_velocity.shape[0]
+    half_rows = frame_count // cores
+    group = half_rows // chips
     branch_side = lax.axis_index("branch")
-    own_half = lax.dynamic_slice_in_dim(own_velocity, branch_side * half_rows, half_rows, 1)
-    peer_full = partner(own_velocity, "branch", 0)
-    peer_half = lax.dynamic_slice_in_dim(peer_full, branch_side * half_rows, half_rows, 1)
+    own_half = lax.dynamic_slice_in_dim(own_velocity, branch_side * half_rows, half_rows, 0)
+    sent_half = lax.dynamic_slice_in_dim(own_velocity, (1 - branch_side) * half_rows, half_rows, 0)
+    peer_half = lax.ppermute(sent_half, "branch", [(0, 1), (1, 0)])
     conditional = jnp.where(branch_side == 0, own_half, peer_half)
     unconditional = jnp.where(branch_side == 0, peer_half, own_half)
     guided = (1.0 + GUIDE) * conditional - GUIDE * unconditional
     noisy_half = lax.dynamic_slice_in_dim(noisy_mel_state, branch_side * half_rows, half_rows, 1)
-    refined = (noisy_half + step_size * guided).astype(jnp.bfloat16)
+    noisy_rows = jnp.pad(noisy_half.T, ((0, 0), (0, LANES - mel_bins)))
+    refined = noisy_rows + step_size * guided
     owner_half = lax.dynamic_slice_in_dim(frame_holder, branch_side * half_rows, half_rows, 0)
     offset_half = lax.dynamic_slice_in_dim(frame_position, branch_side * half_rows, half_rows, 0)
-    frame_tags = jnp.stack([owner_half, offset_half], axis=0)
+    lane = jnp.arange(LANES)[None, :]
+    refined = jnp.where(lane == mel_bins, owner_half[:, None].astype(jnp.float32), refined)
+    first_flag = (offset_half == 0).astype(jnp.float32)[:, None]
+    refined = jnp.where(lane == mel_bins + 1, first_flag, refined)
+    packed = refined.astype(jnp.bfloat16).reshape(chips, group, LANES)
+    spread = lax.all_to_all(packed, "seq", 0, 0, tiled=True)
+    rows = spread.reshape(chips * group, LANES)
+    owner_of = rows[:, mel_bins].astype(jnp.int32)
+    slot_of = owner_of * group + jnp.arange(chips * group, dtype=jnp.int32) % group
+    onehot = (slot_of[:, None] == jnp.arange(owners * group, dtype=jnp.int32)[None, :]).astype(
+        jnp.bfloat16
+    )
+    slots = lax.dot_general(
+        onehot, rows, (((0,), (0,)), ((), ())), preferred_element_type=jnp.float32
+    ).astype(jnp.bfloat16)
+    arrived = lax.all_to_all(
+        slots.reshape(owners, group, LANES), ("branch", "seq"), 0, 0, tiled=True
+    ).reshape(owners * group, LANES)
+    start = jnp.sum(
+        jnp.arange(owners * group, dtype=jnp.float32) * arrived[:, mel_bins + 1].astype(jnp.float32)
+    ).astype(jnp.int32)
+    twice = jnp.concatenate([arrived, arrived], axis=0)
+    holder_mel = lax.dynamic_slice_in_dim(twice, start, owners * group, 0)[:, :mel_bins].T
     self_owner = lax.axis_index(("branch", "seq"))
-    values = lax.all_gather(refined, ("branch", "seq"), axis=1, tiled=True)
-    tag_rows = lax.all_gather(frame_tags, ("branch", "seq"), axis=1, tiled=True)
-    piece_rows = values.shape[1]
-    block_rows = math.gcd(piece_rows, 512)
-
-    def add_block(block_index, total):
-        block_values = lax.dynamic_slice_in_dim(values, block_index * block_rows, block_rows, 1)
-        block_tags = lax.dynamic_slice_in_dim(tag_rows, block_index * block_rows, block_rows, 1)
-        target = jnp.where(block_tags[0] == self_owner, block_tags[1], frame_count)
-        return total + jnp.dot(
-            block_values, slot_table(target, frame_count), preferred_element_type=jnp.float32
-        )
-
-    gathered_sum = lax.fori_loop(
-        0, piece_rows // block_rows, add_block, jnp.zeros((mel_bins, frame_count), jnp.float32)
-    )
-    holder_mel = gathered_sum.astype(jnp.bfloat16)
     utterance_frames_length = holder_utterance_length[self_owner]
     wave = vocoder_synthesize(
         holder_mel,

time: 622 us -> 175 us (0.28)
  blocking collectives: 321 us -> 0 us
  matrix products: 195 us -> 60.7 us
  waiting for transfers between devices: 1.26 us -> 18.1 us
  starting transfers between devices: 1.53 us -> 18.2 us
  between operations: 14.4 us -> 1.73 us
  other arithmetic: 43.4 us -> 36.8 us
    all_gather x1 -> x0, blocking collectives: 321 us -> none  [local(): tag_rows = lax.all_gather(frame_tags, ('branch', 'seq'), axis=1, tiled=True)]
    dot_general x97 -> x2, matrix products: 137 us -> 3.28 us  [the longest x1 2.69 us: velocity(): jnp.dot(final_norm, mel_velocity_weight, preferred_element_type=jnp.float32)]
    all_to_all x0 -> x2, waiting for transfers between devices: none -> 17.4 us  [the longest x1 10 us: local(): lax.all_to_all(slots.reshape(owners, group, LANES), ('branch', 'seq'), 0,...]
    all_to_all x0 -> x2, starting transfers between devices: none -> 16.7 us  [the longest x1 11.2 us: local(): spread = lax.all_to_all(packed, 'seq', 0, 0, tiled=True)]
    select_n x96 -> x0, other arithmetic: 7.93 us -> none  [add_block(): target = jnp.where(block_tags[0] == self_owner, block_tags[1], frame_count)]
  transfers between devices with their start and end apart: 2 -> 3, of which waited for: 1 -> 3; matrix products, arithmetic and copies ran while one was open for 0% -> 1% of each run, Pallas kernels for 0% -> 0%
where the time goes in v1:
time: 175 us
  matrix products  60.7 us (35%)
  local copies, waits for them, and re-layouts  39.3 us (22%)
  other arithmetic  36.8 us (21%)
  starting transfers between devices  18.2 us (10%)
  waiting for transfers between devices  18.1 us (10%)
    dot_general x2, matrix products, dilated_output(): lax.dot_general(weight, stacked, (((0,), (0,)), ((), ())), preferred_elem...  35.9 us
    convert_element_type x1, other arithmetic, vocoder_synthesize(): snake(upsampled.astype(jnp.float32), snake_freq_first).astype(jnp.bfloat16)  27 us
    dot_general x1, matrix products, velocity(): jnp.dot(active, feedforward_out_weight, preferred_element_type=jnp.float32)  12.4 us
    slice x2, local copies, waits for them, and re-layouts, vocoder_synthesize(): early_part = shifted(phases[UP + pad_up:], -1)  11.8 us
    all_to_all x1, starting transfers between devices, local(): spread = lax.all_to_all(packed, 'seq', 0, 0, tiled=True)  11.2 us
    slice x5, local copies, waits for them, and re-layouts, shifted(): lax.slice_in_dim(padded, pad_width + offset, pad_width + offset + values....  10.2 us
    all_to_all x1, waiting for transfers between devices, local(): lax.all_to_all(slots.reshape(owners, group, LANES), ('branch', 'seq'), 0,...  10 us
    dot_general x1, matrix products, vocoder_synthesize(): jnp.dot(transposed_conv_weight, pre_out, preferred_element_type=jnp.float32)  9.19 us
  transfers between devices with their start and end apart: 3, of which 3 were waited for; matrix products, arithmetic and copies ran while one was open for 1% of the time, Pallas kernels for 0%

profile of v1, /device:TPU:1, one launch (start us, length us, event | category | flops | bytes accessed | tf_op | source)
XLA Modules:
  0.0 174.9 jit_solution(16468817930435709198)
XLA Ops:
  0.0 1.0 slice_add_fusion
  1.0 1.7 convert_reduce_fusion
  2.7 2.0 %fusion.56 = f32[768]{0:T(1024)S(1)} fusion(bf16[1,768,1024]{2,1,0:T(8,128)(2,1)} %param.22, f32[768]{0:T(1024)S(1)} %broadcast_multiply_fusion.1), kind=kLoop, calls=%fused_computation.50 | loop fusion | flops 3144960 | bytes 1579008 | tf_op jit(solution)/shard_map/reduce_sum | solution.py:22
  4.7 12.4 %fusion.93 = (f32[768]{0:T(1024)S(1)}, f32[768,1024]{1,0:T(8,128)}) fusion(f32[1024]{0:T(1024)S(1)} %copy-done.13, bf16[2048,1024]{1,0:T(8,128)(2,1)} %param.27, bf16[1024,2048]{1,0:T(8,128)(2,1)} %param.25, f32[2048]{0:T(1024)S(1)} %copy-done.12, bf16[1,768,1024]{2,1,0:T(8,128)(2,1)S(1)} %copy-done.3, f32[1024]{0:T(1024)S(1)} %bitcast.81, ...), kind=kOutput, calls=%fused_computation.116 | convolution fusion | flops 6466829312 | bytes 13140992 | tf_op jit(solution)/shard_map/dot_general | solution.py:44
  17.1 2.4 %multiply_reduce_fusion = f32[768]{0:T(1024)S(1)} fusion(f32[768,1024]{1,0:T(8,128)} %get-tuple-element.25, f32[768]{0:T(1024)S(1)} %broadcast_multiply_fusion), kind=kLoop, calls=%fused_computation.55 | loop fusion | flops 2358528 | bytes 3151872 | tf_op jit(solution)/shard_map/reduce_sum | solution.py:22
  19.5 0.0 copy-start.4
  19.5 0.0 copy-start.7
  19.5 0.0 copy-start.8
  19.6 0.0 copy-start.19
  19.6 2.7 %fusion.68 = f32[768,128]{1,0:T(8,128)S(1)} fusion(f32[768,1024]{1,0:T(8,128)} %get-tuple-element.25, f32[1024]{0:T(1024)S(1)} %bitcast.80, f32[1024]{0:T(1024)S(1)} %bitcast.79, f32[768]{0:T(1024)S(1)} %add_rsqrt_fusion, f32[768]{0:T(1024)S(1)} %broadcast_multiply_fusion, bf16[1024,100]{0,1:T(8,128)(2,1)S(1)} %copy-done.11, f32[128]{0:T(128)S(1)} %pad.46), kind=kOutput, calls=%fused_computation.66 | convolution fusion | flops 205357056 | bytes 3758592 | tf_op jit(solution)/shard_map/dot_general | solution.py:51
  22.3 1.5 collective-permute-start
  23.8 0.1 copy.27
  24.0 0.1 dynamic-slice_convert_fusion
  24.1 0.1 fusion.82
  24.1 0.7 collective-permute-done
  24.9 0.2 select_convert_fusion.1
  25.1 0.7 reshape.98
  25.7 11.2 %all-to-all-start = ((bf16[64,6,128]{2,1,0:T(8,128)(2,1)}), bf16[64,6,128]{2,1,0:T(8,128)(2,1)S(1)}, u32[]{:S(2)}, u32[]{:S(2)}) async-start(bf16[64,6,128]{2,1,0:T(8,128)(2,1)} %reshape.98), calls=%async_computation | async-start | bytes 262144 | tf_op jit(solution)/shard_map/all_to_all | solution.py:188
  37.0 0.6 dynamic_slice.21
  38.3 7.4 %all-to-all-done = bf16[64,6,128]{2,1,0:T(8,128)(2,1)S(1)} async-done(((bf16[64,6,128]{2,1,0:T(8,128)(2,1)}), bf16[64,6,128]{2,1,0:T(8,128)(2,1)S(1)}, u32[]{:S(2)}, u32[]{:S(2)}) %all-to-all-start) | async-done | bytes 98336 | tf_op jit(solution)/shard_map/all_to_all | solution.py:188
  45.7 0.2 fusion.76
  45.9 0.6 fusion.70
  46.5 0.8 reshape.100
  47.3 5.4 %all-to-all-start.1 = ((bf16[128,6,128]{2,1,0:T(8,128)(2,1)}), bf16[128,6,128]{2,1,0:T(8,128)(2,1)S(1)}, u32[]{:S(2)}, u32[]{:S(2)}) async-start(bf16[128,6,128]{2,1,0:T(8,128)(2,1)} %reshape.100), calls=%async_computation.1 | async-start | bytes 524288 | tf_op jit(solution)/shard_map/all_to_all | solution.py:198
  52.7 0.6 iota_compare_fusion.5
  53.4 10.0 %all-to-all-done.1 = bf16[128,6,128]{2,1,0:T(8,128)(2,1)S(1)} async-done(((bf16[128,6,128]{2,1,0:T(8,128)(2,1)}), bf16[128,6,128]{2,1,0:T(8,128)(2,1)S(1)}, u32[]{:S(2)}, u32[]{:S(2)}) %all-to-all-start.1) | async-done | bytes 196640 | tf_op jit(solution)/shard_map/all_to_all | solution.py:198
  63.4 0.1 reshape.101
  63.5 0.2 convert_reduce_fusion.1
  63.7 0.6 multiply_reduce_fusion.1
  65.0 0.8 fusion.78
  65.7 0.3 pad_slice_fusion.10
  66.0 0.8 concatenate.16
  66.9 9.2 %convolution_bitcast_fusion = f32[4096,768]{0,1:T(8,128)} fusion(bf16[4096,512]{1,0:T(8,128)(2,1)} %param.33, bf16[700,768]{0,1:T(8,128)(2,1)S(1)} %concatenate.16, bf16[700,512]{1,0:T(8,128)(2,1)S(1)} %copy-done, f32[512]{0:T(512)S(1)} %copy-done.14, pred[768]{0:T(1024)(128)(4,1)S(1)} %iota_compare_fusion.5), kind=kOutput, calls=%fused_computation.18 | convolution fusion | flops 3772907520 | bytes 18572032 | tf_op jit(solution)/shard_map/dot_general | solution.py:104
  76.1 6.6 %fusion.92 = (f32[1024,768]{0,1:T(8,128)}, f32[1024,768]{0,1:T(8,128)}) fusion(f32[4096,768]{0,1:T(8,128)} %convolution_bitcast_fusion), kind=kLoop, calls=%fused_computation.115 | loop fusion | bytes 12582912 | tf_op jit(solution)/shard_map/slice | solution.py:109
  82.7 5.2 %slice.98 = f32[4,256,768]{1,0,2:T(4,128)} reshape(f32[1024,768]{0,1:T(8,128)} %get-tuple-element.8) | data formatting | bytes 6291456 | tf_op jit(solution)/shard_map/slice | solution.py:110
  87.9 4.1 %pad_slice_fusion = f32[4,256,768]{1,0,2:T(4,128)} fusion(f32[4,256,768]{1,0,2:T(4,128)} %slice.98), kind=kLoop, calls=%fused_computation.48 | loop fusion | bytes 6291456 | tf_op jit(solution)/shard_map/slice | solution.py:60
  91.9 5.2 %slice.95 = f32[4,256,768]{1,0,2:T(4,128)} reshape(f32[1024,768]{0,1:T(8,128)} %get-tuple-element.7) | data formatting | bytes 6291456 | tf_op jit(solution)/shard_map/slice | solution.py:109
  97.1 2.6 %pad_slice_fusion.1 = f32[4,256,768]{1,0,2:T(4,128)S(1)} fusion(f32[4,256,768]{1,0,2:T(4,128)} %slice.95), kind=kLoop, calls=%fused_computation.49 | loop fusion | bytes 6291456 | tf_op jit(solution)/shard_map/slice | solution.py:60
  99.7 1.1 slice-done
  100.8 3.0 %copy.28 = f32[96,8,8,256]{3,2,1,0:T(8,128)S(1)} copy(f32[96,8,8,256]{3,1,2,0:T(8,128)S(1)} %bitcast.77) | data formatting | bytes 12582912
  103.9 27.0 %fusion.49 = (bf16[256,6144]{0,1:T(8,128)(2,1)S(1)}, bf16[256,6144]{0,1:T(8,128)(2,1)S(1)}) fusion(f32[256]{0:T(256)S(1)} %copy-done.5, f32[256]{0:T(256)S(1)} %copy-done.6, f32[4,256,768]{1,0,2:T(4,128)S(1)} %copy-done.2, f32[4,256,768]{1,0,2:T(4,128)S(1)} %pad_slice_fusion.1, f32[96,8,8,256]{3,2,1,0:T(8,128)S(1)} %copy.28, ...), kind=kLoop, calls=%fused_computation.36 | loop fusion | flops 17301504 | bytes 18882560 | tf_op jit(solution)/shard_map/convert_element_type | solution.py:118
  130.9 0.0 copy-start.9
  130.9 0.0 copy-start.15
  130.9 1.7 pad_slice_fusion.5
  132.6 29.9 %add_convert_fusion = bf16[256,6144]{0,1:T(8,128)(2,1)S(1)} fusion(f32[256]{0:T(256)S(1)} %copy-done.15, f32[256]{0:T(256)S(1)} %copy-done.16, bf16[768,256]{1,0:T(8,128)(2,1)S(1)} %copy-done.9, bf16[256,6144]{0,1:T(8,128)(2,1)S(1)} %get-tuple-element.12, bf16[256,6144]{0,1:T(8,128)(2,1)S(1)} %get-tuple-element.5, ...), kind=kOutput, calls=%fused_computation.41 | convolution fusion | flops 2455240704 | bytes 12984320 | tf_op jit(solution)/shard_map/dot_general | solution.py:72
  162.5 1.7 pad_slice_fusion.3
  164.2 6.0 %fusion.35 = bf16[1,256,6144]{1,2,0:T(8,128)(2,1)} fusion(bf16[768,256]{1,0:T(8,128)(2,1)S(1)} %copy-done.10, bf16[256,6144]{0,1:T(8,128)(2,1)S(1)} %get-tuple-element.10, bf16[256,6144]{0,1:T(8,128)(2,1)S(1)} %add_convert_fusion, bf16[256,6144]{0,1:T(8,128)(2,1)S(1)} %get-tuple-element.9, bf16[256,6144]{0,1:T(8,128)(2,1)S(1)} %get-tuple-element.6, ...), kind=kOutput, calls=%fused_computation.24 | convolution fusion | flops 2452094976 | bytes 16129024 | tf_op jit(solution)/shard_map/dot_general | solution.py:72
  170.2 4.6 %copy.26 = bf16[1,256,6144]{2,1,0:T(8,128)(2,1)} copy(bf16[1,256,6144]{1,2,0:T(8,128)(2,1)} %fusion.35) | data formatting | bytes 6291456 | tf_op jit(solution)/shard_map/broadcast_in_dim | solution.py:222
  (45 shorter events, 0.2 us)
Async XLA Ops:
  0.0 66.9 %copy-start = (bf16[700,512]{1,0:T(8,128)(2,1)S(1)}, bf16[700,512]{1,0:T(8,128)(2,1)}, u32[]{:S(2)}) copy-start(bf16[700,512]{1,0:T(8,128)(2,1)} %param.31) | copy-start | bytes 2150404
  0.0 4.7 %copy-start.3 = (bf16[1,768,1024]{2,1,0:T(8,128)(2,1)S(1)}, bf16[1,768,1024]{2,1,0:T(8,128)(2,1)}, u32[]{:S(2)}) copy-start(bf16[1,768,1024]{2,1,0:T(8,128)(2,1)} %param.22) | copy-start | bytes 4718596
  0.0 4.7 %copy-start.12 = (f32[2048]{0:T(1024)S(1)}, f32[2048]{0:T(1024)}, u32[]{:S(2)}) copy-start(f32[2048]{0:T(1024)} %param.26) | copy-start | bytes 24580
  0.0 4.7 %copy-start.13 = (f32[1024]{0:T(1024)S(1)}, f32[1024]{0:T(1024)}, u32[]{:S(2)}) copy-start(f32[1024]{0:T(1024)} %param.28) | copy-start | bytes 12292
  17.1 2.4 %copy-start.18 = (f32[100]{0:T(128)S(1)}, f32[100]{0:T(128)}, u32[]{:S(2)}) copy-start(f32[100]{0:T(128)} %param.30) | copy-start | bytes 1204
  17.1 2.5 %copy-start.11 = (bf16[1024,100]{0,1:T(8,128)(2,1)S(1)}, bf16[1024,100]{0,1:T(8,128)(2,1)}, u32[]{:S(2)}) copy-start(bf16[1024,100]{0,1:T(8,128)(2,1)} %param.29) | copy-start | bytes 614404
  19.5 4.3 %copy-start.4 = (f32[100,768]{1,0:T(8,128)S(1)}, f32[100,768]{1,0:T(8,128)}, u32[]{:S(2)}) copy-start(f32[100,768]{1,0:T(8,128)} %param.23) | copy-start | bytes 921604
  19.5 4.5 %copy-start.7 = (s32[768]{0:T(1024)S(1)}, s32[768]{0:T(1024)}, u32[]{:S(2)}) copy-start(s32[768]{0:T(1024)} %param.41) | copy-start | bytes 9220
  19.5 4.5 %copy-start.8 = (s32[768]{0:T(1024)S(1)}, s32[768]{0:T(1024)}, u32[]{:S(2)}) copy-start(s32[768]{0:T(1024)} %param.42) | copy-start | bytes 9220
  19.6 17.4 %copy-start.19 = (s32[128]{0:T(128)S(1)}, s32[128]{0:T(128)}, u32[]{:S(2)}) copy-start(s32[128]{0:T(128)} %param.43) | copy-start | bytes 1540
  22.3 2.6 %collective-permute-start = (f32[384,128]{1,0:T(8,128)S(1)}, f32[384,128]{1,0:T(8,128)S(1)}, u32[]{:S(2)}, u32[]{:S(2)}) collective-permute-start(f32[384,128]{1,0:T(8,128)S(1)} %constant_dynamic-slice_fusion), channel_id=1, source_target_pairs={{0,64},{64,0},{1,65},{65,1},{2,66},{66,2},{3,67},{67,3},{4,68},{68... | collective-permute-start | bytes 589832 | tf_op jit(solution)/shard_map/ppermute | solution.py:174
  25.7 19.9 %all-to-all-start = ((bf16[64,6,128]{2,1,0:T(8,128)(2,1)}), bf16[64,6,128]{2,1,0:T(8,128)(2,1)S(1)}, u32[]{:S(2)}, u32[]{:S(2)}) async-start(bf16[64,6,128]{2,1,0:T(8,128)(2,1)} %reshape.98), calls=%async_computation | async-start | bytes 262144 | tf_op jit(solution)/shard_map/all_to_all | solution.py:188
  45.9 21.0 %copy-start.14 = (f32[512]{0:T(512)S(1)}, f32[512]{0:T(512)}, u32[]{:S(2)}) copy-start(f32[512]{0:T(512)} %param.32) | copy-start | bytes 6148
  47.3 16.2 %all-to-all-start.1 = ((bf16[128,6,128]{2,1,0:T(8,128)(2,1)}), bf16[128,6,128]{2,1,0:T(8,128)(2,1)S(1)}, u32[]{:S(2)}, u32[]{:S(2)}) async-start(bf16[128,6,128]{2,1,0:T(8,128)(2,1)} %reshape.100), calls=%async_computation.1 | async-start | bytes 524288 | tf_op jit(solution)/shard_map/all_to_all | solution.py:198
  97.1 3.7 %slice-start = ((f32[4096,768]{0,1:T(8,128)}), f32[2048,768]{0,1:T(8,128)S(1)}, s32[]{:S(2)}) async-start(f32[4096,768]{0,1:T(8,128)} %convolution_bitcast_fusion), calls=%async_computation.2 | async-start | bytes 12582912 | tf_op jit(solution)/shard_map/slice | solution.py:108
  100.8 3.0 %copy-start.2 = (f32[4,256,768]{1,0,2:T(4,128)S(1)}, f32[4,256,768]{1,0,2:T(4,128)}, u32[]{:S(2)}) copy-start(f32[4,256,768]{1,0,2:T(4,128)} %pad_slice_fusion) | copy-start | bytes 9437188
  100.8 3.0 %copy-start.5 = (f32[256]{0:T(256)S(1)}, f32[256]{0:T(256)}, u32[]{:S(2)}) copy-start(f32[256]{0:T(256)} %param.35) | copy-start | bytes 3076
  100.8 3.1 %copy-start.6 = (f32[256]{0:T(256)S(1)}, f32[256]{0:T(256)}, u32[]{:S(2)}) copy-start(f32[256]{0:T(256)} %param.34) | copy-start | bytes 3076
  130.9 1.7 copy-start.9
  130.9 1.7 copy-start.15
  130.9 1.7 copy-start.16
  162.5 1.7 copy-start.10
  162.5 1.7 copy-start.17
  164.2 10.7 %copy-start.1 = (bf16[700,512]{1,0:T(8,128)(2,1)S(1)}, bf16[700,512]{1,0:T(8,128)(2,1)}, u32[]{:S(2)}) copy-start(bf16[700,512]{1,0:T(8,128)(2,1)} %param.31) | copy-start | bytes 2150404

commit v2 on v1

--- a/solution.py
+++ b/solution.py
@@ -1,8 +1,11 @@
+import functools
 import math
 
 import jax
 import jax.numpy as jnp
 from jax import lax
+from jax.experimental import pallas as pl
+from jax.experimental.pallas import tpu as pltpu
 from jax.sharding import PartitionSpec as P
 
 UP = 8
@@ -52,32 +55,189 @@
     return speed + mel_velocity_bias
 
 
-def shifted(values, offset):
-    pad_width = abs(offset)
-    last_axis = values.ndim - 1
-    pad_spec = [(0, 0)] * last_axis + [(pad_width, pad_width)]
-    padded = jnp.pad(values, pad_spec)
-    return lax.slice_in_dim(
-        padded, pad_width + offset, pad_width + offset + values.shape[last_axis], axis=last_axis
-    )
-
-
-def snake(signal, alpha_vec):
-    sine_part = jnp.sin(alpha_vec[:, None] * signal)
-    return signal + sine_part * sine_part / alpha_vec[:, None]
-
-
-def dilated_output(values, weight, bias_vec, spacing, keep_mask):
-    stacked = jnp.concatenate([shifted(values, -spacing), values, shifted(values, spacing)], axis=0)
-    conv_out = lax.dot_general(
-        weight, stacked, (((0,), (0,)), ((), ())), preferred_element_type=jnp.float32
-    )
-    return jnp.where(keep_mask[None, :], conv_out + bias_vec[:, None], 0.0)
-
-
-def vocoder_synthesize(
-    holder_mel,
-    utterance_frames_length,
+SIN_TERMS = (
+    3.141592579805583,
+    -5.167706866168128,
+    2.550031193522954,
+    -0.5980441939334223,
+    0.07721838619602994,
+)
+
+
+def snake_rows(signal, turns, inverse):
+    half_turns = signal * turns
+    part = half_turns - jnp.round(half_turns)
+    square = part * part
+    poly = SIN_TERMS[4] * square + SIN_TERMS[3]
+    poly = poly * square + SIN_TERMS[2]
+    poly = poly * square + SIN_TERMS[1]
+    poly = poly * square + SIN_TERMS[0]
+    sine = poly * part
+    return signal + sine * sine * inverse
+
+
+def nt_dot(left, right):
+    return lax.dot_general(
+        left, right, (((1,), (1,)), ((), ())), preferred_element_type=jnp.float32
+    )
+
+
+def vocoder_kernel(
+    length_ref,
+    arrived_ref,
+    input_weight_ref,
+    input_bias_ref,
+    up_weight_ref,
+    up_bias_ref,
+    freq_first_ref,
+    dilated_weight_ref,
+    dilated_bias_ref,
+    freq_second_ref,
+    second_weight_ref,
+    second_bias_ref,
+    wave_ref,
+    mel_ref,
+    taps_ref,
+    shift_wide_ref,
+    pre_ref,
+    shift_ref,
+    up_ref,
+    first_ref,
+    second_ref,
+    out_ref,
+    *,
+    mel_bins,
+):
+    frames = arrived_ref.shape[0]
+    channels = second_bias_ref.shape[1]
+    block = 128
+    blocks = frames // block
+    halo = 8
+    f32, bf16 = jnp.float32, jnp.bfloat16
+    step = pl.program_id(0)
+    length = length_ref[0]
+
+    def keep_rows(first, count):
+        row = lax.broadcasted_iota(jnp.int32, (count, 1), 0) + first
+        return row < length
+
+    @pl.when(step == 0)
+    def _():
+        arrived = arrived_ref[...]
+        lane = lax.broadcasted_iota(jnp.int32, arrived.shape, 1)
+        place = lax.broadcasted_iota(jnp.int32, arrived.shape, 0).astype(f32)
+        start = jnp.sum(
+            jnp.where(lane == mel_bins + 1, arrived.astype(f32) * place, 0.0), keepdims=True
+        ).astype(jnp.int32)
+        mel_ref[...] = jnp.zeros(mel_ref.shape, f32)
+        for i in range(blocks):
+            ahead = (
+                lax.broadcasted_iota(jnp.int32, (block, frames), 1)
+                - lax.broadcasted_iota(jnp.int32, (block, frames), 0)
+                - (start + i * block)
+            )
+            pick = ((ahead == 0) | (ahead == -frames)).astype(bf16)
+            mel_ref[halo + i * block : halo + (i + 1) * block, :] = jnp.dot(
+                pick, arrived, preferred_element_type=f32
+            )
+        for k in range(KPRE):
+            low = halo + k - KPRE // 2
+            taps_ref[:, k * LANES : (k + 1) * LANES] = mel_ref[low : low + frames, :].astype(bf16)
+        shift_wide_ref[...] = jnp.zeros(shift_wide_ref.shape, f32)
+        for i in range(blocks):
+            rows = slice(i * block, (i + 1) * block)
+            pre = jnp.dot(taps_ref[rows, :], input_weight_ref[...], preferred_element_type=f32)
+            pre = jnp.where(keep_rows(i * block, block), pre + input_bias_ref[...], 0.0)
+            shift_wide_ref[halo + i * block : halo + (i + 1) * block, :] = pre
+        for k in range(3):
+            low = halo + k - 1
+            pre_ref[k] = shift_wide_ref[low : low + frames, :].astype(bf16)
+        shift_ref[...] = jnp.zeros(shift_ref.shape, f32)
+
+        turns_first = freq_first_ref[...] * (1.0 / math.pi)
+        inverse_first = 1.0 / freq_first_ref[...]
+        turns_second = freq_second_ref[...] * (1.0 / math.pi)
+        inverse_second = 1.0 / freq_second_ref[...]
+
+        def neighbour_rows(offset):
+            low = halo + offset
+            return shift_ref[low : low + frames, :].astype(bf16)
+
+        @pl.loop(0, UP)
+        def _(r):
+            side = jnp.where(r < UP // 2, 0, 2)
+            here = up_weight_ref[r + UP // 2]
+            there = up_weight_ref[lax.rem(r + UP // 2 + UP, KT)]
+            for i in range(blocks):
+                rows = slice(i * block, (i + 1) * block)
+                up = nt_dot(pre_ref[1, rows, :], here) + nt_dot(pre_ref[side, rows, :], there)
+                up = jnp.where(keep_rows(i * block, block), up + up_bias_ref[...], 0.0)
+                up = up.astype(bf16)
+                up_ref[r, rows, :] = up
+                first = snake_rows(up.astype(f32), turns_first, inverse_first)
+                first_ref[r + 3, rows, :] = first.astype(bf16)
+
+        for r in range(DILATION_RATE):
+            shift_ref[halo : halo + frames, :] = first_ref[r + 3].astype(f32)
+            first_ref[r + 3 + UP] = neighbour_rows(1)
+        for r in range(UP - DILATION_RATE, UP):
+            shift_ref[halo : halo + frames, :] = first_ref[r + 3].astype(f32)
+            first_ref[r + 3 - UP] = neighbour_rows(-1)
+
+        @pl.loop(0, UP)
+        def _(r):
+            for i in range(blocks):
+                rows = slice(i * block, (i + 1) * block)
+                inner = jnp.dot(
+                    first_ref[r, rows, :], dilated_weight_ref[0], preferred_element_type=f32
+                )
+                inner += jnp.dot(
+                    first_ref[r + 3, rows, :], dilated_weight_ref[1], preferred_element_type=f32
+                )
+                inner += jnp.dot(
+                    first_ref[r + 6, rows, :], dilated_weight_ref[2], preferred_element_type=f32
+                )
+                inner = jnp.where(
+                    keep_rows(i * block, block), inner + dilated_bias_ref[...], 0.0
+                )
+                second = snake_rows(inner, turns_second, inverse_second)
+                second_ref[r + 1, rows, :] = second.astype(bf16)
+
+        shift_ref[halo : halo + frames, :] = second_ref[1].astype(f32)
+        second_ref[UP + 1] = neighbour_rows(1)
+        shift_ref[halo : halo + frames, :] = second_ref[UP].astype(f32)
+        second_ref[0] = neighbour_rows(-1)
+
+    base = pl.multiple_of(step * block, block)
+    for r in range(UP):
+        rows = pl.ds(base, block)
+        outer = jnp.dot(second_ref[r, rows, :], second_weight_ref[0], preferred_element_type=f32)
+        outer += jnp.dot(
+            second_ref[r + 1, rows, :], second_weight_ref[1], preferred_element_type=f32
+        )
+        outer += jnp.dot(
+            second_ref[r + 2, rows, :], second_weight_ref[2], preferred_element_type=f32
+        )
+        outer = jnp.where(keep_rows(base, block), outer + second_bias_ref[...], 0.0)
+        out_ref[r] = (up_ref[r, rows, :].astype(f32) + outer).astype(bf16)
+    narrow = 256 // UP
+    row = lax.broadcasted_iota(jnp.int32, (256, 256), 0)
+    col = lax.broadcasted_iota(jnp.int32, (256, 256), 1)
+    weave = (col == lax.rem(row, narrow) * UP + row // narrow).astype(bf16)
+    for piece in range(block // narrow):
+        phases = jnp.concatenate(
+            [out_ref[r, piece * narrow : (piece + 1) * narrow, :] for r in range(UP)], axis=0
+        )
+        woven = lax.dot_general(
+            phases, weave, (((0,), (0,)), ((), ())), preferred_element_type=f32
+        )
+        wave_ref[0, :, piece * 256 : (piece + 1) * 256] = woven.astype(bf16)
+
+
+def vocoder(
+    arrived,
+    length,
+    mel_bins,
     input_conv_weight,
     input_conv_bias,
     transposed_conv_weight,
@@ -89,41 +249,53 @@
     second_conv_weight,
     second_conv_bias,
 ):
-    most_rows = holder_mel.shape[1]
-    channels = transposed_conv_weight.shape[0] // KT
-    frame_keep = jnp.arange(most_rows) < utterance_frames_length
-    half_kernel = KPRE // 2
-    tap_list = [shifted(holder_mel, tap_index - half_kernel) for tap_index in range(KPRE)]
-    stacked = jnp.concatenate(tap_list, axis=0)
-    pre_out = lax.dot_general(
-        input_conv_weight, stacked, (((0,), (0,)), ((), ())), preferred_element_type=jnp.float32
-    )
-    pre_out = jnp.where(frame_keep[None, :], pre_out + input_conv_bias[:, None], 0.0).astype(
-        jnp.bfloat16
-    )
-    phases = jnp.dot(transposed_conv_weight, pre_out, preferred_element_type=jnp.float32).reshape(
-        KT, channels, most_rows
-    )
-    pad_up = UP // 2
-    direct = phases[pad_up : pad_up + UP]
-    early_part = shifted(phases[UP + pad_up :], -1)
-    late_part = shifted(phases[: UP - pad_up], 1)
-    phase_sum = direct + jnp.concatenate([early_part, late_part], axis=0)
-    woven_out = (
-        jnp.transpose(phase_sum, (1, 2, 0)).reshape(channels, most_rows * UP)
-        + transposed_conv_bias[:, None]
-    )
-    sample_keep_mask = jnp.arange(most_rows * UP) < utterance_frames_length * UP
-    upsampled = jnp.where(sample_keep_mask[None, :], woven_out, 0.0).astype(jnp.bfloat16)
-    first_snake_output = snake(upsampled.astype(jnp.float32), snake_freq_first).astype(jnp.bfloat16)
-    inner_convolved = dilated_output(
-        first_snake_output, dilated_conv_weight, dilated_conv_bias, DILATION_RATE, sample_keep_mask
-    )
-    second_act = snake(inner_convolved, snake_freq_second).astype(jnp.bfloat16)
-    outer_conv = dilated_output(
-        second_act, second_conv_weight, second_conv_bias, 1, sample_keep_mask
-    )
-    return (upsampled.astype(jnp.float32) + outer_conv).astype(jnp.bfloat16)
+    frames = arrived.shape[0]
+    wide = input_conv_bias.shape[0]
+    channels = transposed_conv_bias.shape[0]
+    block = 128
+    f32, bf16 = jnp.float32, jnp.bfloat16
+    taps_weight = jnp.pad(
+        input_conv_weight.reshape(KPRE, mel_bins, wide), ((0, 0), (0, LANES - mel_bins), (0, 0))
+    ).reshape(KPRE * LANES, wide)
+    operands = [
+        arrived,
+        taps_weight,
+        input_conv_bias[None],
+        transposed_conv_weight.reshape(KT, channels, wide),
+        transposed_conv_bias[None],
+        snake_freq_first[None],
+        dilated_conv_weight.reshape(3, channels, channels),
+        dilated_conv_bias[None],
+        snake_freq_second[None],
+        second_conv_weight.reshape(3, channels, channels),
+        second_conv_bias[None],
+    ]
+    return pl.pallas_call(
+        functools.partial(vocoder_kernel, mel_bins=mel_bins),
+        out_shape=jax.ShapeDtypeStruct((1, channels, frames * UP), bf16),
+        grid=(frames // block,),
+        in_specs=[pl.BlockSpec(memory_space=pltpu.SMEM)]
+        + [
+            pl.BlockSpec(
+                x.shape, lambda i, n=x.ndim: (0,) * n, pipeline_mode=pl.Buffered(1)
+            )
+            for x in operands
+        ],
+        out_specs=pl.BlockSpec((1, channels, block * UP), lambda i: (0, 0, i)),
+        scratch_shapes=[
+            pltpu.VMEM((frames + 16, LANES), f32),
+            pltpu.VMEM((frames, KPRE * LANES), bf16),
+            pltpu.VMEM((frames + 16, wide), f32),
+            pltpu.VMEM((3, frames, wide), bf16),
+            pltpu.VMEM((frames + 16, channels), f32),
+            pltpu.VMEM((UP, frames, channels), bf16),
+            pltpu.VMEM((UP + 6, frames, channels), bf16),
+            pltpu.VMEM((UP + 2, frames, channels), bf16),
+            pltpu.VMEM((UP, block, channels), bf16),
+        ],
+        compiler_params=pltpu.CompilerParams(vmem_limit_bytes=48 * 1024 * 1024),
+        name="vocoder",
+    )(length, *operands)
 
 
 def local(
@@ -198,16 +370,12 @@
     arrived = lax.all_to_all(
         slots.reshape(owners, group, LANES), ("branch", "seq"), 0, 0, tiled=True
     ).reshape(owners * group, LANES)
-    start = jnp.sum(
-        jnp.arange(owners * group, dtype=jnp.float32) * arrived[:, mel_bins + 1].astype(jnp.float32)
-    ).astype(jnp.int32)
-    twice = jnp.concatenate([arrived, arrived], axis=0)
-    holder_mel = lax.dynamic_slice_in_dim(twice, start, owners * group, 0)[:, :mel_bins].T
     self_owner = lax.axis_index(("branch", "seq"))
-    utterance_frames_length = holder_utterance_length[self_owner]
-    wave = vocoder_synthesize(
-        holder_mel,
-        utterance_frames_length,
+    length = lax.dynamic_slice_in_dim(holder_utterance_length, self_owner, 1, 0)
+    return vocoder(
+        arrived,
+        length,
+        mel_bins,
         input_conv_weight,
         input_conv_bias,
         transposed_conv_weight,
@@ -219,7 +387,6 @@
         second_conv_weight,
         second_conv_bias,
     )
-    return wave[None]
 
 
 def solution(mesh):

time: 175 us -> 94.6 us (0.54)
  matrix products: 60.7 us -> 15.5 us
  local copies, waits for them, and re-layouts: 39.3 us -> 5.44 us
  other arithmetic: 36.8 us -> 8.61 us
  Pallas kernels: 0 us -> 27.1 us
  blocking collectives: 0 us -> 19.8 us
  starting transfers between devices: 18.2 us -> 6.91 us
  waiting for transfers between devices: 18.1 us -> 10.6 us
    dot_general x3 -> x0, matrix products: 45.1 us -> none  [the longest x2 35.9 us: dilated_output(): lax.dot_general(weight, stacked, (((0,), (0,)), ((), ())), preferred_elem...]
    slice x10 -> x0, local copies, waits for them, and re-layouts: 28.3 us -> none  [the longest x2 11.8 us: vocoder_synthesize(): early_part = shifted(phases[UP + pad_up:], -1)]
    convert_element_type x2 -> x0, other arithmetic: 27.2 us -> none  [the longest x1 27 us: vocoder_synthesize(): snake(upsampled.astype(jnp.float32), snake_freq_first).astype(jnp.bfloat16)]
    pallas_call x0 -> x1, Pallas kernels: none -> 27.1 us  [vocoder(): pl.pallas_call(functools.partial(vocoder_kernel, mel_bins=mel_bins), out_...]
    all_to_all x0 -> x1, blocking collectives: none -> 19.8 us  [local(): spread = lax.all_to_all(packed, 'seq', 0, 0, tiled=True)]
    all_to_all x1 -> x0, starting transfers between devices: 11.2 us -> none  [local(): spread = lax.all_to_all(packed, 'seq', 0, 0, tiled=True)]
    all_to_all x1 -> x0, waiting for transfers between devices: 7.36 us -> none  [local(): spread = lax.all_to_all(packed, 'seq', 0, 0, tiled=True)]
    broadcast_in_dim x1 -> x0, local copies, waits for them, and re-layouts: 4.63 us -> none  [local(): return wave[None]]
  transfers between devices with their start and end apart: 3 -> 2, of which waited for: 3 -> 2; matrix products, arithmetic and copies ran while one was open for 1% -> 1% of each run, Pallas kernels for 0% -> 0%
where the time goes in v2:
time: 94.6 us; the launch traced here: 94.3 us
  Pallas kernels  27.1 us (29%)
  blocking collectives  19.8 us (21%)
  matrix products  15.5 us (16%)
  waiting for transfers between devices  10.6 us (11%)
  other arithmetic  8.61 us (9%)
  starting transfers between devices  6.91 us (7%)
  local copies, waits for them, and re-layouts  5.44 us (6%)
    pallas_call x1, Pallas kernels, vocoder(): pl.pallas_call(functools.partial(vocoder_kernel, mel_bins=mel_bins), out_...  27.1 us
    all_to_all x1, blocking collectives, local(): spread = lax.all_to_all(packed, 'seq', 0, 0, tiled=True)  19.8 us
    dot_general x1, matrix products, velocity(): jnp.dot(active, feedforward_out_weight, preferred_element_type=jnp.float32)  12.4 us
    all_to_all x1, waiting for transfers between devices, local(): lax.all_to_all(slots.reshape(owners, group, LANES), ('branch', 'seq'), 0,...  9.86 us
    all_to_all x1, starting transfers between devices, local(): lax.all_to_all(slots.reshape(owners, group, LANES), ('branch', 'seq'), 0,...  5.42 us
    reduce_sum x2, other arithmetic, layer_norm(): row_var = jnp.mean(centred * centred, axis=-1, keepdims=True)  4.45 us
    unnamed x39, local copies, waits for them, and re-layouts  2.7 us
    dot_general x1, matrix products, velocity(): jnp.dot(final_norm, mel_velocity_weight, preferred_element_type=jnp.float32)  2.48 us
  transfers between devices with their start and end apart: 2, of which 2 were waited for; matrix products, arithmetic and copies ran while one was open for 1% of the time, Pallas kernels for 0%

profile of v2, /device:TPU:1, one launch (start us, length us, event | category | flops | bytes accessed | tf_op | source)
XLA Modules:
  0.0 94.3 jit_solution(661151366038190151)
XLA Ops:
  0.0 1.0 %slice_add_fusion = (f32[1,1024]{1,0:T(1,128)S(1)}, f32[1,1024]{1,0:T(1,128)S(1)}, f32[1,1024]{1,0:T(1,128)S(1)}, f32[1,1024]{1,0:T(1,128)S(1)}, f32[1,1024]{1,0:T(1,128)S(1)}) fusion(f32[5,1024]{1,0:T(8,128)} %param.24), kind=kLoop, calls=%fused_computation.40 | loop fusion | flops 2048 | bytes 40960 | tf_op jit(solution)/shard_map/add | solution.py:51
  1.0 1.7 %convert_reduce_fusion = f32[768]{0:T(1024)S(1)} fusion(bf16[1,768,1024]{2,1,0:T(8,128)(2,1)} %param.22), kind=kLoop, calls=%fused_computation.9 | loop fusion | flops 1572096 | bytes 1575936 | tf_op jit(solution)/shard_map/reduce_sum | solution.py:23
  2.7 2.0 %fusion.12 = f32[768]{0:T(1024)S(1)} fusion(bf16[1,768,1024]{2,1,0:T(8,128)(2,1)} %param.22, f32[768]{0:T(1024)S(1)} %broadcast_multiply_fusion.1), kind=kLoop, calls=%fused_computation.15 | loop fusion | flops 3144960 | bytes 1579008 | tf_op jit(solution)/shard_map/reduce_sum | solution.py:25
  4.7 12.4 %fusion.40 = (f32[768]{0:T(1024)S(1)}, f32[768,1024]{1,0:T(8,128)}) fusion(f32[1024]{0:T(1024)S(1)} %copy-done.16, bf16[2048,1024]{1,0:T(8,128)(2,1)} %param.27, bf16[1024,2048]{1,0:T(8,128)(2,1)} %param.25, f32[2048]{0:T(1024)S(1)} %copy-done.15, bf16[1,768,1024]{2,1,0:T(8,128)(2,1)S(1)} %copy-done.10, f32[1024]{0:T(1024)S(1)} %bitcast.55, ...), kind=kOutput, calls=%fused_computation.58 | convolution fusion | flops 6466829312 | bytes 13140992 | tf_op jit(solution)/shard_map/dot_general | solution.py:47
  17.1 2.5 %multiply_reduce_fusion = f32[768]{0:T(1024)S(1)} fusion(f32[768,1024]{1,0:T(8,128)} %get-tuple-element.11, f32[768]{0:T(1024)S(1)} %broadcast_multiply_fusion), kind=kLoop, calls=%fused_computation.20 | loop fusion | flops 2358528 | bytes 3151872 | tf_op jit(solution)/shard_map/reduce_sum | solution.py:25
  19.6 0.0 copy-start.13
  19.6 0.0 copy-start.14
  19.7 0.0 copy-done.17
  19.7 0.3 copy-done.11
  20.0 2.5 %fusion.22 = f32[768,128]{1,0:T(8,128)} fusion(f32[768,1024]{1,0:T(8,128)S(1)} %copy-done.11, f32[1024]{0:T(1024)S(1)} %bitcast.54, f32[1024]{0:T(1024)S(1)} %bitcast.53, f32[768]{0:T(1024)S(1)} %add_rsqrt_fusion, f32[768]{0:T(1024)S(1)} %broadcast_multiply_fusion, bf16[1024,100]{0,1:T(8,128)(2,1)} %param.29, f32[128]{0:T(128)S(1)} %pad.18), kind=kOutput, calls=%fused_computation.26 | convolution fusion | flops 205357056 | bytes 3758592 | tf_op jit(solution)/shard_map/dot_general | solution.py:54
  22.5 1.0 %constant_dynamic-slice_fusion = f32[384,128]{1,0:T(8,128)S(1)} fusion(f32[768,128]{1,0:T(8,128)} %fusion.22, s32[]{:T(128)S(6)} %select_n.48), kind=kLoop, calls=%fused_computation.49 | loop fusion | bytes 393220 | tf_op jit(solution)/shard_map/dynamic_slice | solution.py:345
  23.5 1.5 %collective-permute-start = (f32[384,128]{1,0:T(8,128)S(1)}, f32[384,128]{1,0:T(8,128)S(1)}, u32[]{:S(2)}, u32[]{:S(2)}) collective-permute-start(f32[384,128]{1,0:T(8,128)S(1)} %constant_dynamic-slice_fusion), channel_id=1, source_target_pairs={{0,64},{64,0},{1,65},{65,1},{2,66},{66,2},{3,67},{67,3},{4,68},{68... | collective-permute-start | bytes 589832 | tf_op jit(solution)/shard_map/ppermute | solution.py:346
  25.0 0.0 copy-done
  25.0 0.1 copy.25
  25.2 0.1 dynamic-slice_convert_fusion
  25.2 0.0 copy-done.14
  25.2 0.1 fusion.34
  25.3 0.7 collective-permute-done
  26.1 1.1 %select_convert_fusion = bf16[384,128]{1,0:T(8,128)(2,1)S(1)} fusion(f32[384,128]{1,0:T(8,128)S(1)} %collective-permute-done, f32[768,128]{1,0:T(8,128)} %fusion.22, s32[]{:T(128)S(6)} %select_n.46, f32[384,100]{1,0:T(8,128)S(1)} %bitcast.52, bf16[384]{0:T(512)(128)(2,1)S(1)} %dynamic-slice_convert_fusion, bf16[384]{0:T(512)(128)(2,1)S(1)} %fusion.34, ...), kind=kLoop, calls=%fused_computation.38 | loop fusion | flops 442368 | bytes 646917 | tf_op jit(solution)/shard_map/convert_element_type | solution.py:359
  27.2 0.0 copy-start.2
  27.2 0.0 copy-start.3
  27.2 0.0 copy-start.4
  27.2 0.0 copy-start.5
  27.2 0.0 copy-start.6
  27.2 0.0 copy-start.7
  27.2 0.0 copy-start.8
  27.2 0.0 copy-start.9
  27.3 19.8 %all_to_all.10 = bf16[64,6,128]{2,1,0:T(8,128)(2,1)S(1)} all-to-all(bf16[64,6,128]{2,1,0:T(8,128)(2,1)S(1)} %reshape.90), channel_id=1, replica_groups=mesh['branch'=2,'seq'=64] {'seq'}, dimensions={0} | all-to-all | bytes 196608 | tf_op jit(solution)/shard_map/all_to_all | solution.py:360
  47.1 0.2 fusion.30
  47.4 0.6 fusion.24
  48.0 0.8 reshape.92
  48.7 5.4 %all-to-all-start.1 = ((bf16[128,6,128]{2,1,0:T(8,128)(2,1)}), bf16[128,6,128]{2,1,0:T(8,128)(2,1)S(1)}, u32[]{:S(2)}, u32[]{:S(2)}) async-start(bf16[128,6,128]{2,1,0:T(8,128)(2,1)} %reshape.92), calls=%async_computation.1 | async-start | bytes 524288 | tf_op jit(solution)/shard_map/all_to_all | solution.py:370
  54.2 0.1 reshape.94
  54.3 0.6 dynamic_slice.18.length_ref
  54.9 0.1 pad.19
  55.0 9.9 %all-to-all-done.1 = bf16[128,6,128]{2,1,0:T(8,128)(2,1)S(1)} async-done(((bf16[128,6,128]{2,1,0:T(8,128)(2,1)}), bf16[128,6,128]{2,1,0:T(8,128)(2,1)S(1)}, u32[]{:S(2)}, u32[]{:S(2)}) %all-to-all-start.1) | async-done | bytes 196640 | tf_op jit(solution)/shard_map/all_to_all | solution.py:370
  64.9 0.1 reshape.93.arrived_ref
  64.9 0.0 copy-done.2
  64.9 0.0 copy-done.3
  65.0 0.0 copy-done.4
  65.0 0.0 copy-done.5
  65.0 0.0 copy-done.6
  65.0 0.0 copy-done.7
  65.0 0.0 copy-done.8
  65.0 0.0 copy-done.9
  65.0 0.0 copy-start.1
  65.0 2.2 %copy-done.1 = bf16[4096,512]{1,0:T(8,128)(2,1)S(1)} copy-done((bf16[4096,512]{1,0:T(8,128)(2,1)S(1)}, bf16[4096,512]{1,0:T(8,128)(2,1)}, u32[]{:S(2)}) %copy-start.1) | copy-done | bytes 4194328
  67.2 27.1 %vocoder.1 = bf16[1,256,6144]{2,1,0:T(8,128)(2,1)} custom-call(s32[1]{0:T(128)} %dynamic_slice.18.length_ref, bf16[768,128]{1,0:T(8,128)(2,1)S(1)} %reshape.93.arrived_ref, bf16[896,512]{1,0:T(8,128)(2,1)S(1)} %bitcast.43, f32[1,512]{1,0:T(1,128)S(1)} %bitcast.46, bf16[16,256,512]{2,1,0:T(8,128)(2,1)S(1)} %bitcast.42, f32[1,256]{1,0:T(1,128)S(1)} %bitcast.47, ...), custom_call_target="tpu_custom_call" | custom-call | tf_op jit(solution)/shard_map/vocoder/pallas_call | solution.py:273
  (23 shorter events, 0.1 us)
Async XLA Ops:
  0.0 25.0 %copy-start = (f32[100,768]{1,0:T(8,128)S(1)}, f32[100,768]{1,0:T(8,128)}, u32[]{:S(2)}) copy-start(f32[100,768]{1,0:T(8,128)} %param.23) | copy-start | bytes 921604
  0.0 4.7 %copy-start.10 = (bf16[1,768,1024]{2,1,0:T(8,128)(2,1)S(1)}, bf16[1,768,1024]{2,1,0:T(8,128)(2,1)}, u32[]{:S(2)}) copy-start(bf16[1,768,1024]{2,1,0:T(8,128)(2,1)} %param.22) | copy-start | bytes 4718596
  0.0 4.7 %copy-start.15 = (f32[2048]{0:T(1024)S(1)}, f32[2048]{0:T(1024)}, u32[]{:S(2)}) copy-start(f32[2048]{0:T(1024)} %param.26) | copy-start | bytes 24580
  0.0 4.7 %copy-start.16 = (f32[1024]{0:T(1024)S(1)}, f32[1024]{0:T(1024)}, u32[]{:S(2)}) copy-start(f32[1024]{0:T(1024)} %param.28) | copy-start | bytes 12292
  17.1 2.5 %copy-start.17 = (f32[100]{0:T(128)S(1)}, f32[100]{0:T(128)}, u32[]{:S(2)}) copy-start(f32[100]{0:T(128)} %param.30) | copy-start | bytes 1204
  17.1 2.8 %copy-start.11 = (f32[768,1024]{1,0:T(8,128)S(1)}, f32[768,1024]{1,0:T(8,128)}, u32[]{:S(2)}) copy-start(f32[768,1024]{1,0:T(8,128)} %get-tuple-element.11) | copy-start | bytes 9437188
  19.6 5.5 %copy-start.13 = (s32[768]{0:T(1024)S(1)}, s32[768]{0:T(1024)}, u32[]{:S(2)}) copy-start(s32[768]{0:T(1024)} %param.41) | copy-start | bytes 9220
  19.6 5.6 %copy-start.14 = (s32[768]{0:T(1024)S(1)}, s32[768]{0:T(1024)}, u32[]{:S(2)}) copy-start(s32[768]{0:T(1024)} %param.42) | copy-start | bytes 9220
  22.5 31.7 %copy-start.12 = (bf16[700,512]{1,0:T(8,128)(2,1)S(1)}, bf16[700,512]{1,0:T(8,128)(2,1)}, u32[]{:S(2)}) copy-start(bf16[700,512]{1,0:T(8,128)(2,1)} %param.31) | copy-start | bytes 2150404
  22.5 31.8 %copy-start.18 = (s32[128]{0:T(128)S(1)}, s32[128]{0:T(128)}, u32[]{:S(2)}) copy-start(s32[128]{0:T(128)} %param.43) | copy-start | bytes 1540
  23.5 2.6 %collective-permute-start = (f32[384,128]{1,0:T(8,128)S(1)}, f32[384,128]{1,0:T(8,128)S(1)}, u32[]{:S(2)}, u32[]{:S(2)}) collective-permute-start(f32[384,128]{1,0:T(8,128)S(1)} %constant_dynamic-slice_fusion), channel_id=1, source_target_pairs={{0,64},{64,0},{1,65},{65,1},{2,66},{66,2},{3,67},{67,3},{4,68},{68... | collective-permute-start | bytes 589832 | tf_op jit(solution)/shard_map/ppermute | solution.py:346
  27.2 37.8 %copy-start.2 = (bf16[768,256]{1,0:T(8,128)(2,1)S(1)}, bf16[768,256]{1,0:T(8,128)(2,1)}, u32[]{:S(2)}) copy-start(bf16[768,256]{1,0:T(8,128)(2,1)} %param.36) | copy-start | bytes 1179652
  27.2 37.8 %copy-start.3 = (bf16[768,256]{1,0:T(8,128)(2,1)S(1)}, bf16[768,256]{1,0:T(8,128)(2,1)}, u32[]{:S(2)}) copy-start(bf16[768,256]{1,0:T(8,128)(2,1)} %param.39) | copy-start | bytes 1179652
  27.2 37.8 %copy-start.4 = (f32[512]{0:T(512)S(1)}, f32[512]{0:T(512)}, u32[]{:S(2)}) copy-start(f32[512]{0:T(512)} %param.32) | copy-start | bytes 6148
  27.2 37.8 %copy-start.5 = (f32[256]{0:T(256)S(1)}, f32[256]{0:T(256)}, u32[]{:S(2)}) copy-start(f32[256]{0:T(256)} %param.34) | copy-start | bytes 3076
  27.2 37.8 %copy-start.6 = (f32[256]{0:T(256)S(1)}, f32[256]{0:T(256)}, u32[]{:S(2)}) copy-start(f32[256]{0:T(256)} %param.35) | copy-start | bytes 3076
  27.2 37.8 %copy-start.7 = (f32[256]{0:T(256)S(1)}, f32[256]{0:T(256)}, u32[]{:S(2)}) copy-start(f32[256]{0:T(256)} %param.37) | copy-start | bytes 3076
  27.2 37.8 %copy-start.8 = (f32[256]{0:T(256)S(1)}, f32[256]{0:T(256)}, u32[]{:S(2)}) copy-start(f32[256]{0:T(256)} %param.38) | copy-start | bytes 3076
  27.2 37.8 %copy-start.9 = (f32[256]{0:T(256)S(1)}, f32[256]{0:T(256)}, u32[]{:S(2)}) copy-start(f32[256]{0:T(256)} %param.40) | copy-start | bytes 3076
  48.7 16.1 %all-to-all-start.1 = ((bf16[128,6,128]{2,1,0:T(8,128)(2,1)}), bf16[128,6,128]{2,1,0:T(8,128)(2,1)S(1)}, u32[]{:S(2)}, u32[]{:S(2)}) async-start(bf16[128,6,128]{2,1,0:T(8,128)(2,1)} %reshape.92), calls=%async_computation.1 | async-start | bytes 524288 | tf_op jit(solution)/shard_map/all_to_all | solution.py:370
  65.0 2.2 %copy-start.1 = (bf16[4096,512]{1,0:T(8,128)(2,1)S(1)}, bf16[4096,512]{1,0:T(8,128)(2,1)}, u32[]{:S(2)}) copy-start(bf16[4096,512]{1,0:T(8,128)(2,1)} %param.33) | copy-start | bytes 12582916

commit v3 on v2

v3 whole, which is shorter than its diff:
```python
import functools
import math

import jax
import jax.numpy as jnp
from jax import lax
from jax.experimental import pallas as pl
from jax.experimental.pallas import tpu as pltpu
from jax.sharding import PartitionSpec as P

UP = 8
KT = 16
KPRE = 7
DILATION_RATE = 3
NFE = 16


GUIDE = 2.0
LANES = 128
GROUP = 8
GELU_SCALE = math.sqrt(2.0 / math.pi)


def layer_norm(row_block):
    row_mean = jnp.mean(row_block, axis=-1, keepdims=True)
    centred = row_block - row_mean
    row_var = jnp.mean(centred * centred, axis=-1, keepdims=True)
    return centred * lax.rsqrt(row_var + 1e-06)


def gelu_tanh(inner):
    slope = inner * (GELU_SCALE + (GELU_SCALE * 0.044715) * (inner * inner))
    half = 0.5 * inner
    return half + half * jnp.tanh(slope)


def velocity_kernel(
    side_ref,
    hidden_ref,
    modulation_ref,
    in_weight_ref,
    in_bias_ref,
    out_weight_ref,
    out_bias_ref,
    mel_weight_ref,
    mel_bias_ref,
    noisy_ref,
    holder_ref,
    position_ref,
    own_ref,
    sent_ref,
    base_ref,
    tall_ref,
    normed_ref,
    total_ref,
    *,
    block,
):
    frames = hidden_ref.shape[1]
    half_rows = own_ref.shape[0]
    norm_block = 128
    f32, bf16 = jnp.float32, jnp.bfloat16
    step = pl.program_id(0)

    @pl.when(step == 0)
    def _():
        scale = 1.0 + modulation_ref[1:2, :]
        for low in range(0, frames, norm_block):
            rows = slice(low, low + norm_block)
            normed = layer_norm(hidden_ref[0, rows, :].astype(f32)) * scale + modulation_ref[0:1, :]
            normed_ref[rows, :] = normed.astype(bf16)
            total_ref[rows, :] = jnp.broadcast_to(
                out_bias_ref[...], (norm_block, out_bias_ref.shape[1])
            )

        mel_bins = noisy_ref.shape[0]
        half = pl.ds(pl.multiple_of(side_ref[0] * half_rows, half_rows), half_rows)
        tall_ref[...] = jnp.zeros(tall_ref.shape, f32)
        tall_ref[:mel_bins, :] = noisy_ref[:, half]
        tall_ref[mel_bins : mel_bins + 1, :] = holder_ref[:, half].astype(f32)
        first_flag = jnp.where(position_ref[:, half] == 0, 1.0, 0.0)
        tall_ref[mel_bins + 1 : mel_bins + 2, :] = first_flag
        base_ref[...] = tall_ref[...].T

    for low in range(0, frames, block):
        rows = slice(low, low + block)
        inner = jnp.dot(normed_ref[rows, :], in_weight_ref[...], preferred_element_type=f32)
        active = gelu_tanh(inner + in_bias_ref[...]).astype(bf16)
        total_ref[rows, :] += jnp.dot(active, out_weight_ref[...], preferred_element_type=f32)

    @pl.when(step == pl.num_programs(0) - 1)
    def _():
        scale = 1.0 + modulation_ref[4:5, :]
        for low in range(0, frames, norm_block):
            rows = slice(low, low + norm_block)
            block_out = hidden_ref[0, rows, :].astype(f32) + modulation_ref[2:3, :] * total_ref[rows, :]
            normed_ref[rows, :] = (
                layer_norm(block_out) * scale + modulation_ref[3:4, :]
            ).astype(bf16)
        for part in range(2):
            rows = slice(part * half_rows, (part + 1) * half_rows)
            speed = (
                jnp.dot(normed_ref[rows, :], mel_weight_ref[...], preferred_element_type=f32)
                + mel_bias_ref[...]
            )

            @pl.when(side_ref[0] == part)
            def _(speed=speed):
                own_ref[...] = speed

            @pl.when(side_ref[0] != part)
            def _(speed=speed):
                sent_ref[...] = speed


def velocity_halves(
    side,
    hidden,
    modulation,
    feedforward_in_weight,
    feedforward_in_bias,
    feedforward_out_weight,
    feedforward_out_bias,
    mel_velocity_weight,
    mel_velocity_bias,
    noisy_mel_state,
    frame_holder,
    frame_position,
    block=768,
    chunk=1024,
):
    frames, width = hidden.shape[1:]
    hidden_units = feedforward_in_weight.shape[1]
    mel_bins = mel_velocity_weight.shape[1]
    half = jax.ShapeDtypeStruct((frames // 2, LANES), jnp.float32)
    whole = pl.Buffered(1)
    fixed = lambda i: (0, 0)
    return pl.pallas_call(
        functools.partial(velocity_kernel, block=block),
        out_shape=(half, half, half),
        grid=(hidden_units // chunk,),
        in_specs=[
            pl.BlockSpec(memory_space=pltpu.SMEM),
            pl.BlockSpec((1, frames, width), lambda i: (0, 0, 0), pipeline_mode=whole),
            pl.BlockSpec(modulation.shape, fixed, pipeline_mode=whole),
            pl.BlockSpec((width, chunk), lambda i: (0, i)),
            pl.BlockSpec((1, chunk), lambda i: (0, i)),
            pl.BlockSpec((chunk, width), lambda i: (i, 0)),
            pl.BlockSpec((1, width), fixed, pipeline_mode=whole),
            pl.BlockSpec((width, LANES), fixed, pipeline_mode=whole),
            pl.BlockSpec((1, LANES), fixed, pipeline_mode=whole),
            pl.BlockSpec(noisy_mel_state.shape, fixed, pipeline_mode=whole),
            pl.BlockSpec((1, frames), fixed, pipeline_mode=whole),
            pl.BlockSpec((1, frames), fixed, pipeline_mode=whole),
        ],
        out_specs=(pl.BlockSpec(half.shape, fixed),) * 3,
        scratch_shapes=[
            pltpu.VMEM((LANES, frames // 2), jnp.float32),
            pltpu.VMEM((frames, width), jnp.bfloat16),
            pltpu.VMEM((frames, width), jnp.float32),
        ],
        compiler_params=pltpu.CompilerParams(vmem_limit_bytes=40 * 1024 * 1024),
        name="velocity",
    )(
        side,
        hidden,
        modulation,
        feedforward_in_weight,
        feedforward_in_bias[None],
        feedforward_out_weight,
        feedforward_out_bias[None],
        jnp.pad(mel_velocity_weight, ((0, 0), (0, LANES - mel_bins))),
        jnp.pad(mel_velocity_bias, (0, LANES - mel_bins))[None],
        noisy_mel_state,
        frame_holder[None],
        frame_position[None],
    )


def combine_kernel(side_ref, own_ref, peer_ref, base_ref, packed_ref, spaced_ref):
    chips = packed_ref.shape[0]
    step_size = math.cos(0.5 * math.pi * (NFE - 1) / NFE)
    first = side_ref[0] == 0
    conditional = jnp.where(first, own_ref[...], peer_ref[...])
    unconditional = jnp.where(first, peer_ref[...], own_ref[...])
    guided = (1.0 + GUIDE) * conditional - GUIDE * unconditional
    refined = base_ref[...] + step_size * guided
    for turn in range(GROUP):
        low = turn * chips
        if low < refined.shape[0]:
            spaced_ref[pl.ds(turn, chips, stride=GROUP), :] = refined[low : low + chips, :]
        else:
            spaced_ref[pl.ds(turn, chips, stride=GROUP), :] = jnp.zeros((chips, LANES), jnp.float32)
    packed_ref[...] = spaced_ref[...].reshape(packed_ref.shape).astype(packed_ref.dtype)


def sort_kernel(spread_ref, slots_ref, spaced_ref, *, mel_bins):
    owners = slots_ref.shape[0]
    rows = spread_ref[...].reshape(-1, LANES)
    count = rows.shape[0]
    column = jnp.broadcast_to(rows[:, mel_bins : mel_bins + 1].astype(jnp.float32), (count, owners))
    owner_of = column.T
    owner = lax.broadcasted_iota(jnp.int32, (owners, count), 0).astype(jnp.float32)
    turn_of = lax.rem(lax.broadcasted_iota(jnp.int32, (1, count), 1), GROUP)
    for turn in range(GROUP):
        pick = ((owner_of == owner) & (turn_of == turn)).astype(jnp.bfloat16)
        spaced_ref[pl.ds(turn, owners, stride=GROUP), :] = jnp.dot(
            pick, rows, preferred_element_type=jnp.float32
        )
    slots_ref[...] = spaced_ref[...].reshape(slots_ref.shape).astype(slots_ref.dtype)


SIN_TERMS = (
    3.141592579805583,
    -5.167706866168128,
    2.550031193522954,
    -0.5980441939334223,
    0.07721838619602994,
)


def snake_rows(signal, turns, inverse):
    half_turns = signal * turns
    part = half_turns - jnp.round(half_turns)
    square = part * part
    poly = SIN_TERMS[4] * square + SIN_TERMS[3]
    poly = poly * square + SIN_TERMS[2]
    poly = poly * square + SIN_TERMS[1]
    poly = poly * square + SIN_TERMS[0]
    sine = poly * part
    return signal + sine * sine * inverse


def nt_dot(left, right):
    return lax.dot_general(
        left, right, (((1,), (1,)), ((), ())), preferred_element_type=jnp.float32
    )


def vocoder_kernel(
    length_ref,
    arrived_ref,
    input_weight_ref,
    input_bias_ref,
    up_weight_hbm,
    up_bias_ref,
    freq_first_ref,
    dilated_weight_ref,
    dilated_bias_ref,
    freq_second_ref,
    second_weight_ref,
    second_bias_ref,
    wave_ref,
    mel_ref,
    taps_ref,
    shift_wide_ref,
    pre_ref,
    shift_ref,
    up_ref,
    first_ref,
    second_ref,
    out_ref,
    up_weight_ref,
    up_sem,
    even_ref,
    odd_ref,
    *,
    mel_bins,
    block,
):
    frames = up_ref.shape[1]
    piece_frames = out_ref.shape[1] // pl.num_programs(0)
    part_rows = arrived_ref.shape[0] // 2
    blocks = frames // block
    halo = 8
    f32, bf16 = jnp.float32, jnp.bfloat16
    step = pl.program_id(0)
    length = length_ref[0]

    def keep_rows(first, count):
        row = lax.broadcasted_iota(jnp.int32, (count, 1), 0) + first
        return row < length

    @pl.when(step == 0)
    def _():
        up_copy = pltpu.make_async_copy(up_weight_hbm, up_weight_ref, up_sem)
        up_copy.start()
        arrived = arrived_ref[...]

        def shard_row(shape, axis):
            i = lax.broadcasted_iota(jnp.int32, shape, axis)
            side = (i >= part_rows).astype(jnp.int32)
            inner = i - side * part_rows
            turn = lax.rem(inner, GROUP)
            row = side * (frames // 2) + turn * (part_rows // GROUP) + inner // GROUP
            return jnp.where(turn < frames * GROUP // (2 * part_rows), row, -4 * frames)

        lane = lax.broadcasted_iota(jnp.int32, arrived.shape, 1)
        flagged = jnp.where(lane == mel_bins + 1, arrived.astype(f32), 0.0)
        start = jnp.sum(
            jnp.where(flagged > 0.5, shard_row(arrived.shape, 0).astype(f32), 0.0), keepdims=True
        ).astype(jnp.int32)
        mel_ref[...] = jnp.zeros(mel_ref.shape, f32)
        turned = shard_row((1, arrived.shape[0]), 1) - start
        for i in range(frames // 128):
            ahead = turned - i * 128 - lax.broadcasted_iota(jnp.int32, (128, 1), 0)
            pick = ((ahead == 0) | (ahead == -frames)).astype(bf16)
            mel_ref[halo + i * 128 : halo + (i + 1) * 128, :] = jnp.dot(
                pick, arrived, preferred_element_type=f32
            )
        for k in range(KPRE):
            low = halo + k - KPRE // 2
            taps_ref[:, k * LANES : (k + 1) * LANES] = mel_ref[low : low + frames, :].astype(bf16)
        shift_wide_ref[...] = jnp.zeros(shift_wide_ref.shape, f32)
        for i in range(blocks):
            rows = slice(i * block, (i + 1) * block)
            pre = jnp.dot(taps_ref[rows, :], input_weight_ref[...], preferred_element_type=f32)
            pre = jnp.where(keep_rows(i * block, block), pre + input_bias_ref[...], 0.0)
            shift_wide_ref[halo + i * block : halo + (i + 1) * block, :] = pre
        for k in range(3):
            low = halo + k - 1
            pre_ref[k] = shift_wide_ref[low : low + frames, :].astype(bf16)
        shift_ref[...] = jnp.zeros(shift_ref.shape, f32)

        turns_first = freq_first_ref[...] * (1.0 / math.pi)
        inverse_first = 1.0 / freq_first_ref[...]
        turns_second = freq_second_ref[...] * (1.0 / math.pi)
        inverse_second = 1.0 / freq_second_ref[...]

        def neighbour_rows(offset):
            low = halo + offset
            return shift_ref[low : low + frames, :].astype(bf16)

        up_copy.wait()

        def pipeline(product, finish):
            for i in range(blocks):
                rows = slice(i * block, (i + 1) * block)
                even_ref[rows, :] = product(0, rows)

            @pl.loop(0, UP // 2)
            def _(pair):
                for r, ready_ref, r_next, next_ref in (
                    (2 * pair, even_ref, 2 * pair + 1, odd_ref),
                    (2 * pair + 1, odd_ref, jnp.minimum(2 * pair + 2, UP - 1), even_ref),
                ):
                    for i in range(blocks):
                        rows = slice(i * block, (i + 1) * block)
                        next_ref[rows, :] = product(r_next, rows)
                        for low in range(i * block, (i + 1) * block, 64):
                            finish(r, low, ready_ref[low : low + 64, :])

        def up_product(r, rows):
            side = jnp.where(r < UP // 2, 0, 2)
            return jnp.dot(
                jnp.concatenate([pre_ref[1, rows, :], pre_ref[side, rows, :]], axis=1),
                jnp.concatenate(
                    [up_weight_ref[r + UP // 2], up_weight_ref[lax.rem(r + UP // 2 + UP, KT)]],
                    axis=0,
                ),
                preferred_element_type=f32,
            )

        def up_finish(r, low, up):
            rows = slice(low, low + 64)
            up = jnp.where(keep_rows(low, 64), up + up_bias_ref[...], 0.0)
            up = up.astype(bf16)
            up_ref[r, rows, :] = up
            first = snake_rows(up.astype(f32), turns_first, inverse_first)
            first_ref[r + 3, rows, :] = first.astype(bf16)

        pipeline(up_product, up_finish)

        for r in range(DILATION_RATE):
            shift_ref[halo : halo + frames, :] = first_ref[r + 3].astype(f32)
            first_ref[r + 3 + UP] = neighbour_rows(1)
        for r in range(UP - DILATION_RATE, UP):
            shift_ref[halo : halo + frames, :] = first_ref[r + 3].astype(f32)
            first_ref[r + 3 - UP] = neighbour_rows(-1)

        def inner_product(r, rows):
            around = [first_ref[r + DILATION_RATE * k, rows, :] for k in range(3)]
            return jnp.dot(
                jnp.concatenate(around, axis=1),
                dilated_weight_ref[...],
                preferred_element_type=f32,
            )

        def inner_finish(r, low, inner):
            inner = jnp.where(keep_rows(low, 64), inner + dilated_bias_ref[...], 0.0)
            second = snake_rows(inner, turns_second, inverse_second)
            second_ref[r + 1, low : low + 64, :] = second.astype(bf16)

        pipeline(inner_product, inner_finish)

        shift_ref[halo : halo + frames, :] = second_ref[1].astype(f32)
        second_ref[UP + 1] = neighbour_rows(1)
        shift_ref[halo : halo + frames, :] = second_ref[UP].astype(f32)
        second_ref[0] = neighbour_rows(-1)

        def outer_product(r, rows):
            around = [second_ref[r + k, rows, :] for k in range(3)]
            return jnp.dot(
                jnp.concatenate(around, axis=1),
                second_weight_ref[...],
                preferred_element_type=f32,
            )

        def outer_finish(r, low, outer):
            rows = slice(low, low + 64)
            outer = jnp.where(keep_rows(low, 64), outer + second_bias_ref[...], 0.0)
            out_ref[r, rows, :] = (up_ref[r, rows, :].astype(f32) + outer).astype(bf16)

        pipeline(outer_product, outer_finish)

    base = pl.multiple_of(step * piece_frames, piece_frames)
    narrow = 256 // UP
    row = lax.broadcasted_iota(jnp.int32, (256, 256), 0)
    col = lax.broadcasted_iota(jnp.int32, (256, 256), 1)
    weave = (col == lax.rem(row, narrow) * UP + row // narrow).astype(bf16)
    for piece in range(piece_frames // narrow):
        rows = pl.ds(base + piece * narrow, narrow)
        phases = jnp.concatenate([out_ref[r, rows, :] for r in range(UP)], axis=0)
        woven = lax.dot_general(
            phases, weave, (((0,), (0,)), ((), ())), preferred_element_type=f32
        )
        wave_ref[0, :, piece * 256 : (piece + 1) * 256] = woven.astype(bf16)


def vocoder(
    arrived,
    length,
    mel_bins,
    input_conv_weight,
    input_conv_bias,
    transposed_conv_weight,
    transposed_conv_bias,
    snake_freq_first,
    dilated_conv_weight,
    dilated_conv_bias,
    snake_freq_second,
    second_conv_weight,
    second_conv_bias,
    frames,
    block=256,
    piece=256,
):
    wide = input_conv_bias.shape[0]
    channels = transposed_conv_bias.shape[0]
    f32, bf16 = jnp.float32, jnp.bfloat16
    taps_weight = jnp.pad(
        input_conv_weight.reshape(KPRE, mel_bins, wide), ((0, 0), (0, LANES - mel_bins), (0, 0))
    ).reshape(KPRE * LANES, wide)
    operands = [
        arrived,
        taps_weight,
        input_conv_bias[None],
        transposed_conv_weight.reshape(KT, channels, wide).transpose(0, 2, 1),
        transposed_conv_bias[None],
        snake_freq_first[None],
        dilated_conv_weight,
        dilated_conv_bias[None],
        snake_freq_second[None],
        second_conv_weight,
        second_conv_bias[None],
    ]
    return pl.pallas_call(
        functools.partial(vocoder_kernel, mel_bins=mel_bins, block=block),
        out_shape=jax.ShapeDtypeStruct((1, channels, frames * UP), bf16),
        grid=(frames // piece,),
        in_specs=[pl.BlockSpec(memory_space=pltpu.SMEM)]
        + [
            pl.BlockSpec(memory_space=pl.ANY)
            if x.ndim == 3 and x.shape[0] == KT
            else pl.BlockSpec(x.shape, lambda i, n=x.ndim: (0,) * n, pipeline_mode=pl.Buffered(1))
            for x in operands
        ],
        out_specs=pl.BlockSpec((1, channels, piece * UP), lambda i: (0, 0, i)),
        scratch_shapes=[
            pltpu.VMEM((frames + 16, LANES), f32),
            pltpu.VMEM((frames, KPRE * LANES), bf16),
            pltpu.VMEM((frames + 16, wide), f32),
            pltpu.VMEM((3, frames, wide), bf16),
            pltpu.VMEM((frames + 16, channels), f32),
            pltpu.VMEM((UP, frames, channels), bf16),
            pltpu.VMEM((UP + 6, frames, channels), bf16),
            pltpu.VMEM((UP + 2, frames, channels), bf16),
            pltpu.VMEM((UP, frames, channels), bf16),
            pltpu.VMEM((KT, wide, channels), bf16),
            pltpu.SemaphoreType.DMA(()),
            pltpu.VMEM((frames, channels), f32),
            pltpu.VMEM((frames, channels), f32),
        ],
        compiler_params=pltpu.CompilerParams(vmem_limit_bytes=48 * 1024 * 1024),
        name="vocoder",
    )(length, *operands)


def local(
    hidden,
    noisy_mel_state,
    modulation,
    feedforward_in_weight,
    feedforward_in_bias,
    feedforward_out_weight,
    feedforward_out_bias,
    mel_velocity_weight,
    mel_velocity_bias,
    input_conv_weight,
    input_conv_bias,
    transposed_conv_weight,
    transposed_conv_bias,
    snake_freq_first,
    dilated_conv_weight,
    dilated_conv_bias,
    snake_freq_second,
    second_conv_weight,
    second_conv_bias,
    frame_holder,
    frame_position,
    holder_utterance_length,
):
    chips = lax.axis_size("seq")
    owners = lax.axis_size("branch") * chips
    mel_bins, frames = noisy_mel_state.shape
    side = lax.axis_index("branch").astype(jnp.int32)[None]
    own_half, sent_half, base = velocity_halves(
        side,
        hidden,
        modulation,
        feedforward_in_weight,
        feedforward_in_bias,
        feedforward_out_weight,
        feedforward_out_bias,
        mel_velocity_weight,
        mel_velocity_bias,
        noisy_mel_state,
        frame_holder,
        frame_position,
    )
    peer_half = lax.ppermute(sent_half, "branch", [(0, 1), (1, 0)])
    packed = pl.pallas_call(
        combine_kernel,
        out_shape=jax.ShapeDtypeStruct((chips, GROUP, LANES), jnp.bfloat16),
        in_specs=[pl.BlockSpec(memory_space=pltpu.SMEM)]
        + [pl.BlockSpec(memory_space=pltpu.VMEM)] * 3,
        scratch_shapes=[pltpu.VMEM((chips * GROUP, LANES), jnp.float32)],
        name="combine",
    )(side, own_half, peer_half, base)
    spread = lax.all_to_all(packed, "seq", 0, 0, tiled=True)
    slots = pl.pallas_call(
        functools.partial(sort_kernel, mel_bins=mel_bins),
        out_shape=jax.ShapeDtypeStruct((owners, GROUP, LANES), jnp.bfloat16),
        scratch_shapes=[pltpu.VMEM((owners * GROUP, LANES), jnp.float32)],
        name="sort",
    )(spread)
    arrived = lax.all_to_all(slots, ("branch", "seq"), 0, 0, tiled=True)
    arrived = arrived.reshape(owners * GROUP, LANES)
    self_owner = lax.axis_index(("branch", "seq"))
    length = lax.dynamic_slice_in_dim(holder_utterance_length, self_owner, 1, 0)
    return vocoder(
        arrived,
        length,
        mel_bins,
        input_conv_weight,
        input_conv_bias,
        transposed_conv_weight,
        transposed_conv_bias,
        snake_freq_first,
        dilated_conv_weight,
        dilated_conv_bias,
        snake_freq_second,
        second_conv_weight,
        second_conv_bias,
        frames,
    )


def solution(mesh):
    return jax.shard_map(
        local,
        mesh=mesh,
        in_specs=(
            P("branch", "seq", None),
            P(None, "seq"),
            P(),
            P(),
            P(),
            P(),
            P(),
            P(),
            P(),
            P(),
            P(),
            P(),
            P(),
            P(),
            P(),
            P(),
            P(),
            P(),
            P(),
            P("seq"),
            P("seq"),
            P(),
        ),
        out_specs=P(("branch", "seq"), None, None),
        check_vma=False,
    )
```

time: 94.6 us -> 94.8 us (level)
  local copies, waits for them, and re-layouts: 5.44 us -> 23.6 us
  matrix products: 15.5 us -> 0 us
  Pallas kernels: 27.1 us -> 38.8 us
  other arithmetic: 8.61 us -> 0 us
  waiting for transfers between devices: 10.6 us -> 4.35 us
    dot_general x3 -> x0, matrix products: 15.5 us -> none  [the longest x1 12.4 us: velocity(): jnp.dot(active, feedforward_out_weight, preferred_element_type=jnp.float32)]
    pallas_call x1 -> x4, Pallas kernels: 27.1 us -> 38.8 us  [the longest x1 23.5 us: vocoder(): pl.pallas_call(functools.partial(vocoder_kernel, mel_bins=mel_bins, block...]
    unnamed x39 -> x43, local copies, waits for them, and re-layouts: 2.7 us -> 14.3 us
    all_to_all x1, waiting for transfers between devices: 9.86 us -> 3.28 us  [local(): arrived = lax.all_to_all(slots, ('branch', 'seq'), 0, 0, tiled=True)]
    reduce_sum x3 -> x0, other arithmetic: 6.13 us -> none  [the longest x2 4.45 us: layer_norm(): row_var = jnp.mean(centred * centred, axis=-1, keepdims=True)]
    reshape x4 -> x1, local copies, waits for them, and re-layouts: 0.92 us -> 6.44 us  [vocoder(): transposed_conv_weight.reshape(KT, channels, wide).transpose(0, 2, 1)]
    broadcast_in_dim x0 -> x3, local copies, waits for them, and re-layouts: none -> 2.04 us  [the longest x1 0.69 us: velocity_halves(): frame_position[None]]
    convert_element_type x3 -> x0, other arithmetic: 1.25 us -> none  [the longest x1 1.1 us: local(): packed = refined.astype(jnp.bfloat16).reshape(chips, group, LANES)]
  transfers between devices with their start and end apart: 2 -> 2, of which waited for: 2 -> 2; matrix products, arithmetic and copies ran while one was open for 1% -> 8% of each run, Pallas kernels for 0% -> 0%
where the time goes in v3:
time: 94.8 us; the launch traced here: 94 us
  Pallas kernels  38.8 us (41%)
  local copies, waits for them, and re-layouts  23.6 us (25%)
  blocking collectives  20 us (21%)
  starting transfers between devices  6.77 us (7%)
  waiting for transfers between devices  4.35 us (5%)
    pallas_call x1, Pallas kernels, vocoder(): pl.pallas_call(functools.partial(vocoder_kernel, mel_bins=mel_bins, block...  23.5 us
    all_to_all x1, blocking collectives, local(): spread = lax.all_to_all(packed, 'seq', 0, 0, tiled=True)  20 us
    unnamed x43, local copies, waits for them, and re-layouts  14.3 us
    pallas_call x1, Pallas kernels, velocity_halves(): pl.pallas_call(functools.partial(velocity_kernel, block=block), out_shape...  11.2 us
    reshape x1, local copies, waits for them, and re-layouts, vocoder(): transposed_conv_weight.reshape(KT, channels, wide).transpose(0, 2, 1)  6.44 us
    all_to_all x1, starting transfers between devices, local(): arrived = lax.all_to_all(slots, ('branch', 'seq'), 0, 0, tiled=True)  5.39 us
    all_to_all x1, waiting for transfers between devices, local(): arrived = lax.all_to_all(slots, ('branch', 'seq'), 0, 0, tiled=True)  3.28 us
    pallas_call x1, Pallas kernels, local(): pl.pallas_call(functools.partial(sort_kernel, mel_bins=mel_bins), out_sha...  2.19 us
  transfers between devices with their start and end apart: 2, of which 2 were waited for; matrix products, arithmetic and copies ran while one was open for 8% of the time, Pallas kernels for 0%

profile of v3, /device:TPU:1, one launch (start us, length us, event | category | flops | bytes accessed | tf_op | source)
XLA Modules:
  0.0 94.0 jit_solution(704793258824038733)
XLA Ops:
  0.0 0.7 pad_bitcast_fusion.mel_bias_ref
  0.7 0.7 broadcast_in_dim.40.holder_ref
  1.3 0.7 broadcast_in_dim.41.position_ref
  2.0 1.1 %copy.24 = bf16[1024,100]{1,0:T(8,128)(2,1)S(1)} copy(bf16[1024,100]{0,1:T(8,128)(2,1)} %param.29) | data formatting | bytes 409600 | tf_op args[7]
  3.2 0.1 pad.12.mel_weight_ref
  3.2 0.0 copy-start.1
  3.2 2.2 %copy-done.1 = bf16[1024,2048]{1,0:T(8,128)(2,1)S(1)} copy-done((bf16[1024,2048]{1,0:T(8,128)(2,1)S(1)}, bf16[1024,2048]{1,0:T(8,128)(2,1)}, u32[]{:S(2)}) %copy-start.1) | copy-done | bytes 4194328
  5.4 2.2 %copy-done.2 = bf16[2048,1024]{1,0:T(8,128)(2,1)S(1)} copy-done((bf16[2048,1024]{1,0:T(8,128)(2,1)S(1)}, bf16[2048,1024]{1,0:T(8,128)(2,1)}, u32[]{:S(2)}) %copy-start.2) | copy-done | bytes 4194328
  7.6 1.4 %copy-done.3 = bf16[1,768,1024]{2,1,0:T(8,128)(2,1)S(1)} copy-done((bf16[1,768,1024]{2,1,0:T(8,128)(2,1)S(1)}, bf16[1,768,1024]{2,1,0:T(8,128)(2,1)}, u32[]{:S(2)}) %copy-start.3) | copy-done | bytes 1572888
  9.0 1.0 %copy-done.6 = f32[100,768]{1,0:T(8,128)S(1)} copy-done((f32[100,768]{1,0:T(8,128)S(1)}, f32[100,768]{1,0:T(8,128)}, u32[]{:S(2)}) %copy-start.6) | copy-done | bytes 307224
  10.0 0.8 copy-done.9
  10.7 0.7 copy-done.10
  11.4 0.7 copy-done.11
  12.1 11.2 %velocity.1 = (f32[384,128]{1,0:T(8,128)S(1)}, f32[384,128]{1,0:T(8,128)S(1)}, f32[384,128]{1,0:T(8,128)S(1)}) custom-call(s32[1]{0:T(128)} %bitcast.side_ref, bf16[1,768,1024]{2,1,0:T(8,128)(2,1)S(1)} %copy-done.3, f32[5,1024]{1,0:T(8,128)S(1)} %copy-done.9, bf16[1024,2048]{1,0:T(8,128)(2,1)S(1)} %copy-done.1, f32[1,2048]{1,0:T(1,128)S(1)} %bitcast.18, ...), custom_call_target="tpu_custom_call" | custom-call | tf_op jit(solution)/shard_map/velocity/pallas_call | solution.py:138
  23.3 0.0 copy-start.7
  23.3 0.7 copy-done.7
  24.0 0.7 copy-done.8
  24.6 1.4 %collective-permute-start = (f32[384,128]{1,0:T(8,128)S(1)}, f32[384,128]{1,0:T(8,128)S(1)}, u32[]{:S(2)}, u32[]{:S(2)}) collective-permute-start(f32[384,128]{1,0:T(8,128)S(1)} %get-tuple-element.9), channel_id=1, source_target_pairs={{0,64},{64,0},{1,65},{65,1},{2,66},{66,2},{3,67},{67,3},{4,68},{68... | collective-permute-start | bytes 589832 | tf_op jit(solution)/shard_map/ppermute | solution.py:541
  26.0 1.1 %collective-permute-done.peer_ref = f32[384,128]{1,0:T(8,128)S(1)} collective-permute-done((f32[384,128]{1,0:T(8,128)S(1)}, f32[384,128]{1,0:T(8,128)S(1)}, u32[]{:S(2)}, u32[]{:S(2)}) %collective-permute-start) | collective-permute-done | bytes 196640 | tf_op jit(solution)/shard_map/ppermute | solution.py:541
  27.1 0.7 copy-done.19
  27.8 1.9 %combine.1 = bf16[64,8,128]{2,1,0:T(8,128)(2,1)} custom-call(s32[1]{0:T(128)} %bitcast.side_ref, f32[384,128]{1,0:T(8,128)} %copy-done.7, f32[384,128]{1,0:T(8,128)} %copy-done.19, f32[384,128]{1,0:T(8,128)} %copy-done.8), custom_call_target="tpu_custom_call" | custom-call | tf_op jit(solution)/shard_map/combine/pallas_call | solution.py:542
  29.7 20.0 %all_to_all.10.spread_ref = bf16[64,8,128]{2,1,0:T(8,128)(2,1)} all-to-all(bf16[64,8,128]{2,1,0:T(8,128)(2,1)} %combine.1), channel_id=1, replica_groups=mesh['branch'=2,'seq'=64] {'seq'}, dimensions={0} | all-to-all | bytes 262144 | tf_op jit(solution)/shard_map/all_to_all | solution.py:550
  49.7 2.2 %sort.1 = bf16[128,8,128]{2,1,0:T(8,128)(2,1)} custom-call(bf16[64,8,128]{2,1,0:T(8,128)(2,1)} %all_to_all.10.spread_ref), custom_call_target="tpu_custom_call" | custom-call | tf_op jit(solution)/shard_map/sort/pallas_call | solution.py:551
  51.9 5.4 %all-to-all-start.1 = ((bf16[128,8,128]{2,1,0:T(8,128)(2,1)}), bf16[128,8,128]{2,1,0:T(8,128)(2,1)S(1)}, u32[]{:S(2)}, u32[]{:S(2)}) async-start(bf16[128,8,128]{2,1,0:T(8,128)(2,1)} %sort.1), calls=%async_computation.1 | async-start | bytes 524288 | tf_op jit(solution)/shard_map/all_to_all | solution.py:557
  57.3 0.0 copy-done.18
  57.3 0.1 reshape.13
  57.4 0.1 pad.14
  57.5 0.0 copy-start.20
  57.5 0.0 copy-start.4
  57.6 0.0 copy-start.5
  57.6 0.0 copy-start.12
  57.6 0.0 copy-start.13
  57.6 0.0 copy-start.14
  57.6 0.0 copy-start.15
  57.6 0.0 copy-start.16
  57.6 0.0 copy-start.17
  57.6 6.4 %copy.25 = bf16[16,256,512]{1,2,0:T(8,128)(2,1)} copy(bf16[16,256,512]{2,1,0:T(8,128)(2,1)} %bitcast.26) | data formatting | bytes 8388608 | tf_op jit(solution)/shard_map/reshape | solution.py:458
  64.1 0.0 copy-done.20
  64.1 0.6 dynamic_slice.3.length_ref
  64.7 3.3 %all-to-all-done.1 = bf16[128,8,128]{2,1,0:T(8,128)(2,1)S(1)} async-done(((bf16[128,8,128]{2,1,0:T(8,128)(2,1)}), bf16[128,8,128]{2,1,0:T(8,128)(2,1)S(1)}, u32[]{:S(2)}, u32[]{:S(2)}) %all-to-all-start.1) | async-done | bytes 262176 | tf_op jit(solution)/shard_map/all_to_all | solution.py:557
  68.0 0.0 copy-done.4
  68.0 0.0 copy-done.5
  68.0 0.0 copy-done.12
  68.0 0.0 copy-done.13
  68.0 0.0 copy-done.14
  68.0 0.0 copy-done.15
  68.1 2.2 %copy-done = bf16[16,256,512]{1,2,0:T(8,128)(2,1)S(1)} copy-done((bf16[16,256,512]{1,2,0:T(8,128)(2,1)S(1)}, bf16[16,256,512]{1,2,0:T(8,128)(2,1)}, u32[]{:S(2)}) %copy-start) | copy-done | bytes 4194328
  70.3 23.5 %vocoder.1 = bf16[1,256,6144]{2,1,0:T(8,128)(2,1)} custom-call(s32[1]{0:T(128)} %dynamic_slice.3.length_ref, bf16[1024,128]{1,0:T(8,128)(2,1)S(1)} %bitcast.17, bf16[896,512]{1,0:T(8,128)(2,1)S(1)} %bitcast.16, f32[1,512]{1,0:T(1,128)S(1)} %bitcast.20, bf16[16,512,256]{2,1,0:T(8,128)(2,1)S(1)} %bitcast.15, f32[1,256]{1,0:T(1,128)S(1)} %bitcast.21, ...), custom_call_target="tpu_custom_call" | custom-call | tf_op jit(solution)/shard_map/vocoder/pallas_call | solution.py:467
  (12 shorter events, 0.0 us)
Async XLA Ops:
  3.2 2.2 %copy-start.1 = (bf16[1024,2048]{1,0:T(8,128)(2,1)S(1)}, bf16[1024,2048]{1,0:T(8,128)(2,1)}, u32[]{:S(2)}) copy-start(bf16[1024,2048]{1,0:T(8,128)(2,1)} %in_weight_ref.1) | copy-start | bytes 12582916
  5.4 2.2 %copy-start.2 = (bf16[2048,1024]{1,0:T(8,128)(2,1)S(1)}, bf16[2048,1024]{1,0:T(8,128)(2,1)}, u32[]{:S(2)}) copy-start(bf16[2048,1024]{1,0:T(8,128)(2,1)} %out_weight_ref.1) | copy-start | bytes 12582916
  7.6 1.4 %copy-start.3 = (bf16[1,768,1024]{2,1,0:T(8,128)(2,1)S(1)}, bf16[1,768,1024]{2,1,0:T(8,128)(2,1)}, u32[]{:S(2)}) copy-start(bf16[1,768,1024]{2,1,0:T(8,128)(2,1)} %hidden_ref.1) | copy-start | bytes 4718596
  9.0 1.0 %copy-start.6 = (f32[100,768]{1,0:T(8,128)S(1)}, f32[100,768]{1,0:T(8,128)}, u32[]{:S(2)}) copy-start(f32[100,768]{1,0:T(8,128)} %noisy_ref.1) | copy-start | bytes 921604
  10.0 0.8 copy-start.9
  10.7 0.7 copy-start.10
  11.4 0.7 copy-start.11
  12.1 45.2 %copy-start.18 = (bf16[700,512]{1,0:T(8,128)(2,1)S(1)}, bf16[700,512]{1,0:T(8,128)(2,1)}, u32[]{:S(2)}) copy-start(bf16[700,512]{1,0:T(8,128)(2,1)} %param.31) | copy-start | bytes 2150404
  23.3 0.7 copy-start.7
  24.0 0.7 copy-start.8
  24.6 2.5 %collective-permute-start = (f32[384,128]{1,0:T(8,128)S(1)}, f32[384,128]{1,0:T(8,128)S(1)}, u32[]{:S(2)}, u32[]{:S(2)}) collective-permute-start(f32[384,128]{1,0:T(8,128)S(1)} %get-tuple-element.9), channel_id=1, source_target_pairs={{0,64},{64,0},{1,65},{65,1},{2,66},{66,2},{3,67},{67,3},{4,68},{68... | collective-permute-start | bytes 589832 | tf_op jit(solution)/shard_map/ppermute | solution.py:541
  27.1 0.7 copy-start.19
  51.9 16.1 %all-to-all-start.1 = ((bf16[128,8,128]{2,1,0:T(8,128)(2,1)}), bf16[128,8,128]{2,1,0:T(8,128)(2,1)S(1)}, u32[]{:S(2)}, u32[]{:S(2)}) async-start(bf16[128,8,128]{2,1,0:T(8,128)(2,1)} %sort.1), calls=%async_computation.1 | async-start | bytes 524288 | tf_op jit(solution)/shard_map/all_to_all | solution.py:557
  57.5 6.6 %copy-start.20 = (s32[128]{0:T(128)S(1)}, s32[128]{0:T(128)}, u32[]{:S(2)}) copy-start(s32[128]{0:T(128)} %param.43) | copy-start | bytes 1540
  57.5 10.5 %copy-start.4 = (bf16[768,256]{1,0:T(8,128)(2,1)S(1)}, bf16[768,256]{1,0:T(8,128)(2,1)}, u32[]{:S(2)}) copy-start(bf16[768,256]{1,0:T(8,128)(2,1)} %dilated_weight_ref.1) | copy-start | bytes 1179652
  57.6 10.5 %copy-start.5 = (bf16[768,256]{1,0:T(8,128)(2,1)S(1)}, bf16[768,256]{1,0:T(8,128)(2,1)}, u32[]{:S(2)}) copy-start(bf16[768,256]{1,0:T(8,128)(2,1)} %second_weight_ref.1) | copy-start | bytes 1179652
  57.6 10.5 %copy-start.12 = (f32[512]{0:T(512)S(1)}, f32[512]{0:T(512)}, u32[]{:S(2)}) copy-start(f32[512]{0:T(512)} %param.32) | copy-start | bytes 6148
  57.6 10.4 %copy-start.13 = (f32[256]{0:T(256)S(1)}, f32[256]{0:T(256)}, u32[]{:S(2)}) copy-start(f32[256]{0:T(256)} %param.34) | copy-start | bytes 3076
  57.6 10.4 %copy-start.14 = (f32[256]{0:T(256)S(1)}, f32[256]{0:T(256)}, u32[]{:S(2)}) copy-start(f32[256]{0:T(256)} %param.35) | copy-start | bytes 3076
  57.6 10.4 %copy-start.15 = (f32[256]{0:T(256)S(1)}, f32[256]{0:T(256)}, u32[]{:S(2)}) copy-start(f32[256]{0:T(256)} %param.37) | copy-start | bytes 3076
  57.6 10.4 %copy-start.16 = (f32[256]{0:T(256)S(1)}, f32[256]{0:T(256)}, u32[]{:S(2)}) copy-start(f32[256]{0:T(256)} %param.38) | copy-start | bytes 3076
  57.6 10.4 %copy-start.17 = (f32[256]{0:T(256)S(1)}, f32[256]{0:T(256)}, u32[]{:S(2)}) copy-start(f32[256]{0:T(256)} %param.40) | copy-start | bytes 3076
  68.1 2.2 %copy-start = (bf16[16,256,512]{1,2,0:T(8,128)(2,1)S(1)}, bf16[16,256,512]{1,2,0:T(8,128)(2,1)}, u32[]{:S(2)}) copy-start(bf16[16,256,512]{1,2,0:T(8,128)(2,1)} %copy.25) | copy-start | bytes 12582916

commit v4 on v3

--- a/solution.py
+++ b/solution.py
@@ -34,13 +34,19 @@
     return half + half * jnp.tanh(slope)
 
 
+def nt_dot(left, right):
+    return lax.dot_general(
+        left, right, (((1,), (1,)), ((), ())), preferred_element_type=jnp.float32
+    )
+
+
 def velocity_kernel(
     side_ref,
-    hidden_ref,
+    hidden_hbm,
     modulation_ref,
-    in_weight_ref,
+    in_weight_hbm,
     in_bias_ref,
-    out_weight_ref,
+    out_weight_hbm,
     out_bias_ref,
     mel_weight_ref,
     mel_bias_ref,
@@ -50,67 +56,130 @@
     own_ref,
     sent_ref,
     base_ref,
+    hidden_ref,
+    in_weight_ref,
+    out_weight_ref,
+    mel_pad_ref,
+    bias_pad_ref,
     tall_ref,
     normed_ref,
-    total_ref,
+    active_ref,
+    speed_ref,
+    back_ref,
+    hidden_sem,
+    in_sem,
+    out_sem,
     *,
     block,
+    tail,
+    in_chunk,
 ):
-    frames = hidden_ref.shape[1]
-    half_rows = own_ref.shape[0]
-    norm_block = 128
+    frames, width = hidden_ref.shape
+    units = in_weight_ref.shape[1]
+    half_rows = frames // 2
+    mel_bins = noisy_ref.shape[0]
+    chips = own_ref.shape[0] // GROUP
     f32, bf16 = jnp.float32, jnp.bfloat16
-    step = pl.program_id(0)
-
-    @pl.when(step == 0)
+    hidden_copies = []
+    for i in range(frames // block):
+        rows = pl.ds(i * block, block)
+        copy = pltpu.make_async_copy(
+            hidden_hbm.at[0, rows, :], hidden_ref.at[rows, :], hidden_sem.at[i]
+        )
+        copy.start()
+        hidden_copies.append(copy)
+    in_copies = []
+    for i in range(units // in_chunk):
+        columns = pl.ds(i * in_chunk, in_chunk)
+        copy = pltpu.make_async_copy(
+            in_weight_hbm.at[:, columns], in_weight_ref.at[:, columns], in_sem.at[i]
+        )
+        copy.start()
+        in_copies.append(copy)
+    out_copy = pltpu.make_async_copy(out_weight_hbm, out_weight_ref, out_sem)
+    out_copy.start()
+
+    def spaced_store(ref, first, values):
+        for i in range(values.shape[0] // chips):
+            ref[pl.ds(first + i, chips, stride=GROUP), :] = values[i * chips : (i + 1) * chips, :]
+
+    used = half_rows // chips
+    blank = jnp.zeros(((GROUP - used) * chips, LANES), f32)
+    half = pl.ds(pl.multiple_of(side_ref[0] * half_rows, half_rows), half_rows)
+    tall_ref[...] = jnp.zeros(tall_ref.shape, f32)
+    tall_ref[:mel_bins, :] = noisy_ref[:, half]
+    for i in range(half_rows // LANES):
+        row = pl.ds(side_ref[0] * (half_rows // LANES) + i, 1)
+        columns = slice(i * LANES, (i + 1) * LANES)
+        tall_ref[mel_bins : mel_bins + 1, columns] = holder_ref[row, :].astype(f32)
+        tall_ref[mel_bins + 1 : mel_bins + 2, columns] = jnp.where(
+            position_ref[row, :] == 0, 1.0, 0.0
+        )
+    spaced_store(base_ref, 0, tall_ref[...].T)
+    spaced_store(base_ref, used, blank)
+    spaced_store(speed_ref.at[0], used, blank)
+    spaced_store(speed_ref.at[1], used, blank)
+    mel_pad_ref[...] = jnp.zeros(mel_pad_ref.shape, bf16)
+    mel_pad_ref[:mel_bins, :] = mel_weight_ref[...]
+    bias_pad_ref[...] = jnp.zeros(bias_pad_ref.shape, f32)
+    bias_pad_ref[:, :mel_bins] = mel_bias_ref[...]
+
+    scale = 1.0 + modulation_ref[1:2, :]
+    for i in range(frames // block):
+        hidden_copies[i].wait()
+        for low in range(i * block, (i + 1) * block, 64):
+            rows = slice(low, low + 64)
+            normed = layer_norm(hidden_ref[rows, :].astype(f32)) * scale + modulation_ref[0:1, :]
+            normed_ref[rows, :] = normed.astype(bf16)
+
+    for j in range(units // in_chunk):
+        columns = slice(j * in_chunk, (j + 1) * in_chunk)
+        in_copies[j].wait()
+        for i in range(frames // block):
+            rows = slice(i * block, (i + 1) * block)
+            inner = jnp.dot(
+                normed_ref[rows, :], in_weight_ref[:, columns], preferred_element_type=f32
+            )
+            active_ref[rows, columns] = gelu_tanh(inner + in_bias_ref[:, columns]).astype(bf16)
+
+    out_copy.wait()
+    out_scale = 1.0 + modulation_ref[4:5, :]
+
+    def finish(i):
+        for low in range(i * tail, (i + 1) * tail, 64):
+            rows = slice(low, low + 64)
+            back = back_ref[i % 2, low - i * tail : low - i * tail + 64, :] + out_bias_ref[...]
+            block_out = hidden_ref[rows, :].astype(f32) + modulation_ref[2:3, :] * back
+            final = layer_norm(block_out) * out_scale + modulation_ref[3:4, :]
+            normed_ref[rows, :] = final.astype(bf16)
+
+    def emit(i):
+        first = i * tail
+        speed = nt_dot(normed_ref[first : first + tail, :], mel_pad_ref[...]) + bias_pad_ref[...]
+        part = first // half_rows
+        spaced_store(speed_ref.at[part], (first - part * half_rows) // chips, speed)
+
+    count = frames // tail
+    for i in range(count + 1):
+        if i < count:
+            back_ref[i % 2] = jnp.dot(
+                active_ref[i * tail : (i + 1) * tail, :],
+                out_weight_ref[...],
+                preferred_element_type=f32,
+            )
+        if i > 0:
+            finish(i - 1)
+            emit(i - 1)
+
+    @pl.when(side_ref[0] == 0)
     def _():
-        scale = 1.0 + modulation_ref[1:2, :]
-        for low in range(0, frames, norm_block):
-            rows = slice(low, low + norm_block)
-            normed = layer_norm(hidden_ref[0, rows, :].astype(f32)) * scale + modulation_ref[0:1, :]
-            normed_ref[rows, :] = normed.astype(bf16)
-            total_ref[rows, :] = jnp.broadcast_to(
-                out_bias_ref[...], (norm_block, out_bias_ref.shape[1])
-            )
-
-        mel_bins = noisy_ref.shape[0]
-        half = pl.ds(pl.multiple_of(side_ref[0] * half_rows, half_rows), half_rows)
-        tall_ref[...] = jnp.zeros(tall_ref.shape, f32)
-        tall_ref[:mel_bins, :] = noisy_ref[:, half]
-        tall_ref[mel_bins : mel_bins + 1, :] = holder_ref[:, half].astype(f32)
-        first_flag = jnp.where(position_ref[:, half] == 0, 1.0, 0.0)
-        tall_ref[mel_bins + 1 : mel_bins + 2, :] = first_flag
-        base_ref[...] = tall_ref[...].T
-
-    for low in range(0, frames, block):
-        rows = slice(low, low + block)
-        inner = jnp.dot(normed_ref[rows, :], in_weight_ref[...], preferred_element_type=f32)
-        active = gelu_tanh(inner + in_bias_ref[...]).astype(bf16)
-        total_ref[rows, :] += jnp.dot(active, out_weight_ref[...], preferred_element_type=f32)
-
-    @pl.when(step == pl.num_programs(0) - 1)
+        own_ref[...] = speed_ref[0]
+        sent_ref[...] = speed_ref[1]
+
+    @pl.when(side_ref[0] != 0)
     def _():
-        scale = 1.0 + modulation_ref[4:5, :]
-        for low in range(0, frames, norm_block):
-            rows = slice(low, low + norm_block)
-            block_out = hidden_ref[0, rows, :].astype(f32) + modulation_ref[2:3, :] * total_ref[rows, :]
-            normed_ref[rows, :] = (
-                layer_norm(block_out) * scale + modulation_ref[3:4, :]
-            ).astype(bf16)
-        for part in range(2):
-            rows = slice(part * half_rows, (part + 1) * half_rows)
-            speed = (
-                jnp.dot(normed_ref[rows, :], mel_weight_ref[...], preferred_element_type=f32)
-                + mel_bias_ref[...]
-            )
-
-            @pl.when(side_ref[0] == part)
-            def _(speed=speed):
-                own_ref[...] = speed
-
-            @pl.when(side_ref[0] != part)
-            def _(speed=speed):
-                sent_ref[...] = speed
+        own_ref[...] = speed_ref[1]
+        sent_ref[...] = speed_ref[0]
 
 
 def velocity_halves(
@@ -126,40 +195,38 @@
     noisy_mel_state,
     frame_holder,
     frame_position,
-    block=768,
-    chunk=1024,
+    chips,
+    block=384,
+    tail=384,
+    in_chunk=1024,
 ):
     frames, width = hidden.shape[1:]
-    hidden_units = feedforward_in_weight.shape[1]
-    mel_bins = mel_velocity_weight.shape[1]
-    half = jax.ShapeDtypeStruct((frames // 2, LANES), jnp.float32)
-    whole = pl.Buffered(1)
-    fixed = lambda i: (0, 0)
+    units = feedforward_in_weight.shape[1]
+    f32, bf16 = jnp.float32, jnp.bfloat16
+    spaced = jax.ShapeDtypeStruct((chips * GROUP, LANES), f32)
+    vmem = pl.BlockSpec(memory_space=pltpu.VMEM)
+    hbm = pl.BlockSpec(memory_space=pl.ANY)
     return pl.pallas_call(
-        functools.partial(velocity_kernel, block=block),
-        out_shape=(half, half, half),
-        grid=(hidden_units // chunk,),
-        in_specs=[
-            pl.BlockSpec(memory_space=pltpu.SMEM),
-            pl.BlockSpec((1, frames, width), lambda i: (0, 0, 0), pipeline_mode=whole),
-            pl.BlockSpec(modulation.shape, fixed, pipeline_mode=whole),
-            pl.BlockSpec((width, chunk), lambda i: (0, i)),
-            pl.BlockSpec((1, chunk), lambda i: (0, i)),
-            pl.BlockSpec((chunk, width), lambda i: (i, 0)),
-            pl.BlockSpec((1, width), fixed, pipeline_mode=whole),
-            pl.BlockSpec((width, LANES), fixed, pipeline_mode=whole),
-            pl.BlockSpec((1, LANES), fixed, pipeline_mode=whole),
-            pl.BlockSpec(noisy_mel_state.shape, fixed, pipeline_mode=whole),
-            pl.BlockSpec((1, frames), fixed, pipeline_mode=whole),
-            pl.BlockSpec((1, frames), fixed, pipeline_mode=whole),
+        functools.partial(velocity_kernel, block=block, tail=tail, in_chunk=in_chunk),
+        out_shape=(spaced,) * 3,
+        in_specs=[pl.BlockSpec(memory_space=pltpu.SMEM), hbm, vmem, hbm, vmem, hbm] + [vmem] * 6,
+        out_specs=(vmem,) * 3,
+        scratch_shapes=[
+            pltpu.VMEM((frames, width), bf16),
+            pltpu.VMEM((width, units), bf16),
+            pltpu.VMEM((units, width), bf16),
+            pltpu.VMEM((LANES, width), bf16),
+            pltpu.VMEM((1, LANES), f32),
+            pltpu.VMEM((LANES, frames // 2), f32),
+            pltpu.VMEM((frames, width), bf16),
+            pltpu.VMEM((frames, units), bf16),
+            pltpu.VMEM((2, chips * GROUP, LANES), f32),
+            pltpu.VMEM((2, tail, width), f32),
+            pltpu.SemaphoreType.DMA((frames // block,)),
+            pltpu.SemaphoreType.DMA((units // in_chunk,)),
+            pltpu.SemaphoreType.DMA(()),
         ],
-        out_specs=(pl.BlockSpec(half.shape, fixed),) * 3,
-        scratch_shapes=[
-            pltpu.VMEM((LANES, frames // 2), jnp.float32),
-            pltpu.VMEM((frames, width), jnp.bfloat16),
-            pltpu.VMEM((frames, width), jnp.float32),
-        ],
-        compiler_params=pltpu.CompilerParams(vmem_limit_bytes=40 * 1024 * 1024),
+        compiler_params=pltpu.CompilerParams(vmem_limit_bytes=60 * 1024 * 1024),
         name="velocity",
     )(
         side,
@@ -169,45 +236,12 @@
         feedforward_in_bias[None],
         feedforward_out_weight,
         feedforward_out_bias[None],
-        jnp.pad(mel_velocity_weight, ((0, 0), (0, LANES - mel_bins))),
-        jnp.pad(mel_velocity_bias, (0, LANES - mel_bins))[None],
+        mel_velocity_weight.T,
+        mel_velocity_bias[None],
         noisy_mel_state,
-        frame_holder[None],
-        frame_position[None],
+        frame_holder.reshape(-1, LANES),
+        frame_position.reshape(-1, LANES),
     )
-
-
-def combine_kernel(side_ref, own_ref, peer_ref, base_ref, packed_ref, spaced_ref):
-    chips = packed_ref.shape[0]
-    step_size = math.cos(0.5 * math.pi * (NFE - 1) / NFE)
-    first = side_ref[0] == 0
-    conditional = jnp.where(first, own_ref[...], peer_ref[...])
-    unconditional = jnp.where(first, peer_ref[...], own_ref[...])
-    guided = (1.0 + GUIDE) * conditional - GUIDE * unconditional
-    refined = base_ref[...] + step_size * guided
-    for turn in range(GROUP):
-        low = turn * chips
-        if low < refined.shape[0]:
-            spaced_ref[pl.ds(turn, chips, stride=GROUP), :] = refined[low : low + chips, :]
-        else:
-            spaced_ref[pl.ds(turn, chips, stride=GROUP), :] = jnp.zeros((chips, LANES), jnp.float32)
-    packed_ref[...] = spaced_ref[...].reshape(packed_ref.shape).astype(packed_ref.dtype)
-
-
-def sort_kernel(spread_ref, slots_ref, spaced_ref, *, mel_bins):
-    owners = slots_ref.shape[0]
-    rows = spread_ref[...].reshape(-1, LANES)
-    count = rows.shape[0]
-    column = jnp.broadcast_to(rows[:, mel_bins : mel_bins + 1].astype(jnp.float32), (count, owners))
-    owner_of = column.T
-    owner = lax.broadcasted_iota(jnp.int32, (owners, count), 0).astype(jnp.float32)
-    turn_of = lax.rem(lax.broadcasted_iota(jnp.int32, (1, count), 1), GROUP)
-    for turn in range(GROUP):
-        pick = ((owner_of == owner) & (turn_of == turn)).astype(jnp.bfloat16)
-        spaced_ref[pl.ds(turn, owners, stride=GROUP), :] = jnp.dot(
-            pick, rows, preferred_element_type=jnp.float32
-        )
-    slots_ref[...] = spaced_ref[...].reshape(slots_ref.shape).astype(slots_ref.dtype)
 
 
 SIN_TERMS = (
@@ -229,12 +263,6 @@
     poly = poly * square + SIN_TERMS[0]
     sine = poly * part
     return signal + sine * sine * inverse
-
-
-def nt_dot(left, right):
-    return lax.dot_general(
-        left, right, (((1,), (1,)), ((), ())), preferred_element_type=jnp.float32
-    )
 
 
 def vocoder_kernel(
@@ -352,13 +380,12 @@
 
         def up_product(r, rows):
             side = jnp.where(r < UP // 2, 0, 2)
-            return jnp.dot(
+            return nt_dot(
                 jnp.concatenate([pre_ref[1, rows, :], pre_ref[side, rows, :]], axis=1),
                 jnp.concatenate(
                     [up_weight_ref[r + UP // 2], up_weight_ref[lax.rem(r + UP // 2 + UP, KT)]],
-                    axis=0,
+                    axis=1,
                 ),
-                preferred_element_type=f32,
             )
 
         def up_finish(r, low, up):
@@ -455,7 +482,7 @@
         arrived,
         taps_weight,
         input_conv_bias[None],
-        transposed_conv_weight.reshape(KT, channels, wide).transpose(0, 2, 1),
+        transposed_conv_weight.reshape(KT, channels, wide),
         transposed_conv_bias[None],
         snake_freq_first[None],
         dilated_conv_weight,
@@ -486,12 +513,12 @@
             pltpu.VMEM((UP + 6, frames, channels), bf16),
             pltpu.VMEM((UP + 2, frames, channels), bf16),
             pltpu.VMEM((UP, frames, channels), bf16),
-            pltpu.VMEM((KT, wide, channels), bf16),
+            pltpu.VMEM((KT, channels, wide), bf16),
             pltpu.SemaphoreType.DMA(()),
             pltpu.VMEM((frames, channels), f32),
             pltpu.VMEM((frames, channels), f32),
         ],
-        compiler_params=pltpu.CompilerParams(vmem_limit_bytes=48 * 1024 * 1024),
+        compiler_params=pltpu.CompilerParams(vmem_limit_bytes=60 * 1024 * 1024),
         name="vocoder",
     )(length, *operands)
 
@@ -520,12 +547,13 @@
     frame_position,
     holder_utterance_length,
 ):
+    step_size = math.cos(0.5 * math.pi * (NFE - 1) / NFE)
     chips = lax.axis_size("seq")
     owners = lax.axis_size("branch") * chips
     mel_bins, frames = noisy_mel_state.shape
-    side = lax.axis_index("branch").astype(jnp.int32)[None]
+    branch_side = lax.axis_index("branch").astype(jnp.int32)
     own_half, sent_half, base = velocity_halves(
-        side,
+        branch_side[None],
         hidden,
         modulation,
         feedforward_in_weight,
@@ -537,25 +565,26 @@
         noisy_mel_state,
         frame_holder,
         frame_position,
+        chips,
     )
     peer_half = lax.ppermute(sent_half, "branch", [(0, 1), (1, 0)])
-    packed = pl.pallas_call(
-        combine_kernel,
-        out_shape=jax.ShapeDtypeStruct((chips, GROUP, LANES), jnp.bfloat16),
-        in_specs=[pl.BlockSpec(memory_space=pltpu.SMEM)]
-        + [pl.BlockSpec(memory_space=pltpu.VMEM)] * 3,
-        scratch_shapes=[pltpu.VMEM((chips * GROUP, LANES), jnp.float32)],
-        name="combine",
-    )(side, own_half, peer_half, base)
-    spread = lax.all_to_all(packed, "seq", 0, 0, tiled=True)
-    slots = pl.pallas_call(
-        functools.partial(sort_kernel, mel_bins=mel_bins),
-        out_shape=jax.ShapeDtypeStruct((owners, GROUP, LANES), jnp.bfloat16),
-        scratch_shapes=[pltpu.VMEM((owners * GROUP, LANES), jnp.float32)],
-        name="sort",
-    )(spread)
-    arrived = lax.all_to_all(slots, ("branch", "seq"), 0, 0, tiled=True)
-    arrived = arrived.reshape(owners * GROUP, LANES)
+    conditional = jnp.where(branch_side == 0, own_half, peer_half)
+    unconditional = jnp.where(branch_side == 0, peer_half, own_half)
+    guided = (1.0 + GUIDE) * conditional - GUIDE * unconditional
+    packed = (base + step_size * guided).astype(jnp.bfloat16)
+    spread = lax.all_to_all(packed.reshape(chips, GROUP, LANES), "seq", 0, 0, tiled=True)
+    rows = spread.reshape(chips * GROUP, LANES)
+    owner_of = rows[:, mel_bins].astype(jnp.int32)
+    slot_of = owner_of * GROUP + jnp.arange(chips * GROUP, dtype=jnp.int32) % GROUP
+    onehot = (slot_of[:, None] == jnp.arange(owners * GROUP, dtype=jnp.int32)[None, :]).astype(
+        jnp.bfloat16
+    )
+    slots = lax.dot_general(
+        onehot, rows, (((0,), (0,)), ((), ())), preferred_element_type=jnp.float32
+    ).astype(jnp.bfloat16)
+    arrived = lax.all_to_all(
+        slots.reshape(owners, GROUP, LANES), ("branch", "seq"), 0, 0, tiled=True
+    ).reshape(owners * GROUP, LANES)
     self_owner = lax.axis_index(("branch", "seq"))
     length = lax.dynamic_slice_in_dim(holder_utterance_length, self_owner, 1, 0)
     return vocoder(

time: 94.8 us -> 81.3 us (0.86)
  local copies, waits for them, and re-layouts: 23.6 us -> 2.51 us
  waiting for transfers between devices: 4.35 us -> 10.3 us
  matrix products: 0 us -> 1.53 us
  other arithmetic: 0 us -> 1.33 us
    unnamed x43 -> x6, local copies, waits for them, and re-layouts: 14.3 us -> 0.73 us
    reshape x1 -> x0, local copies, waits for them, and re-layouts: 6.44 us -> none  [vocoder(): transposed_conv_weight.reshape(KT, channels, wide).transpose(0, 2, 1)]
    all_to_all x1, waiting for transfers between devices: 3.28 us -> 8.88 us  [local(): lax.all_to_all(slots.reshape(owners, GROUP, LANES), ('branch', 'seq'), 0,...]
    broadcast_in_dim x3 -> x0, local copies, waits for them, and re-layouts: 2.04 us -> none  [the longest x1 0.69 us: velocity_halves(): frame_position[None]]
    dot_general x0 -> x1, matrix products: none -> 1.53 us  [local(): lax.dot_general(onehot, rows, (((0,), (0,)), ((), ())), preferred_element...]
    pallas_call x3 -> x1, Pallas kernels: 15.3 us -> 13.8 us  [velocity_halves(): pl.pallas_call(functools.partial(velocity_kernel, block=block, tail=tail,...]
    pallas_call x1, Pallas kernels: 23.5 us -> 24.7 us  [vocoder(): pl.pallas_call(functools.partial(vocoder_kernel, mel_bins=mel_bins, block...]
    reshape x0 -> x1, other arithmetic: none -> 1.1 us  [local(): packed.reshape(chips, GROUP, LANES)]
  transfers between devices with their start and end apart: 2 -> 2, of which waited for: 2 -> 2; matrix products, arithmetic and copies ran while one was open for 8% -> 2% of each run, Pallas kernels for 0% -> 0%
where the time goes in v4:
time: 81.3 us; the launch traced here: 81 us
  Pallas kernels  38.6 us (47%)
  blocking collectives  19.7 us (24%)
  waiting for transfers between devices  10.3 us (13%)
  starting transfers between devices  6.92 us (9%)
  local copies, waits for them, and re-layouts  2.51 us (3%)
  matrix products  1.53 us (2%)
  other arithmetic  1.33 us (2%)
    pallas_call x1, Pallas kernels, vocoder(): pl.pallas_call(functools.partial(vocoder_kernel, mel_bins=mel_bins, block...  24.7 us
    all_to_all x1, blocking collectives, local(): lax.all_to_all(packed.reshape(chips, GROUP, LANES), 'seq', 0, 0, tiled=True)  19.7 us
    pallas_call x1, Pallas kernels, velocity_halves(): pl.pallas_call(functools.partial(velocity_kernel, block=block, tail=tail,...  13.8 us
    all_to_all x1, waiting for transfers between devices, local(): lax.all_to_all(slots.reshape(owners, GROUP, LANES), ('branch', 'seq'), 0,...  8.88 us
    all_to_all x1, starting transfers between devices, local(): lax.all_to_all(slots.reshape(owners, GROUP, LANES), ('branch', 'seq'), 0,...  5.42 us
  transfers between devices with their start and end apart: 2, of which 2 were waited for; matrix products, arithmetic and copies ran while one was open for 2% of the time, Pallas kernels for 0%

profile of v4, /device:TPU:1, one launch (start us, length us, event | category | flops | bytes accessed | tf_op | source)
XLA Modules:
  0.0 81.0 jit_solution(16891312486285305521)
XLA Ops:
  0.0 13.8 %velocity.1 = (f32[512,128]{1,0:T(8,128)}, f32[512,128]{1,0:T(8,128)}, f32[512,128]{1,0:T(8,128)}) custom-call(s32[1]{0:T(128)} %bitcast.side_ref, bf16[1,768,1024]{2,1,0:T(8,128)(2,1)} %hidden_hbm.1, f32[5,1024]{1,0:T(8,128)} %modulation_ref.1, bf16[1024,2048]{1,0:T(8,128)(2,1)} %in_weight_hbm.1, f32[1,2048]{1,0:T(1,128)} %bitcast.28, ...), custom_call_target="tpu_custom_call" | custom-call | tf_op jit(solution)/shard_map/velocity/pallas_call | solution.py:209
  13.8 0.0 copy-start.1
  13.8 0.0 copy-start.2
  13.9 1.5 %collective-permute-start = (f32[512,128]{1,0:T(8,128)}, f32[512,128]{1,0:T(8,128)S(1)}, u32[]{:S(2)}, u32[]{:S(2)}) collective-permute-start(f32[512,128]{1,0:T(8,128)} %get-tuple-element.10), channel_id=1, source_target_pairs={{0,64},{64,0},{1,65},{65,1},{2,66},{66,2},{3,67},{67,3},{4,68},{68... | collective-permute-start | bytes 786440 | tf_op jit(solution)/shard_map/ppermute | solution.py:570
  15.4 1.4 %collective-permute-done = f32[512,128]{1,0:T(8,128)S(1)} collective-permute-done((f32[512,128]{1,0:T(8,128)}, f32[512,128]{1,0:T(8,128)S(1)}, u32[]{:S(2)}, u32[]{:S(2)}) %collective-permute-start) | collective-permute-done | bytes 262176 | tf_op jit(solution)/shard_map/ppermute | solution.py:570
  16.7 1.1 %fusion.9 = bf16[64,8,128]{2,1,0:T(8,128)(2,1)S(1)} fusion(f32[512,128]{1,0:T(8,128)} %get-tuple-element.8, f32[512,128]{1,0:T(8,128)S(1)} %collective-permute-done, f32[512,128]{1,0:T(8,128)} %get-tuple-element.9, pred[]{:T(512)S(6)} %eq.21), kind=kLoop, calls=%fused_computation.13 | loop fusion | flops 524288 | bytes 917505 | tf_op jit(solution)/shard_map/reshape | solution.py:575
  17.8 19.7 %all_to_all.10 = bf16[64,8,128]{2,1,0:T(8,128)(2,1)S(1)} all-to-all(bf16[64,8,128]{2,1,0:T(8,128)(2,1)S(1)} %fusion.9), channel_id=1, replica_groups=mesh['branch'=2,'seq'=64] {'seq'}, dimensions={0} | all-to-all | bytes 262144 | tf_op jit(solution)/shard_map/all_to_all | solution.py:575
  37.5 0.2 fusion.5
  37.7 1.5 %fusion.2 = bf16[128,8,128]{2,1,0:T(8,128)(2,1)} fusion(s32[512]{0:T(512)S(1)} %fusion.5, bf16[64,8,128]{2,1,0:T(8,128)(2,1)S(1)} %all_to_all.10), kind=kOutput, calls=%fused_computation.3 | convolution fusion | flops 134873088 | bytes 395264 | tf_op jit(solution)/shard_map/dot_general | solution.py:582
  39.3 5.4 %all-to-all-start.1 = ((bf16[128,8,128]{2,1,0:T(8,128)(2,1)}), bf16[128,8,128]{2,1,0:T(8,128)(2,1)S(1)}, u32[]{:S(2)}, u32[]{:S(2)}) async-start(bf16[128,8,128]{2,1,0:T(8,128)(2,1)} %fusion.2), calls=%async_computation.1 | async-start | bytes 524288 | tf_op jit(solution)/shard_map/all_to_all | solution.py:585
  44.7 0.0 copy-done.1
  44.7 0.1 reshape.55
  44.8 0.0 copy-done.2
  44.8 0.7 dynamic_slice.3.length_ref
  45.5 1.0 %pad.4 = bf16[7,128,512]{2,1,0:T(8,128)(2,1)} pad(bf16[7,100,512]{2,1,0:T(8,128)(2,1)S(1)} %reshape.55, bf16[]{:T(256)} %constant.38.clone.1), padding=0_0x0_28x0_0 | pad | bytes 1634306 | tf_op jit(solution)/shard_map/jit(_pad)/pad | solution.py:478
  46.5 8.9 %all-to-all-done.1 = bf16[128,8,128]{2,1,0:T(8,128)(2,1)S(1)} async-done(((bf16[128,8,128]{2,1,0:T(8,128)(2,1)}), bf16[128,8,128]{2,1,0:T(8,128)(2,1)S(1)}, u32[]{:S(2)}, u32[]{:S(2)}) %all-to-all-start.1) | async-done | bytes 262176 | tf_op jit(solution)/shard_map/all_to_all | solution.py:585
  55.4 0.0 copy-start
  55.4 0.7 copy-done
  56.1 24.7 %vocoder.1 = bf16[1,256,6144]{2,1,0:T(8,128)(2,1)} custom-call(s32[1]{0:T(128)} %dynamic_slice.3.length_ref, bf16[1024,128]{1,0:T(8,128)(2,1)} %bitcast.25, bf16[896,512]{1,0:T(8,128)(2,1)} %bitcast.24, f32[1,512]{1,0:T(1,128)} %bitcast.32, bf16[16,256,512]{2,1,0:T(8,128)(2,1)} %bitcast.23, f32[1,256]{1,0:T(1,128)} %bitcast.33, f32[1,256]{1,0:T(1,128)} %bitcast.34, ...), custom_call_target="tpu_custom_call" | custom-call | tf_op jit(solution)/shard_map/vocoder/pallas_call | solution.py:494
Async XLA Ops:
  13.8 30.9 %copy-start.1 = (bf16[700,512]{1,0:T(8,128)(2,1)S(1)}, bf16[700,512]{1,0:T(8,128)(2,1)}, u32[]{:S(2)}) copy-start(bf16[700,512]{1,0:T(8,128)(2,1)} %param.31) | copy-start | bytes 2150404
  13.8 31.0 %copy-start.2 = (s32[128]{0:T(128)S(1)}, s32[128]{0:T(128)}, u32[]{:S(2)}) copy-start(s32[128]{0:T(128)} %param.43) | copy-start | bytes 1540
  13.9 2.9 %collective-permute-start = (f32[512,128]{1,0:T(8,128)}, f32[512,128]{1,0:T(8,128)S(1)}, u32[]{:S(2)}, u32[]{:S(2)}) collective-permute-start(f32[512,128]{1,0:T(8,128)} %get-tuple-element.10), channel_id=1, source_target_pairs={{0,64},{64,0},{1,65},{65,1},{2,66},{66,2},{3,67},{67,3},{4,68},{68... | collective-permute-start | bytes 786440 | tf_op jit(solution)/shard_map/ppermute | solution.py:570
  39.3 16.1 %all-to-all-start.1 = ((bf16[128,8,128]{2,1,0:T(8,128)(2,1)}), bf16[128,8,128]{2,1,0:T(8,128)(2,1)S(1)}, u32[]{:S(2)}, u32[]{:S(2)}) async-start(bf16[128,8,128]{2,1,0:T(8,128)(2,1)} %fusion.2), calls=%async_computation.1 | async-start | bytes 524288 | tf_op jit(solution)/shard_map/all_to_all | solution.py:585
  55.4 0.7 copy-start

commit v5 on v4

--- a/solution.py
+++ b/solution.py
@@ -278,7 +278,7 @@
     freq_second_ref,
     second_weight_ref,
     second_bias_ref,
-    wave_ref,
+    wave_hbm,
     mel_ref,
     taps_ref,
     shift_wide_ref,
@@ -292,166 +292,177 @@
     up_sem,
     even_ref,
     odd_ref,
+    wave_ref,
+    wave_sem,
     *,
     mel_bins,
     block,
 ):
     frames = up_ref.shape[1]
-    piece_frames = out_ref.shape[1] // pl.num_programs(0)
     part_rows = arrived_ref.shape[0] // 2
     blocks = frames // block
     halo = 8
     f32, bf16 = jnp.float32, jnp.bfloat16
-    step = pl.program_id(0)
     length = length_ref[0]
 
     def keep_rows(first, count):
         row = lax.broadcasted_iota(jnp.int32, (count, 1), 0) + first
         return row < length
 
-    @pl.when(step == 0)
-    def _():
-        up_copy = pltpu.make_async_copy(up_weight_hbm, up_weight_ref, up_sem)
-        up_copy.start()
-        arrived = arrived_ref[...]
-
-        def shard_row(shape, axis):
-            i = lax.broadcasted_iota(jnp.int32, shape, axis)
-            side = (i >= part_rows).astype(jnp.int32)
-            inner = i - side * part_rows
-            turn = lax.rem(inner, GROUP)
-            row = side * (frames // 2) + turn * (part_rows // GROUP) + inner // GROUP
-            return jnp.where(turn < frames * GROUP // (2 * part_rows), row, -4 * frames)
-
-        lane = lax.broadcasted_iota(jnp.int32, arrived.shape, 1)
-        flagged = jnp.where(lane == mel_bins + 1, arrived.astype(f32), 0.0)
-        start = jnp.sum(
-            jnp.where(flagged > 0.5, shard_row(arrived.shape, 0).astype(f32), 0.0), keepdims=True
-        ).astype(jnp.int32)
-        mel_ref[...] = jnp.zeros(mel_ref.shape, f32)
-        turned = shard_row((1, arrived.shape[0]), 1) - start
-        for i in range(frames // 128):
-            ahead = turned - i * 128 - lax.broadcasted_iota(jnp.int32, (128, 1), 0)
-            pick = ((ahead == 0) | (ahead == -frames)).astype(bf16)
-            mel_ref[halo + i * 128 : halo + (i + 1) * 128, :] = jnp.dot(
-                pick, arrived, preferred_element_type=f32
-            )
-        for k in range(KPRE):
-            low = halo + k - KPRE // 2
-            taps_ref[:, k * LANES : (k + 1) * LANES] = mel_ref[low : low + frames, :].astype(bf16)
-        shift_wide_ref[...] = jnp.zeros(shift_wide_ref.shape, f32)
+    up_copy = pltpu.make_async_copy(up_weight_hbm, up_weight_ref, up_sem)
+    up_copy.start()
+    arrived = arrived_ref[...]
+
+    def shard_row(shape, axis):
+        i = lax.broadcasted_iota(jnp.int32, shape, axis)
+        side = (i >= part_rows).astype(jnp.int32)
+        inner = i - side * part_rows
+        turn = lax.rem(inner, GROUP)
+        row = side * (frames // 2) + turn * (part_rows // GROUP) + inner // GROUP
+        return jnp.where(turn < frames * GROUP // (2 * part_rows), row, -4 * frames)
+
+    lane = lax.broadcasted_iota(jnp.int32, arrived.shape, 1)
+    flagged = jnp.where(lane == mel_bins + 1, arrived.astype(f32), 0.0)
+    start = jnp.sum(
+        jnp.where(flagged > 0.5, shard_row(arrived.shape, 0).astype(f32), 0.0), keepdims=True
+    ).astype(jnp.int32)
+    mel_ref[...] = jnp.zeros(mel_ref.shape, f32)
+    turned = shard_row((1, arrived.shape[0]), 1) - start
+    for i in range(frames // 128):
+        ahead = turned - i * 128 - lax.broadcasted_iota(jnp.int32, (128, 1), 0)
+        pick = ((ahead == 0) | (ahead == -frames)).astype(bf16)
+        mel_ref[halo + i * 128 : halo + (i + 1) * 128, :] = jnp.dot(
+            pick, arrived, preferred_element_type=f32
+        )
+    for k in range(KPRE):
+        low = halo + k - KPRE // 2
+        taps_ref[:, k * LANES : (k + 1) * LANES] = mel_ref[low : low + frames, :].astype(bf16)
+    shift_wide_ref[...] = jnp.zeros(shift_wide_ref.shape, f32)
+    for i in range(blocks):
+        rows = slice(i * block, (i + 1) * block)
+        pre = jnp.dot(taps_ref[rows, :], input_weight_ref[...], preferred_element_type=f32)
+        pre = jnp.where(keep_rows(i * block, block), pre + input_bias_ref[...], 0.0)
+        shift_wide_ref[halo + i * block : halo + (i + 1) * block, :] = pre
+    for k in range(3):
+        low = halo + k - 1
+        pre_ref[k] = shift_wide_ref[low : low + frames, :].astype(bf16)
+    shift_ref[...] = jnp.zeros(shift_ref.shape, f32)
+
+    turns_first = freq_first_ref[...] * (1.0 / math.pi)
+    inverse_first = 1.0 / freq_first_ref[...]
+    turns_second = freq_second_ref[...] * (1.0 / math.pi)
+    inverse_second = 1.0 / freq_second_ref[...]
+
+    def neighbour_rows(offset):
+        low = halo + offset
+        return shift_ref[low : low + frames, :].astype(bf16)
+
+    up_copy.wait()
+
+    def pipeline(product, finish):
         for i in range(blocks):
             rows = slice(i * block, (i + 1) * block)
-            pre = jnp.dot(taps_ref[rows, :], input_weight_ref[...], preferred_element_type=f32)
-            pre = jnp.where(keep_rows(i * block, block), pre + input_bias_ref[...], 0.0)
-            shift_wide_ref[halo + i * block : halo + (i + 1) * block, :] = pre
-        for k in range(3):
-            low = halo + k - 1
-            pre_ref[k] = shift_wide_ref[low : low + frames, :].astype(bf16)
-        shift_ref[...] = jnp.zeros(shift_ref.shape, f32)
-
-        turns_first = freq_first_ref[...] * (1.0 / math.pi)
-        inverse_first = 1.0 / freq_first_ref[...]
-        turns_second = freq_second_ref[...] * (1.0 / math.pi)
-        inverse_second = 1.0 / freq_second_ref[...]
-
-        def neighbour_rows(offset):
-            low = halo + offset
-            return shift_ref[low : low + frames, :].astype(bf16)
-
-        up_copy.wait()
-
-        def pipeline(product, finish):
+            even_ref[rows, :] = product(0, rows)
+
+        for r in range(UP):
+            ready_ref, next_ref = (even_ref, odd_ref) if r % 2 == 0 else (odd_ref, even_ref)
             for i in range(blocks):
                 rows = slice(i * block, (i + 1) * block)
-                even_ref[rows, :] = product(0, rows)
-
-            @pl.loop(0, UP // 2)
-            def _(pair):
-                for r, ready_ref, r_next, next_ref in (
-                    (2 * pair, even_ref, 2 * pair + 1, odd_ref),
-                    (2 * pair + 1, odd_ref, jnp.minimum(2 * pair + 2, UP - 1), even_ref),
-                ):
-                    for i in range(blocks):
-                        rows = slice(i * block, (i + 1) * block)
-                        next_ref[rows, :] = product(r_next, rows)
-                        for low in range(i * block, (i + 1) * block, 64):
-                            finish(r, low, ready_ref[low : low + 64, :])
-
-        def up_product(r, rows):
-            side = jnp.where(r < UP // 2, 0, 2)
-            return nt_dot(
-                jnp.concatenate([pre_ref[1, rows, :], pre_ref[side, rows, :]], axis=1),
-                jnp.concatenate(
-                    [up_weight_ref[r + UP // 2], up_weight_ref[lax.rem(r + UP // 2 + UP, KT)]],
-                    axis=1,
-                ),
-            )
-
-        def up_finish(r, low, up):
-            rows = slice(low, low + 64)
-            up = jnp.where(keep_rows(low, 64), up + up_bias_ref[...], 0.0)
-            up = up.astype(bf16)
-            up_ref[r, rows, :] = up
-            first = snake_rows(up.astype(f32), turns_first, inverse_first)
-            first_ref[r + 3, rows, :] = first.astype(bf16)
-
-        pipeline(up_product, up_finish)
-
-        for r in range(DILATION_RATE):
-            shift_ref[halo : halo + frames, :] = first_ref[r + 3].astype(f32)
-            first_ref[r + 3 + UP] = neighbour_rows(1)
-        for r in range(UP - DILATION_RATE, UP):
-            shift_ref[halo : halo + frames, :] = first_ref[r + 3].astype(f32)
-            first_ref[r + 3 - UP] = neighbour_rows(-1)
-
-        def inner_product(r, rows):
-            around = [first_ref[r + DILATION_RATE * k, rows, :] for k in range(3)]
-            return jnp.dot(
-                jnp.concatenate(around, axis=1),
-                dilated_weight_ref[...],
-                preferred_element_type=f32,
-            )
-
-        def inner_finish(r, low, inner):
-            inner = jnp.where(keep_rows(low, 64), inner + dilated_bias_ref[...], 0.0)
-            second = snake_rows(inner, turns_second, inverse_second)
-            second_ref[r + 1, low : low + 64, :] = second.astype(bf16)
-
-        pipeline(inner_product, inner_finish)
-
-        shift_ref[halo : halo + frames, :] = second_ref[1].astype(f32)
-        second_ref[UP + 1] = neighbour_rows(1)
-        shift_ref[halo : halo + frames, :] = second_ref[UP].astype(f32)
-        second_ref[0] = neighbour_rows(-1)
-
-        def outer_product(r, rows):
-            around = [second_ref[r + k, rows, :] for k in range(3)]
-            return jnp.dot(
+                if r + 1 < UP:
+                    next_ref[rows, :] = product(r + 1, rows)
+                for low in range(i * block, (i + 1) * block, 64):
+                    finish(r, low, ready_ref[low : low + 64, :])
+
+    def up_product(r, rows):
+        side = 0 if r < UP // 2 else 2
+        return jnp.dot(
+            jnp.concatenate([pre_ref[1, rows, :], pre_ref[side, rows, :]], axis=1),
+            jnp.concatenate(
+                [up_weight_ref[r + UP // 2], up_weight_ref[(r + UP // 2 + UP) % KT]],
+                axis=0,
+            ),
+            preferred_element_type=f32,
+        )
+
+    def up_finish(r, low, up):
+        rows = slice(low, low + 64)
+        up = jnp.where(keep_rows(low, 64), up + up_bias_ref[...], 0.0)
+        up = up.astype(bf16)
+        up_ref[r, rows, :] = up
+        first = snake_rows(up.astype(f32), turns_first, inverse_first)
+        first_ref[r + 3, rows, :] = first.astype(bf16)
+
+    pipeline(up_product, up_finish)
+
+    for r in range(DILATION_RATE):
+        shift_ref[halo : halo + frames, :] = first_ref[r + 3].astype(f32)
+        first_ref[r + 3 + UP] = neighbour_rows(1)
+    for r in range(UP - DILATION_RATE, UP):
+        shift_ref[halo : halo + frames, :] = first_ref[r + 3].astype(f32)
+        first_ref[r + 3 - UP] = neighbour_rows(-1)
+
+    def inner_product(r, rows):
+        around = [first_ref[r + DILATION_RATE * k, rows, :] for k in range(3)]
+        return jnp.dot(
+            jnp.concatenate(around, axis=1),
+            dilated_weight_ref[...],
+            preferred_element_type=f32,
+        )
+
+    def inner_finish(r, low, inner):
+        inner = jnp.where(keep_rows(low, 64), inner + dilated_bias_ref[...], 0.0)
+        second = snake_rows(inner, turns_second, inverse_second)
+        second_ref[r + 1, low : low + 64, :] = second.astype(bf16)
+
+    pipeline(inner_product, inner_finish)
+
+    shift_ref[halo : halo + frames, :] = second_ref[1].astype(f32)
+    second_ref[UP + 1] = neighbour_rows(1)
+    shift_ref[halo : halo + frames, :] = second_ref[UP].astype(f32)
+    second_ref[0] = neighbour_rows(-1)
+
+    narrow = 256 // UP
+    row = lax.broadcasted_iota(jnp.int32, (256, 256), 0)
+    col = lax.broadcasted_iota(jnp.int32, (256, 256), 1)
+    weave = (col == lax.rem(row, narrow) * UP + row // narrow).astype(bf16)
+
+    def outer_product(low):
+        for r in range(UP):
+            around = [second_ref[r + k, low : low + 128, :] for k in range(3)]
+            outer = jnp.dot(
                 jnp.concatenate(around, axis=1),
                 second_weight_ref[...],
                 preferred_element_type=f32,
             )
-
-        def outer_finish(r, low, outer):
-            rows = slice(low, low + 64)
-            outer = jnp.where(keep_rows(low, 64), outer + second_bias_ref[...], 0.0)
-            out_ref[r, rows, :] = (up_ref[r, rows, :].astype(f32) + outer).astype(bf16)
-
-        pipeline(outer_product, outer_finish)
-
-    base = pl.multiple_of(step * piece_frames, piece_frames)
-    narrow = 256 // UP
-    row = lax.broadcasted_iota(jnp.int32, (256, 256), 0)
-    col = lax.broadcasted_iota(jnp.int32, (256, 256), 1)
-    weave = (col == lax.rem(row, narrow) * UP + row // narrow).astype(bf16)
-    for piece in range(piece_frames // narrow):
-        rows = pl.ds(base + piece * narrow, narrow)
-        phases = jnp.concatenate([out_ref[r, rows, :] for r in range(UP)], axis=0)
-        woven = lax.dot_general(
-            phases, weave, (((0,), (0,)), ((), ())), preferred_element_type=f32
+            outer = jnp.where(keep_rows(low, 128), outer + second_bias_ref[...], 0.0)
+            up = up_ref[r, low : low + 128, :].astype(f32)
+            out_ref[r, low : low + 128, :] = (up + outer).astype(bf16)
+
+    copies = []
+
+    def woven(low):
+        for first in range(low, low + 128, narrow):
+            phases = jnp.concatenate(
+                [out_ref[r, first : first + narrow, :] for r in range(UP)], axis=0
+            )
+            samples = lax.dot_general(
+                phases, weave, (((0,), (0,)), ((), ())), preferred_element_type=f32
+            )
+            wave_ref[:, first * UP : (first + narrow) * UP] = samples.astype(bf16)
+        columns = pl.ds(low * UP, 128 * UP)
+        copy = pltpu.make_async_copy(
+            wave_ref.at[:, columns], wave_hbm.at[0, :, columns], wave_sem.at[low // 128]
         )
-        wave_ref[0, :, piece * 256 : (piece + 1) * 256] = woven.astype(bf16)
+        copy.start()
+        copies.append(copy)
+
+    for low in range(0, frames + 128, 128):
+        if low < frames:
+            outer_product(low)
+        if low > 0:
+            woven(low - 128)
+    for copy in copies:
+        copy.wait()
 
 
 def vocoder(
@@ -469,8 +480,7 @@
     second_conv_weight,
     second_conv_bias,
     frames,
-    block=256,
-    piece=256,
+    block=128,
 ):
     wide = input_conv_bias.shape[0]
     channels = transposed_conv_bias.shape[0]
@@ -482,7 +492,7 @@
         arrived,
         taps_weight,
         input_conv_bias[None],
-        transposed_conv_weight.reshape(KT, channels, wide),
+        transposed_conv_weight.reshape(KT, channels, wide).transpose(0, 2, 1),
         transposed_conv_bias[None],
         snake_freq_first[None],
         dilated_conv_weight,
@@ -494,15 +504,14 @@
     return pl.pallas_call(
         functools.partial(vocoder_kernel, mel_bins=mel_bins, block=block),
         out_shape=jax.ShapeDtypeStruct((1, channels, frames * UP), bf16),
-        grid=(frames // piece,),
         in_specs=[pl.BlockSpec(memory_space=pltpu.SMEM)]
         + [
             pl.BlockSpec(memory_space=pl.ANY)
             if x.ndim == 3 and x.shape[0] == KT
-            else pl.BlockSpec(x.shape, lambda i, n=x.ndim: (0,) * n, pipeline_mode=pl.Buffered(1))
+            else pl.BlockSpec(memory_space=pltpu.VMEM)
             for x in operands
         ],
-        out_specs=pl.BlockSpec((1, channels, piece * UP), lambda i: (0, 0, i)),
+        out_specs=pl.BlockSpec(memory_space=pl.ANY),
         scratch_shapes=[
             pltpu.VMEM((frames + 16, LANES), f32),
             pltpu.VMEM((frames, KPRE * LANES), bf16),
@@ -513,10 +522,12 @@
             pltpu.VMEM((UP + 6, frames, channels), bf16),
             pltpu.VMEM((UP + 2, frames, channels), bf16),
             pltpu.VMEM((UP, frames, channels), bf16),
-            pltpu.VMEM((KT, channels, wide), bf16),
+            pltpu.VMEM((KT, wide, channels), bf16),
             pltpu.SemaphoreType.DMA(()),
             pltpu.VMEM((frames, channels), f32),
             pltpu.VMEM((frames, channels), f32),
+            pltpu.VMEM((channels, frames * UP), bf16),
+            pltpu.SemaphoreType.DMA((frames // 128,)),
         ],
         compiler_params=pltpu.CompilerParams(vmem_limit_bytes=60 * 1024 * 1024),
         name="vocoder",

time: 81.3 us -> 77.2 us (0.950)
  waiting for transfers between devices: 10.3 us -> 3.92 us
  local copies, waits for them, and re-layouts: 2.51 us -> 8.83 us
  Pallas kernels: 38.6 us -> 34.3 us
    reshape x0 -> x1, local copies, waits for them, and re-layouts: none -> 6.39 us  [vocoder(): transposed_conv_weight.reshape(KT, channels, wide).transpose(0, 2, 1)]
    all_to_all x1, waiting for transfers between devices: 8.88 us -> 2.55 us  [local(): lax.all_to_all(slots.reshape(owners, GROUP, LANES), ('branch', 'seq'), 0,...]
    pallas_call x1, Pallas kernels: 24.7 us -> 20.4 us  [vocoder(): pl.pallas_call(functools.partial(vocoder_kernel, mel_bins=mel_bins, block...]
  transfers between devices with their start and end apart: 2 -> 2, of which waited for: 2 -> 2; matrix products, arithmetic and copies ran while one was open for 2% -> 11% of each run, Pallas kernels for 0% -> 0%
where the time goes in v5:
time: 77.2 us; the launch traced here: 76.8 us
  Pallas kernels  34.3 us (44%)
  blocking collectives  19.7 us (26%)
  local copies, waits for them, and re-layouts  8.83 us (11%)
  starting transfers between devices  6.91 us (9%)
  waiting for transfers between devices  3.92 us (5%)
  matrix products  1.53 us (2%)
  other arithmetic  1.33 us (2%)
    pallas_call x1, Pallas kernels, vocoder(): pl.pallas_call(functools.partial(vocoder_kernel, mel_bins=mel_bins, block...  20.4 us
    all_to_all x1, blocking collectives, local(): lax.all_to_all(packed.reshape(chips, GROUP, LANES), 'seq', 0, 0, tiled=True)  19.7 us
    pallas_call x1, Pallas kernels, velocity_halves(): pl.pallas_call(functools.partial(velocity_kernel, block=block, tail=tail,...  13.9 us
    reshape x1, local copies, waits for them, and re-layouts, vocoder(): transposed_conv_weight.reshape(KT, channels, wide).transpose(0, 2, 1)  6.39 us
    all_to_all x1, starting transfers between devices, local(): lax.all_to_all(slots.reshape(owners, GROUP, LANES), ('branch', 'seq'), 0,...  5.41 us
    all_to_all x1, waiting for transfers between devices, local(): lax.all_to_all(slots.reshape(owners, GROUP, LANES), ('branch', 'seq'), 0,...  2.55 us
  transfers between devices with their start and end apart: 2, of which 2 were waited for; matrix products, arithmetic and copies ran while one was open for 11% of the time, Pallas kernels for 0%

profile of v5, /device:TPU:1, one launch (start us, length us, event | category | flops | bytes accessed | tf_op | source)
XLA Modules:
  0.0 76.8 jit_solution(3277400788563014181)
XLA Ops:
  0.0 0.0 copy-start.1
  0.0 13.9 %velocity.1 = (f32[512,128]{1,0:T(8,128)}, f32[512,128]{1,0:T(8,128)}, f32[512,128]{1,0:T(8,128)}) custom-call(s32[1]{0:T(128)} %bitcast.side_ref, bf16[1,768,1024]{2,1,0:T(8,128)(2,1)} %hidden_hbm.1, f32[5,1024]{1,0:T(8,128)} %modulation_ref.1, bf16[1024,2048]{1,0:T(8,128)(2,1)} %in_weight_hbm.1, f32[1,2048]{1,0:T(1,128)} %bitcast.30, ...), custom_call_target="tpu_custom_call" | custom-call | tf_op jit(solution)/shard_map/velocity/pallas_call | solution.py:209
  13.9 1.5 %collective-permute-start = (f32[512,128]{1,0:T(8,128)}, f32[512,128]{1,0:T(8,128)S(1)}, u32[]{:S(2)}, u32[]{:S(2)}) collective-permute-start(f32[512,128]{1,0:T(8,128)} %get-tuple-element.10), channel_id=1, source_target_pairs={{0,64},{64,0},{1,65},{65,1},{2,66},{66,2},{3,67},{67,3},{4,68},{68... | collective-permute-start | bytes 786440 | tf_op jit(solution)/shard_map/ppermute | solution.py:581
  15.4 1.4 %collective-permute-done = f32[512,128]{1,0:T(8,128)S(1)} collective-permute-done((f32[512,128]{1,0:T(8,128)}, f32[512,128]{1,0:T(8,128)S(1)}, u32[]{:S(2)}, u32[]{:S(2)}) %collective-permute-start) | collective-permute-done | bytes 262176 | tf_op jit(solution)/shard_map/ppermute | solution.py:581
  16.8 1.1 %fusion.9 = bf16[64,8,128]{2,1,0:T(8,128)(2,1)S(1)} fusion(f32[512,128]{1,0:T(8,128)} %get-tuple-element.8, f32[512,128]{1,0:T(8,128)S(1)} %collective-permute-done, f32[512,128]{1,0:T(8,128)} %get-tuple-element.9, pred[]{:T(512)S(6)} %eq.21), kind=kLoop, calls=%fused_computation.13 | loop fusion | flops 524288 | bytes 917505 | tf_op jit(solution)/shard_map/reshape | solution.py:586
  17.9 19.7 %all_to_all.10 = bf16[64,8,128]{2,1,0:T(8,128)(2,1)S(1)} all-to-all(bf16[64,8,128]{2,1,0:T(8,128)(2,1)S(1)} %fusion.9), channel_id=1, replica_groups=mesh['branch'=2,'seq'=64] {'seq'}, dimensions={0} | all-to-all | bytes 262144 | tf_op jit(solution)/shard_map/all_to_all | solution.py:586
  37.5 0.2 fusion.5
  37.8 1.5 %fusion.2 = bf16[128,8,128]{2,1,0:T(8,128)(2,1)} fusion(s32[512]{0:T(512)S(1)} %fusion.5, bf16[64,8,128]{2,1,0:T(8,128)(2,1)S(1)} %all_to_all.10), kind=kOutput, calls=%fused_computation.3 | convolution fusion | flops 134873088 | bytes 395264 | tf_op jit(solution)/shard_map/dot_general | solution.py:593
  39.3 5.4 %all-to-all-start.1 = ((bf16[128,8,128]{2,1,0:T(8,128)(2,1)}), bf16[128,8,128]{2,1,0:T(8,128)(2,1)S(1)}, u32[]{:S(2)}, u32[]{:S(2)}) async-start(bf16[128,8,128]{2,1,0:T(8,128)(2,1)} %fusion.2), calls=%async_computation.1 | async-start | bytes 524288 | tf_op jit(solution)/shard_map/all_to_all | solution.py:596
  44.7 0.0 copy-done.1
  44.7 0.1 reshape.55
  44.9 0.0 copy-start.2
  44.9 6.4 %copy.25 = bf16[16,256,512]{1,2,0:T(8,128)(2,1)} copy(bf16[16,256,512]{2,1,0:T(8,128)(2,1)} %bitcast.25) | data formatting | bytes 8388608 | tf_op jit(solution)/shard_map/reshape | solution.py:495
  51.3 0.0 copy-done.2
  51.3 0.6 dynamic_slice.3.length_ref
  51.9 1.0 %pad.4 = bf16[7,128,512]{2,1,0:T(8,128)(2,1)} pad(bf16[7,100,512]{2,1,0:T(8,128)(2,1)S(1)} %reshape.55, bf16[]{:T(256)} %constant.38.clone.1), padding=0_0x0_28x0_0 | pad | bytes 1634306 | tf_op jit(solution)/shard_map/jit(_pad)/pad | solution.py:488
  52.9 2.5 %all-to-all-done.1 = bf16[128,8,128]{2,1,0:T(8,128)(2,1)S(1)} async-done(((bf16[128,8,128]{2,1,0:T(8,128)(2,1)}), bf16[128,8,128]{2,1,0:T(8,128)(2,1)S(1)}, u32[]{:S(2)}, u32[]{:S(2)}) %all-to-all-start.1) | async-done | bytes 262176 | tf_op jit(solution)/shard_map/all_to_all | solution.py:596
  55.4 0.0 copy-start
  55.4 0.7 copy-done
  56.1 20.4 %vocoder.1 = bf16[1,256,6144]{2,1,0:T(8,128)(2,1)} custom-call(s32[1]{0:T(128)} %dynamic_slice.3.length_ref, bf16[1024,128]{1,0:T(8,128)(2,1)} %bitcast.27, bf16[896,512]{1,0:T(8,128)(2,1)} %bitcast.26, f32[1,512]{1,0:T(1,128)} %bitcast.34, bf16[16,512,256]{2,1,0:T(8,128)(2,1)} %bitcast.24, f32[1,256]{1,0:T(1,128)} %bitcast.35, f32[1,256]{1,0:T(1,128)} %bitcast.36, ...), custom_call_target="tpu_custom_call" | custom-call | tf_op jit(solution)/shard_map/vocoder/pallas_call | solution.py:504
Async XLA Ops:
  0.0 44.7 %copy-start.1 = (bf16[700,512]{1,0:T(8,128)(2,1)S(1)}, bf16[700,512]{1,0:T(8,128)(2,1)}, u32[]{:S(2)}) copy-start(bf16[700,512]{1,0:T(8,128)(2,1)} %param.31) | copy-start | bytes 2150404
  13.9 2.9 %collective-permute-start = (f32[512,128]{1,0:T(8,128)}, f32[512,128]{1,0:T(8,128)S(1)}, u32[]{:S(2)}, u32[]{:S(2)}) collective-permute-start(f32[512,128]{1,0:T(8,128)} %get-tuple-element.10), channel_id=1, source_target_pairs={{0,64},{64,0},{1,65},{65,1},{2,66},{66,2},{3,67},{67,3},{4,68},{68... | collective-permute-start | bytes 786440 | tf_op jit(solution)/shard_map/ppermute | solution.py:581
  39.3 16.1 %all-to-all-start.1 = ((bf16[128,8,128]{2,1,0:T(8,128)(2,1)}), bf16[128,8,128]{2,1,0:T(8,128)(2,1)S(1)}, u32[]{:S(2)}, u32[]{:S(2)}) async-start(bf16[128,8,128]{2,1,0:T(8,128)(2,1)} %fusion.2), calls=%async_computation.1 | async-start | bytes 524288 | tf_op jit(solution)/shard_map/all_to_all | solution.py:596
  44.9 6.4 %copy-start.2 = (s32[128]{0:T(128)S(1)}, s32[128]{0:T(128)}, u32[]{:S(2)}) copy-start(s32[128]{0:T(128)} %param.43) | copy-start | bytes 1540
  55.4 0.7 copy-start

commit v6 on v5

--- a/solution.py
+++ b/solution.py
@@ -529,7 +529,7 @@
             pltpu.VMEM((channels, frames * UP), bf16),
             pltpu.SemaphoreType.DMA((frames // 128,)),
         ],
-        compiler_params=pltpu.CompilerParams(vmem_limit_bytes=60 * 1024 * 1024),
+        compiler_params=pltpu.CompilerParams(vmem_limit_bytes=50 * 1024 * 1024),
         name="vocoder",
     )(length, *operands)
 

time: 77.2 us -> 74 us (0.959)
  Pallas kernels: 34.3 us -> 31.8 us
  local copies, waits for them, and re-layouts: 8.83 us -> 7.3 us
  waiting for transfers between devices: 3.92 us -> 4.7 us
    pallas_call x1, Pallas kernels: 20.4 us -> 18 us  [vocoder(): pl.pallas_call(functools.partial(vocoder_kernel, mel_bins=mel_bins, block...]
    pad x1, local copies, waits for them, and re-layouts: 1.01 us -> 0.08 us  [vocoder(): jnp.pad(input_conv_weight.reshape(KPRE, mel_bins, wide), ((0, 0), (0, LAN...]
    all_to_all x1, waiting for transfers between devices: 2.55 us -> 3.32 us  [local(): lax.all_to_all(slots.reshape(owners, GROUP, LANES), ('branch', 'seq'), 0,...]
  transfers between devices with their start and end apart: 2 -> 2, of which waited for: 2 -> 2; matrix products, arithmetic and copies ran while one was open for 11% -> 10% of each run, Pallas kernels for 0% -> 0%
where the time goes in v6:
time: 74 us; the launch traced here: 73.6 us
  Pallas kernels  31.8 us (43%)
  blocking collectives  19.7 us (27%)
  local copies, waits for them, and re-layouts  7.3 us (10%)
  starting transfers between devices  6.91 us (9%)
  waiting for transfers between devices  4.7 us (6%)
  matrix products  1.53 us (2%)
  other arithmetic  1.33 us (2%)
    all_to_all x1, blocking collectives, local(): lax.all_to_all(packed.reshape(chips, GROUP, LANES), 'seq', 0, 0, tiled=True)  19.7 us
    pallas_call x1, Pallas kernels, vocoder(): pl.pallas_call(functools.partial(vocoder_kernel, mel_bins=mel_bins, block...  18 us
    pallas_call x1, Pallas kernels, velocity_halves(): pl.pallas_call(functools.partial(velocity_kernel, block=block, tail=tail,...  13.9 us
    reshape x1, local copies, waits for them, and re-layouts, vocoder(): transposed_conv_weight.reshape(KT, channels, wide).transpose(0, 2, 1)  6.46 us
    all_to_all x1, starting transfers between devices, local(): lax.all_to_all(slots.reshape(owners, GROUP, LANES), ('branch', 'seq'), 0,...  5.41 us
    all_to_all x1, waiting for transfers between devices, local(): lax.all_to_all(slots.reshape(owners, GROUP, LANES), ('branch', 'seq'), 0,...  3.32 us
    dot_general x1, matrix products, local(): lax.dot_general(onehot, rows, (((0,), (0,)), ((), ())), preferred_element...  1.53 us
    ppermute x1, starting transfers between devices, local(): peer_half = lax.ppermute(sent_half, 'branch', [(0, 1), (1, 0)])  1.49 us
  transfers between devices with their start and end apart: 2, of which 2 were waited for; matrix products, arithmetic and copies ran while one was open for 10% of the time, Pallas kernels for 0%

profile of v6, /device:TPU:1, one launch (start us, length us, event | category | flops | bytes accessed | tf_op | source)
XLA Modules:
  0.0 73.6 jit_solution(12985823627294134809)
XLA Ops:
  0.0 0.0 copy-start.8
  0.0 13.9 %velocity.1 = (f32[512,128]{1,0:T(8,128)}, f32[512,128]{1,0:T(8,128)}, f32[512,128]{1,0:T(8,128)}) custom-call(s32[1]{0:T(128)} %bitcast.side_ref, bf16[1,768,1024]{2,1,0:T(8,128)(2,1)} %hidden_hbm.1, f32[5,1024]{1,0:T(8,128)} %modulation_ref.1, bf16[1024,2048]{1,0:T(8,128)(2,1)} %in_weight_hbm.1, f32[1,2048]{1,0:T(1,128)} %bitcast.36, ...), custom_call_target="tpu_custom_call" | custom-call | tf_op jit(solution)/shard_map/velocity/pallas_call | solution.py:209
  13.9 1.5 %collective-permute-start = (f32[512,128]{1,0:T(8,128)}, f32[512,128]{1,0:T(8,128)S(1)}, u32[]{:S(2)}, u32[]{:S(2)}) collective-permute-start(f32[512,128]{1,0:T(8,128)} %get-tuple-element.10), channel_id=1, source_target_pairs={{0,64},{64,0},{1,65},{65,1},{2,66},{66,2},{3,67},{67,3},{4,68},{68... | collective-permute-start | bytes 786440 | tf_op jit(solution)/shard_map/ppermute | solution.py:581
  15.4 1.4 %collective-permute-done = f32[512,128]{1,0:T(8,128)S(1)} collective-permute-done((f32[512,128]{1,0:T(8,128)}, f32[512,128]{1,0:T(8,128)S(1)}, u32[]{:S(2)}, u32[]{:S(2)}) %collective-permute-start) | collective-permute-done | bytes 262176 | tf_op jit(solution)/shard_map/ppermute | solution.py:581
  16.8 1.1 %fusion.9 = bf16[64,8,128]{2,1,0:T(8,128)(2,1)S(1)} fusion(f32[512,128]{1,0:T(8,128)} %get-tuple-element.8, f32[512,128]{1,0:T(8,128)S(1)} %collective-permute-done, f32[512,128]{1,0:T(8,128)} %get-tuple-element.9, pred[]{:T(512)S(6)} %eq.21), kind=kLoop, calls=%fused_computation.13 | loop fusion | flops 524288 | bytes 917505 | tf_op jit(solution)/shard_map/reshape | solution.py:586
  17.9 19.7 %all_to_all.10 = bf16[64,8,128]{2,1,0:T(8,128)(2,1)S(1)} all-to-all(bf16[64,8,128]{2,1,0:T(8,128)(2,1)S(1)} %fusion.9), channel_id=1, replica_groups=mesh['branch'=2,'seq'=64] {'seq'}, dimensions={0} | all-to-all | bytes 262144 | tf_op jit(solution)/shard_map/all_to_all | solution.py:586
  37.5 0.2 fusion.5
  37.8 1.5 %fusion.2 = bf16[128,8,128]{2,1,0:T(8,128)(2,1)} fusion(s32[512]{0:T(512)S(1)} %fusion.5, bf16[64,8,128]{2,1,0:T(8,128)(2,1)S(1)} %all_to_all.10), kind=kOutput, calls=%fused_computation.3 | convolution fusion | flops 134873088 | bytes 395264 | tf_op jit(solution)/shard_map/dot_general | solution.py:593
  39.3 5.4 %all-to-all-start.1 = ((bf16[128,8,128]{2,1,0:T(8,128)(2,1)}), bf16[128,8,128]{2,1,0:T(8,128)(2,1)S(1)}, u32[]{:S(2)}, u32[]{:S(2)}) async-start(bf16[128,8,128]{2,1,0:T(8,128)(2,1)} %fusion.2), calls=%async_computation.1 | async-start | bytes 524288 | tf_op jit(solution)/shard_map/all_to_all | solution.py:596
  44.7 0.0 copy-done.8
  44.7 0.1 reshape.55
  44.9 0.0 copy-start.9
  44.9 0.0 copy-start
  44.9 0.0 copy-start.1
  44.9 0.0 copy-start.2
  44.9 0.0 copy-start.3
  44.9 0.0 copy-start.4
  44.9 0.0 copy-start.5
  44.9 0.0 copy-start.6
  45.0 0.0 copy-start.7
  45.0 6.5 %copy.25 = bf16[16,256,512]{1,2,0:T(8,128)(2,1)} copy(bf16[16,256,512]{2,1,0:T(8,128)(2,1)} %bitcast.33) | data formatting | bytes 8388608 | tf_op jit(solution)/shard_map/reshape | solution.py:495
  51.4 0.0 copy-done.9
  51.4 0.6 dynamic_slice.3.length_ref
  52.0 0.1 pad.4
  52.1 3.3 %all-to-all-done.1 = bf16[128,8,128]{2,1,0:T(8,128)(2,1)S(1)} async-done(((bf16[128,8,128]{2,1,0:T(8,128)(2,1)}), bf16[128,8,128]{2,1,0:T(8,128)(2,1)S(1)}, u32[]{:S(2)}, u32[]{:S(2)}) %all-to-all-start.1) | async-done | bytes 262176 | tf_op jit(solution)/shard_map/all_to_all | solution.py:596
  55.4 0.0 copy-done
  55.4 0.0 copy-done.1
  55.4 0.0 copy-done.2
  55.4 0.0 copy-done.3
  55.4 0.0 copy-done.4
  55.5 0.0 copy-done.5
  55.5 0.0 copy-done.6
  55.5 0.0 copy-done.7
  55.5 18.0 %vocoder.1 = bf16[1,256,6144]{2,1,0:T(8,128)(2,1)} custom-call(s32[1]{0:T(128)} %dynamic_slice.3.length_ref, bf16[1024,128]{1,0:T(8,128)(2,1)S(1)} %bitcast.25, bf16[896,512]{1,0:T(8,128)(2,1)S(1)} %bitcast.24, f32[1,512]{1,0:T(1,128)S(1)} %bitcast.26, bf16[16,512,256]{2,1,0:T(8,128)(2,1)} %bitcast.32, f32[1,256]{1,0:T(1,128)S(1)} %bitcast.27, ...), custom_call_target="tpu_custom_call" | custom-call | tf_op jit(solution)/shard_map/vocoder/pallas_call | solution.py:504
Async XLA Ops:
  0.0 44.7 %copy-start.8 = (bf16[700,512]{1,0:T(8,128)(2,1)S(1)}, bf16[700,512]{1,0:T(8,128)(2,1)}, u32[]{:S(2)}) copy-start(bf16[700,512]{1,0:T(8,128)(2,1)} %param.31) | copy-start | bytes 2150404
  13.9 2.9 %collective-permute-start = (f32[512,128]{1,0:T(8,128)}, f32[512,128]{1,0:T(8,128)S(1)}, u32[]{:S(2)}, u32[]{:S(2)}) collective-permute-start(f32[512,128]{1,0:T(8,128)} %get-tuple-element.10), channel_id=1, source_target_pairs={{0,64},{64,0},{1,65},{65,1},{2,66},{66,2},{3,67},{67,3},{4,68},{68... | collective-permute-start | bytes 786440 | tf_op jit(solution)/shard_map/ppermute | solution.py:581
  39.3 16.1 %all-to-all-start.1 = ((bf16[128,8,128]{2,1,0:T(8,128)(2,1)}), bf16[128,8,128]{2,1,0:T(8,128)(2,1)S(1)}, u32[]{:S(2)}, u32[]{:S(2)}) async-start(bf16[128,8,128]{2,1,0:T(8,128)(2,1)} %fusion.2), calls=%async_computation.1 | async-start | bytes 524288 | tf_op jit(solution)/shard_map/all_to_all | solution.py:596
  44.9 6.6 %copy-start.9 = (s32[128]{0:T(128)S(1)}, s32[128]{0:T(128)}, u32[]{:S(2)}) copy-start(s32[128]{0:T(128)} %param.43) | copy-start | bytes 1540
  44.9 10.6 %copy-start = (bf16[768,256]{1,0:T(8,128)(2,1)S(1)}, bf16[768,256]{1,0:T(8,128)(2,1)}, u32[]{:S(2)}) copy-start(bf16[768,256]{1,0:T(8,128)(2,1)} %dilated_weight_ref.1) | copy-start | bytes 1179652
  44.9 10.6 %copy-start.1 = (bf16[768,256]{1,0:T(8,128)(2,1)S(1)}, bf16[768,256]{1,0:T(8,128)(2,1)}, u32[]{:S(2)}) copy-start(bf16[768,256]{1,0:T(8,128)(2,1)} %second_weight_ref.1) | copy-start | bytes 1179652
  44.9 10.5 %copy-start.2 = (f32[512]{0:T(512)S(1)}, f32[512]{0:T(512)}, u32[]{:S(2)}) copy-start(f32[512]{0:T(512)} %param.32) | copy-start | bytes 6148
  44.9 10.5 %copy-start.3 = (f32[256]{0:T(256)S(1)}, f32[256]{0:T(256)}, u32[]{:S(2)}) copy-start(f32[256]{0:T(256)} %param.34) | copy-start | bytes 3076
  44.9 10.5 %copy-start.4 = (f32[256]{0:T(256)S(1)}, f32[256]{0:T(256)}, u32[]{:S(2)}) copy-start(f32[256]{0:T(256)} %param.35) | copy-start | bytes 3076
  44.9 10.5 %copy-start.5 = (f32[256]{0:T(256)S(1)}, f32[256]{0:T(256)}, u32[]{:S(2)}) copy-start(f32[256]{0:T(256)} %param.37) | copy-start | bytes 3076
  44.9 10.5 %copy-start.6 = (f32[256]{0:T(256)S(1)}, f32[256]{0:T(256)}, u32[]{:S(2)}) copy-start(f32[256]{0:T(256)} %param.38) | copy-start | bytes 3076
  45.0 10.5 %copy-start.7 = (f32[256]{0:T(256)S(1)}, f32[256]{0:T(256)}, u32[]{:S(2)}) copy-start(f32[256]{0:T(256)} %param.40) | copy-start | bytes 3076

commit v7 on v6

--- a/solution.py
+++ b/solution.py
@@ -55,7 +55,6 @@
     position_ref,
     own_ref,
     sent_ref,
-    base_ref,
     hidden_ref,
     in_weight_ref,
     out_weight_ref,
@@ -66,6 +65,7 @@
     active_ref,
     speed_ref,
     back_ref,
+    base_ref,
     hidden_sem,
     in_sem,
     out_sem,
@@ -171,14 +171,16 @@
             finish(i - 1)
             emit(i - 1)
 
+    step_size = math.cos(0.5 * math.pi * (NFE - 1) / NFE)
+
     @pl.when(side_ref[0] == 0)
     def _():
-        own_ref[...] = speed_ref[0]
+        own_ref[...] = base_ref[...] + (step_size * (1.0 + GUIDE)) * speed_ref[0]
         sent_ref[...] = speed_ref[1]
 
     @pl.when(side_ref[0] != 0)
     def _():
-        own_ref[...] = speed_ref[1]
+        own_ref[...] = base_ref[...] - (step_size * GUIDE) * speed_ref[1]
         sent_ref[...] = speed_ref[0]
 
 
@@ -208,9 +210,9 @@
     hbm = pl.BlockSpec(memory_space=pl.ANY)
     return pl.pallas_call(
         functools.partial(velocity_kernel, block=block, tail=tail, in_chunk=in_chunk),
-        out_shape=(spaced,) * 3,
+        out_shape=(spaced,) * 2,
         in_specs=[pl.BlockSpec(memory_space=pltpu.SMEM), hbm, vmem, hbm, vmem, hbm] + [vmem] * 6,
-        out_specs=(vmem,) * 3,
+        out_specs=(vmem,) * 2,
         scratch_shapes=[
             pltpu.VMEM((frames, width), bf16),
             pltpu.VMEM((width, units), bf16),
@@ -222,6 +224,7 @@
             pltpu.VMEM((frames, units), bf16),
             pltpu.VMEM((2, chips * GROUP, LANES), f32),
             pltpu.VMEM((2, tail, width), f32),
+            pltpu.VMEM((chips * GROUP, LANES), f32),
             pltpu.SemaphoreType.DMA((frames // block,)),
             pltpu.SemaphoreType.DMA((units // in_chunk,)),
             pltpu.SemaphoreType.DMA(()),
@@ -563,7 +566,7 @@
     owners = lax.axis_size("branch") * chips
     mel_bins, frames = noisy_mel_state.shape
     branch_side = lax.axis_index("branch").astype(jnp.int32)
-    own_half, sent_half, base = velocity_halves(
+    own_half, sent_half = velocity_halves(
         branch_side[None],
         hidden,
         modulation,
@@ -579,10 +582,8 @@
         chips,
     )
     peer_half = lax.ppermute(sent_half, "branch", [(0, 1), (1, 0)])
-    conditional = jnp.where(branch_side == 0, own_half, peer_half)
-    unconditional = jnp.where(branch_side == 0, peer_half, own_half)
-    guided = (1.0 + GUIDE) * conditional - GUIDE * unconditional
-    packed = (base + step_size * guided).astype(jnp.bfloat16)
+    peer_weight = jnp.where(branch_side == 0, -step_size * GUIDE, step_size * (1.0 + GUIDE))
+    packed = (own_half + peer_weight * peer_half).astype(jnp.bfloat16)
     spread = lax.all_to_all(packed.reshape(chips, GROUP, LANES), "seq", 0, 0, tiled=True)
     rows = spread.reshape(chips * GROUP, LANES)
     owner_of = rows[:, mel_bins].astype(jnp.int32)

time: 74 us -> 73.9 us (level)
  no operation moved by 1% of the time
where the time goes in v7:
time: 73.9 us; the launch traced here: 73.5 us
  Pallas kernels  31.8 us (43%)
  blocking collectives  19.7 us (27%)
  local copies, waits for them, and re-layouts  7.3 us (10%)
  starting transfers between devices  6.9 us (9%)
  waiting for transfers between devices  4.7 us (6%)
  matrix products  1.53 us (2%)
  other arithmetic  1.21 us (2%)
    all_to_all x1, blocking collectives, local(): lax.all_to_all(packed.reshape(chips, GROUP, LANES), 'seq', 0, 0, tiled=True)  19.7 us
    pallas_call x1, Pallas kernels, vocoder(): pl.pallas_call(functools.partial(vocoder_kernel, mel_bins=mel_bins, block...  18 us
    pallas_call x1, Pallas kernels, velocity_halves(): pl.pallas_call(functools.partial(velocity_kernel, block=block, tail=tail,...  13.8 us
    reshape x1, local copies, waits for them, and re-layouts, vocoder(): transposed_conv_weight.reshape(KT, channels, wide).transpose(0, 2, 1)  6.46 us
    all_to_all x1, starting transfers between devices, local(): lax.all_to_all(slots.reshape(owners, GROUP, LANES), ('branch', 'seq'), 0,...  5.41 us
    all_to_all x1, waiting for transfers between devices, local(): lax.all_to_all(slots.reshape(owners, GROUP, LANES), ('branch', 'seq'), 0,...  3.32 us
    dot_general x1, matrix products, local(): lax.dot_general(onehot, rows, (((0,), (0,)), ((), ())), preferred_element...  1.53 us
    ppermute x1, starting transfers between devices, local(): peer_half = lax.ppermute(sent_half, 'branch', [(0, 1), (1, 0)])  1.49 us
  transfers between devices with their start and end apart: 2, of which 2 were waited for; matrix products, arithmetic and copies ran while one was open for 10% of the time, Pallas kernels for 0%

profile of v7, /device:TPU:1, one launch (start us, length us, event | category | flops | bytes accessed | tf_op | source)
XLA Modules:
  0.0 73.5 jit_solution(15731073442744678002)
XLA Ops:
  0.0 0.0 copy-start.8
  0.0 13.8 %velocity.1 = (f32[512,128]{1,0:T(8,128)}, f32[512,128]{1,0:T(8,128)}) custom-call(s32[1]{0:T(128)} %bitcast.side_ref, bf16[1,768,1024]{2,1,0:T(8,128)(2,1)} %hidden_hbm.1, f32[5,1024]{1,0:T(8,128)} %modulation_ref.1, bf16[1024,2048]{1,0:T(8,128)(2,1)} %in_weight_hbm.1, f32[1,2048]{1,0:T(1,128)} %bitcast.36, bf16[2048,1024]{1,0:T(8,128)(2,1)} %out_weight_hbm.1, ...), custom_call_target="tpu_custom_call" | custom-call | tf_op jit(solution)/shard_map/velocity/pallas_call | solution.py:211
  13.8 1.5 %collective-permute-start = (f32[512,128]{1,0:T(8,128)}, f32[512,128]{1,0:T(8,128)S(1)}, u32[]{:S(2)}, u32[]{:S(2)}) collective-permute-start(f32[512,128]{1,0:T(8,128)} %get-tuple-element.8), channel_id=1, source_target_pairs={{0,64},{64,0},{1,65},{65,1},{2,66},{66,2},{3,67},{67,3},{4,68},{68... | collective-permute-start | bytes 786440 | tf_op jit(solution)/shard_map/ppermute | solution.py:584
  15.3 1.4 %collective-permute-done = f32[512,128]{1,0:T(8,128)S(1)} collective-permute-done((f32[512,128]{1,0:T(8,128)}, f32[512,128]{1,0:T(8,128)S(1)}, u32[]{:S(2)}, u32[]{:S(2)}) %collective-permute-start) | collective-permute-done | bytes 262176 | tf_op jit(solution)/shard_map/ppermute | solution.py:584
  16.7 1.0 %fusion.9 = bf16[64,8,128]{2,1,0:T(8,128)(2,1)S(1)} fusion(f32[512,128]{1,0:T(8,128)} %get-tuple-element.7, f32[512,128]{1,0:T(8,128)S(1)} %collective-permute-done, f32[]{:T(128)S(6)} %select_n.22), kind=kLoop, calls=%fused_computation.13 | loop fusion | flops 196608 | bytes 655364 | tf_op jit(solution)/shard_map/reshape | solution.py:587
  17.7 19.7 %all_to_all.10 = bf16[64,8,128]{2,1,0:T(8,128)(2,1)S(1)} all-to-all(bf16[64,8,128]{2,1,0:T(8,128)(2,1)S(1)} %fusion.9), channel_id=1, replica_groups=mesh['branch'=2,'seq'=64] {'seq'}, dimensions={0} | all-to-all | bytes 262144 | tf_op jit(solution)/shard_map/all_to_all | solution.py:587
  37.4 0.2 fusion.5
  37.6 1.5 %fusion.2 = bf16[128,8,128]{2,1,0:T(8,128)(2,1)} fusion(s32[512]{0:T(512)S(1)} %fusion.5, bf16[64,8,128]{2,1,0:T(8,128)(2,1)S(1)} %all_to_all.10), kind=kOutput, calls=%fused_computation.3 | convolution fusion | flops 134873088 | bytes 395264 | tf_op jit(solution)/shard_map/dot_general | solution.py:594
  39.1 5.4 %all-to-all-start.1 = ((bf16[128,8,128]{2,1,0:T(8,128)(2,1)}), bf16[128,8,128]{2,1,0:T(8,128)(2,1)S(1)}, u32[]{:S(2)}, u32[]{:S(2)}) async-start(bf16[128,8,128]{2,1,0:T(8,128)(2,1)} %fusion.2), calls=%async_computation.1 | async-start | bytes 524288 | tf_op jit(solution)/shard_map/all_to_all | solution.py:597
  44.5 0.0 copy-done.8
  44.5 0.1 reshape.55
  44.7 0.0 copy-start.9
  44.7 0.0 copy-start
  44.7 0.0 copy-start.1
  44.7 0.0 copy-start.2
  44.7 0.0 copy-start.3
  44.7 0.0 copy-start.4
  44.7 0.0 copy-start.5
  44.8 0.0 copy-start.6
  44.8 0.0 copy-start.7
  44.8 6.5 %copy.25 = bf16[16,256,512]{1,2,0:T(8,128)(2,1)} copy(bf16[16,256,512]{2,1,0:T(8,128)(2,1)} %bitcast.33) | data formatting | bytes 8388608 | tf_op jit(solution)/shard_map/reshape | solution.py:498
  51.2 0.0 copy-done.9
  51.2 0.6 dynamic_slice.3.length_ref
  51.8 0.1 pad.4
  51.9 3.3 %all-to-all-done.1 = bf16[128,8,128]{2,1,0:T(8,128)(2,1)S(1)} async-done(((bf16[128,8,128]{2,1,0:T(8,128)(2,1)}), bf16[128,8,128]{2,1,0:T(8,128)(2,1)S(1)}, u32[]{:S(2)}, u32[]{:S(2)}) %all-to-all-start.1) | async-done | bytes 262176 | tf_op jit(solution)/shard_map/all_to_all | solution.py:597
  55.2 0.0 copy-done
  55.2 0.0 copy-done.1
  55.2 0.0 copy-done.2
  55.3 0.0 copy-done.3
  55.3 0.0 copy-done.4
  55.3 0.0 copy-done.5
  55.3 0.0 copy-done.6
  55.3 0.0 copy-done.7
  55.3 18.0 %vocoder.1 = bf16[1,256,6144]{2,1,0:T(8,128)(2,1)} custom-call(s32[1]{0:T(128)} %dynamic_slice.3.length_ref, bf16[1024,128]{1,0:T(8,128)(2,1)S(1)} %bitcast.25, bf16[896,512]{1,0:T(8,128)(2,1)S(1)} %bitcast.24, f32[1,512]{1,0:T(1,128)S(1)} %bitcast.26, bf16[16,512,256]{2,1,0:T(8,128)(2,1)} %bitcast.32, f32[1,256]{1,0:T(1,128)S(1)} %bitcast.27, ...), custom_call_target="tpu_custom_call" | custom-call | tf_op jit(solution)/shard_map/vocoder/pallas_call | solution.py:507
Async XLA Ops:
  0.0 44.5 %copy-start.8 = (bf16[700,512]{1,0:T(8,128)(2,1)S(1)}, bf16[700,512]{1,0:T(8,128)(2,1)}, u32[]{:S(2)}) copy-start(bf16[700,512]{1,0:T(8,128)(2,1)} %param.31) | copy-start | bytes 2150404
  13.8 2.9 %collective-permute-start = (f32[512,128]{1,0:T(8,128)}, f32[512,128]{1,0:T(8,128)S(1)}, u32[]{:S(2)}, u32[]{:S(2)}) collective-permute-start(f32[512,128]{1,0:T(8,128)} %get-tuple-element.8), channel_id=1, source_target_pairs={{0,64},{64,0},{1,65},{65,1},{2,66},{66,2},{3,67},{67,3},{4,68},{68... | collective-permute-start | bytes 786440 | tf_op jit(solution)/shard_map/ppermute | solution.py:584
  39.1 16.1 %all-to-all-start.1 = ((bf16[128,8,128]{2,1,0:T(8,128)(2,1)}), bf16[128,8,128]{2,1,0:T(8,128)(2,1)S(1)}, u32[]{:S(2)}, u32[]{:S(2)}) async-start(bf16[128,8,128]{2,1,0:T(8,128)(2,1)} %fusion.2), calls=%async_computation.1 | async-start | bytes 524288 | tf_op jit(solution)/shard_map/all_to_all | solution.py:597
  44.7 6.6 %copy-start.9 = (s32[128]{0:T(128)S(1)}, s32[128]{0:T(128)}, u32[]{:S(2)}) copy-start(s32[128]{0:T(128)} %param.43) | copy-start | bytes 1540
  44.7 10.6 %copy-start = (bf16[768,256]{1,0:T(8,128)(2,1)S(1)}, bf16[768,256]{1,0:T(8,128)(2,1)}, u32[]{:S(2)}) copy-start(bf16[768,256]{1,0:T(8,128)(2,1)} %dilated_weight_ref.1) | copy-start | bytes 1179652
  44.7 10.6 %copy-start.1 = (bf16[768,256]{1,0:T(8,128)(2,1)S(1)}, bf16[768,256]{1,0:T(8,128)(2,1)}, u32[]{:S(2)}) copy-start(bf16[768,256]{1,0:T(8,128)(2,1)} %second_weight_ref.1) | copy-start | bytes 1179652
  44.7 10.5 %copy-start.2 = (f32[512]{0:T(512)S(1)}, f32[512]{0:T(512)}, u32[]{:S(2)}) copy-start(f32[512]{0:T(512)} %param.32) | copy-start | bytes 6148
  44.7 10.5 %copy-start.3 = (f32[256]{0:T(256)S(1)}, f32[256]{0:T(256)}, u32[]{:S(2)}) copy-start(f32[256]{0:T(256)} %param.34) | copy-start | bytes 3076
  44.7 10.5 %copy-start.4 = (f32[256]{0:T(256)S(1)}, f32[256]{0:T(256)}, u32[]{:S(2)}) copy-start(f32[256]{0:T(256)} %param.35) | copy-start | bytes 3076
  44.7 10.5 %copy-start.5 = (f32[256]{0:T(256)S(1)}, f32[256]{0:T(256)}, u32[]{:S(2)}) copy-start(f32[256]{0:T(256)} %param.37) | copy-start | bytes 3076
  44.8 10.5 %copy-start.6 = (f32[256]{0:T(256)S(1)}, f32[256]{0:T(256)}, u32[]{:S(2)}) copy-start(f32[256]{0:T(256)} %param.38) | copy-start | bytes 3076
  44.8 10.5 %copy-start.7 = (f32[256]{0:T(256)S(1)}, f32[256]{0:T(256)}, u32[]{:S(2)}) copy-start(f32[256]{0:T(256)} %param.40) | copy-start | bytes 3076
